TPU v7x, 32 devices: a whole 2x2x4 slice. The times are simulated.
32 devices in a mesh: wide: 8 (over z, x), narrow: 4 (over y, core).
Axes of the slice: x: 2, y: 2, z: 4, core: 2. Of those that a mesh axis runs over, the one named last changes fastest.
Arguments:
- dec_input: bfloat16 [24, 512, 768], P('wide', 'narrow'), may hold values from -6 to 6
- enc_out: bfloat16 [24, 4096, 768], P('wide', 'narrow'), may hold values from -6 to 6
- enc_len: int32 [24], P('wide'), may hold values from 512 to 4096, as said below
- cotangent: bfloat16 [24, 512, 768], P('wide', 'narrow'), may hold values from -6 to 6
- self_query: float32 [768, 768], P('wide'), may hold values from -0.0546875 to 0.0546875
- self_key: float32 [768, 768], P('wide'), may hold values from -0.21875 to 0.21875
- self_value: float32 [768, 768], P('wide'), may hold values from -0.21875 to 0.21875
- self_output: float32 [768, 768], P('wide'), may hold values from -0.4375 to 0.4375
- cross_query: float32 [768, 768], P('wide'), may hold values from -0.0546875 to 0.0546875
- cross_key: float32 [768, 768], P('wide'), may hold values from -0.21875 to 0.21875
- cross_value: float32 [768, 768], P('wide'), may hold values from -0.21875 to 0.21875
- cross_output: float32 [768, 768], P('wide'), may hold values from -0.875 to 0.875
- ffn_gate: float32 [768, 2048], P('wide'), may hold values from -0.21875 to 0.21875
- ffn_up: float32 [768, 2048], P('wide'), may hold values from -0.21875 to 0.21875
- ffn_down: float32 [2048, 768], P('wide'), may hold values from -0.125 to 0.125
- self_gain: float32 [768], P('wide'), may hold values from 0.5 to 1.5
- cross_gain: float32 [768], P('wide'), may hold values from 0.5 to 1.5
- ffn_gain: float32 [768], P('wide'), may hold values from 0.5 to 1.5
- bias_table: float32 [384], P('wide'), may hold values from -4 to 4
Outputs:
- layer_out: bfloat16 [24, 512, 768], P('wide', 'narrow')
- input_grad: bfloat16 [24, 512, 768], P('wide', 'narrow')
- enc_grad: bfloat16 [24, 4096, 768], P('wide', 'narrow')
- grad_self_query: float32 [768, 768], P('wide')
- grad_self_key: float32 [768, 768], P('wide')
- grad_self_value: float32 [768, 768], P('wide')
- grad_self_output: float32 [768, 768], P('wide')
- grad_cross_query: float32 [768, 768], P('wide')
- grad_cross_key: float32 [768, 768], P('wide')
- grad_cross_value: float32 [768, 768], P('wide')
- grad_cross_output: float32 [768, 768], P('wide')
- grad_ffn_gate: float32 [768, 2048], P('wide')
- grad_ffn_up: float32 [768, 2048], P('wide')
- grad_ffn_down: float32 [2048, 768], P('wide')
- grad_self_gain: float32 [768], P('wide')
- grad_cross_gain: float32 [768], P('wide')
- grad_ffn_gain: float32 [768], P('wide')
- grad_bias_table: float32 [384], P('wide')
Inputs may be any that keep to these rules, and one draw needn't show every extreme that they name: `enc_len`: at least one example in every draw has exactly 4096 live encoder rows.
All inputs are finite; a program needn't handle non-finite values.
Results may differ from a plain program's by a relative error of at most 0.03.
The roundings to bfloat16 on the way count: a program that leaves them out, or rounds other values in their place, can miss the bound.
Values may be sent and summed in bfloat16 or wider, within the bound.
No kernel may reach another device: no remote copies, remote signals or barrier semaphores. Data moves between devices by JAX's collectives and lax.ppermute only.
A program may use at most 192 MiB of HBM per device.

v0:
```python
import math

import jax
import jax.numpy as jnp
from jax import lax
from jax.sharding import PartitionSpec as P

HD = 64
BUCKETS = 32
MAXDIST = 128


NEG_FILL = -1000000000.0
NORM_EPS = 1e-06
FULL_ACCURACY = lax.Precision.HIGHEST


def bucket_edges():
    exact = BUCKETS // 2
    edges = []
    for target in range(exact + 1, BUCKETS):
        for distance in range(exact, MAXDIST + 1):
            scaled = math.log(distance / exact) / math.log(MAXDIST / exact) * (BUCKETS - exact)
            grown = min(exact + math.floor(scaled), BUCKETS - 1)
            if grown >= target:
                edges.append(distance)
                break
    return edges


def bucket_of(distance):
    found = jnp.minimum(distance, BUCKETS // 2)
    for edge in bucket_edges():
        found = found + (distance >= edge).astype(jnp.int32)
    return found


def root_norm(values, gain):
    return values * lax.rsqrt(jnp.mean(values * values, axis=-1, keepdims=True) + NORM_EPS) * gain


def project(acts, weight):
    return jnp.einsum("etd,df->etf", acts, weight, preferred_element_type=jnp.float32)


def project_back(grads, weight):
    return jnp.einsum("etf,df->etd", grads, weight, preferred_element_type=jnp.float32)


def weight_grad(acts, grads):
    return jnp.einsum("etd,etf->df", acts, grads, preferred_element_type=jnp.float32)


def to_items(tensor):
    examples, length, features = tensor.shape
    groups = features // HD
    moved = jnp.transpose(tensor.reshape(examples, length, groups, HD), (2, 0, 1, 3))
    return moved.reshape(groups * examples, 1, length, HD)


def from_items(item_set, examples):
    total_items, batch, length, depth = item_set.shape
    groups = total_items * batch // examples
    merged = jnp.transpose(item_set.reshape(groups, examples, length, depth), (1, 2, 0, 3))
    return merged.reshape(examples, length, groups * depth)


def item_lengths(lengths, groups):
    spread = jnp.broadcast_to(lengths[None, :], (groups, lengths.shape[0]))
    return spread.reshape(-1, 1)


def self_scores(query_heads_all, key_heads_all, relative_position_bias, causal):
    attention_scores = jnp.einsum(
        "eqhd,ekhd->ehqk", query_heads_all, key_heads_all, preferred_element_type=jnp.float32
    )
    return jnp.where(causal[None, None], attention_scores + relative_position_bias[None], NEG_FILL)


def cross_scores(query_heads_all, key_heads_all, lengths):
    attention_scores = jnp.einsum(
        "xug,xwg->xuw", query_heads_all, key_heads_all, preferred_element_type=jnp.float32
    )
    live = jnp.arange(key_heads_all.shape[1])[None, None, :] < lengths[:, None, None]
    return jnp.where(live, attention_scores, NEG_FILL)


def cross_forward(window_extent, query_heads_all, key_heads_all, values, lengths):

    def one_item(operands):
        query_row_block, key_rows, value_row_block, length_rows = operands
        attention_scores = cross_scores(query_row_block, key_rows[:, :window_extent], length_rows)
        row_peak = jnp.max(attention_scores, axis=-1, keepdims=True)
        raised = jnp.exp(attention_scores - row_peak)
        row_total = jnp.sum(raised, axis=-1, keepdims=True)
        attention_weight = (raised / row_total).astype(jnp.bfloat16)
        mixed = jnp.einsum(
            "lzg,lgx->lzx",
            attention_weight,
            value_row_block[:, :window_extent],
            preferred_element_type=jnp.float32,
        )
        return (mixed, (row_peak + jnp.log(row_total))[..., 0])

    return lax.map(one_item, (query_heads_all, key_heads_all, values, lengths))


def cross_backward(
    window_extent, query_heads_all, key_heads_all, values, lengths, log_sums, grad_mixed
):

    def one_item(operands):
        query_row_block, key_rows, value_row_block, length_rows, lse_rows, gradient_row_block = (
            operands
        )
        key_portion = key_rows[:, :window_extent]
        value_portion = value_row_block[:, :window_extent]
        attention_scores = cross_scores(query_row_block, key_portion, length_rows)
        attention_weight = jnp.exp(attention_scores - lse_rows[..., None])
        grad_weights = jnp.einsum(
            "xug,xwg->xuw", gradient_row_block, value_portion, preferred_element_type=jnp.float32
        )
        inner_sum = jnp.sum(attention_weight * grad_weights, axis=-1, keepdims=True)
        score_gradient = (attention_weight * (grad_weights - inner_sum)).astype(jnp.bfloat16)
        grad_query = jnp.einsum(
            "lzg,lgx->lzx", score_gradient, key_portion, preferred_element_type=jnp.float32
        )
        grad_key = jnp.einsum(
            "vhm,vhf->vmf", score_gradient, query_row_block, preferred_element_type=jnp.float32
        )
        grad_value = jnp.einsum(
            "vhm,vhf->vmf",
            attention_weight.astype(jnp.bfloat16),
            gradient_row_block,
            preferred_element_type=jnp.float32,
        )
        padding = ((0, 0), (0, key_rows.shape[1] - window_extent), (0, 0))
        return (grad_query, jnp.pad(grad_key, padding), jnp.pad(grad_value, padding))

    return lax.map(
        one_item, (query_heads_all, key_heads_all, values, lengths, log_sums, grad_mixed)
    )


def by_span(kernel, full, operands):
    result = kernel(full, *operands)
    return result


def local(
    dec_input,
    enc_out,
    enc_len,
    cotangent,
    self_query,
    self_key,
    self_value,
    self_output,
    cross_query,
    cross_key,
    cross_value,
    cross_output,
    ffn_gate,
    ffn_up,
    ffn_down,
    self_gain,
    cross_gain,
    ffn_gain,
    bias_table,
):
    (
        query_matrix,
        key_matrix,
        value_matrix,
        output_matrix,
        memory_query,
        memory_key,
        memory_value,
        memory_output,
        gate_matrix,
        up_matrix,
        down_matrix,
        gain_first,
        gain_second,
        gain_third,
        table_flat,
    ) = (
        lax.all_gather(self_query.astype(jnp.bfloat16), "wide", axis=0, tiled=True),
        lax.all_gather(self_key.astype(jnp.bfloat16), "wide", axis=0, tiled=True),
        lax.all_gather(self_value.astype(jnp.bfloat16), "wide", axis=0, tiled=True),
        lax.all_gather(self_output.astype(jnp.bfloat16), "wide", axis=0, tiled=True),
        lax.all_gather(cross_query.astype(jnp.bfloat16), "wide", axis=0, tiled=True),
        lax.all_gather(cross_key.astype(jnp.bfloat16), "wide", axis=0, tiled=True),
        lax.all_gather(cross_value.astype(jnp.bfloat16), "wide", axis=0, tiled=True),
        lax.all_gather(cross_output.astype(jnp.bfloat16), "wide", axis=0, tiled=True),
        lax.all_gather(ffn_gate.astype(jnp.bfloat16), "wide", axis=0, tiled=True),
        lax.all_gather(ffn_up.astype(jnp.bfloat16), "wide", axis=0, tiled=True),
        lax.all_gather(ffn_down.astype(jnp.bfloat16), "wide", axis=0, tiled=True),
        lax.all_gather(self_gain.astype(jnp.bfloat16), "wide", axis=0, tiled=True),
        lax.all_gather(cross_gain.astype(jnp.bfloat16), "wide", axis=0, tiled=True),
        lax.all_gather(ffn_gain.astype(jnp.bfloat16), "wide", axis=0, tiled=True),
        lax.all_gather(bias_table.astype(jnp.bfloat16), "wide", axis=0, tiled=True),
    )
    narrow_rank = lax.axis_index("narrow")
    narrow_size = lax.axis_size("narrow")
    examples, local_rows, model_width = dec_input.shape
    head_count = model_width // HD
    target_rows = local_rows * narrow_size
    gain_one = gain_first.astype(jnp.float32)
    gain_two = gain_second.astype(jnp.float32)
    gain_three = gain_third.astype(jnp.float32)
    residual = dec_input.astype(jnp.float32)
    normed_one = root_norm(residual, gain_one).astype(jnp.bfloat16)
    query_heads_all = project(normed_one, query_matrix).astype(jnp.bfloat16)
    keys_own = project(normed_one, key_matrix).astype(jnp.bfloat16)
    values_own = project(normed_one, value_matrix).astype(jnp.bfloat16)
    keys_all, values_all = (
        lax.all_gather(keys_own, "narrow", axis=1, tiled=True),
        lax.all_gather(values_own, "narrow", axis=1, tiled=True),
    )
    query_four = query_heads_all.reshape(examples, local_rows, head_count, HD)
    key_four = keys_all.reshape(examples, target_rows, head_count, HD)
    value_four = values_all.reshape(examples, target_rows, head_count, HD)
    query_place = narrow_rank * local_rows + jnp.arange(local_rows)
    key_place = jnp.arange(target_rows)
    distance = jnp.maximum(query_place[:, None] - key_place[None, :], 0)
    bucket_indicator = (bucket_of(distance)[None] == jnp.arange(BUCKETS)[:, None, None]).astype(
        jnp.float32
    )
    bucket_bias_lookup = table_flat.astype(jnp.float32).reshape(BUCKETS, head_count)
    relative_position_bias = jnp.einsum(
        "jpu,jy->ypu", bucket_indicator, bucket_bias_lookup, precision=FULL_ACCURACY
    )
    causal = key_place[None, :] <= query_place[:, None]
    attention_scores = self_scores(query_four, key_four, relative_position_bias, causal)
    row_peak = jnp.max(attention_scores, axis=-1, keepdims=True)
    raised = jnp.exp(attention_scores - row_peak)
    row_total = jnp.sum(raised, axis=-1, keepdims=True)
    self_lse = row_peak + jnp.log(row_total)
    weights_self = (raised / row_total).astype(jnp.bfloat16)
    mixed = jnp.einsum(
        "ehqk,ekhd->eqhd", weights_self, value_four, preferred_element_type=jnp.float32
    )
    mixed = mixed.reshape(examples, local_rows, model_width).astype(jnp.bfloat16)
    first = residual + project(mixed, output_matrix)
    normed_two = root_norm(first, gain_two).astype(jnp.bfloat16)
    cross_local = project(normed_two, memory_query).astype(jnp.bfloat16)
    memory_keys = project(enc_out, memory_key).astype(jnp.bfloat16)
    memory_values = project(enc_out, memory_value).astype(jnp.bfloat16)
    cross_queries, cross_keys, cross_values = (
        lax.all_to_all(cross_local, "narrow", split_axis=2, concat_axis=1, tiled=True),
        lax.all_to_all(memory_keys, "narrow", split_axis=2, concat_axis=1, tiled=True),
        lax.all_to_all(memory_values, "narrow", split_axis=2, concat_axis=1, tiled=True),
    )
    memory_total = cross_keys.shape[1]
    query_items = to_items(cross_queries)
    key_items = to_items(cross_keys)
    value_items = to_items(cross_values)
    length_items = item_lengths(enc_len, cross_queries.shape[2] // HD)
    out_items, cross_lse = by_span(
        cross_forward, memory_total, (query_items, key_items, value_items, length_items)
    )
    cross_heads_out = from_items(out_items, examples).astype(jnp.bfloat16)
    cross_mixed = lax.all_to_all(cross_heads_out, "narrow", split_axis=1, concat_axis=2, tiled=True)
    second = first + project(cross_mixed, memory_output)
    normed_three = root_norm(second, gain_three).astype(jnp.bfloat16)
    gate_pre = project(normed_three, gate_matrix)
    up_pre = project(normed_three, up_matrix)
    hidden = (jax.nn.gelu(gate_pre, approximate=True) * up_pre).astype(jnp.bfloat16)
    layer_out = (second + project(hidden, down_matrix)).astype(jnp.bfloat16)
    (
        query_matrix,
        key_matrix,
        value_matrix,
        output_matrix,
        memory_query,
        memory_key,
        memory_value,
        memory_output,
        gate_matrix,
        up_matrix,
        down_matrix,
    ) = (
        lax.all_gather(self_query.astype(jnp.bfloat16), "wide", axis=0, tiled=True),
        lax.all_gather(self_key.astype(jnp.bfloat16), "wide", axis=0, tiled=True),
        lax.all_gather(self_value.astype(jnp.bfloat16), "wide", axis=0, tiled=True),
        lax.all_gather(self_output.astype(jnp.bfloat16), "wide", axis=0, tiled=True),
        lax.all_gather(cross_query.astype(jnp.bfloat16), "wide", axis=0, tiled=True),
        lax.all_gather(cross_key.astype(jnp.bfloat16), "wide", axis=0, tiled=True),
        lax.all_gather(cross_value.astype(jnp.bfloat16), "wide", axis=0, tiled=True),
        lax.all_gather(cross_output.astype(jnp.bfloat16), "wide", axis=0, tiled=True),
        lax.all_gather(ffn_gate.astype(jnp.bfloat16), "wide", axis=0, tiled=True),
        lax.all_gather(ffn_up.astype(jnp.bfloat16), "wide", axis=0, tiled=True),
        lax.all_gather(ffn_down.astype(jnp.bfloat16), "wide", axis=0, tiled=True),
    )
    grad_out = cotangent.astype(jnp.float32)
    grad_rounded = grad_out.astype(jnp.bfloat16)
    grad_down = weight_grad(hidden, grad_rounded)
    grad_hidden = project_back(grad_rounded, down_matrix)

    def gated(gate_in, up_in):
        return jax.nn.gelu(gate_in, approximate=True) * up_in

    unused, gated_pull = jax.vjp(gated, gate_pre, up_pre)
    grad_gate_pre, grad_up_pre = gated_pull(grad_hidden)
    gate_rounded = grad_gate_pre.astype(jnp.bfloat16)
    up_rounded = grad_up_pre.astype(jnp.bfloat16)
    grad_gate = weight_grad(normed_three, gate_rounded)
    grad_up = weight_grad(normed_three, up_rounded)
    grad_normed_three = project_back(gate_rounded, gate_matrix) + project_back(
        up_rounded, up_matrix
    )
    unused, norm_pull_three = jax.vjp(root_norm, second, gain_three)
    grad_second_norm, grad_gain_three = norm_pull_three(grad_normed_three)
    grad_second = grad_out + grad_second_norm
    second_rounded = grad_second.astype(jnp.bfloat16)
    grad_memory_output = weight_grad(cross_mixed, second_rounded)
    grad_cross_mixed = project_back(second_rounded, memory_output).astype(jnp.bfloat16)
    grad_heads_in = lax.all_to_all(
        grad_cross_mixed, "narrow", split_axis=2, concat_axis=1, tiled=True
    )
    grad_items = to_items(grad_heads_in)
    grad_query_items, grad_key_items, grad_value_items = by_span(
        cross_backward,
        memory_total,
        (query_items, key_items, value_items, length_items, cross_lse, grad_items),
    )
    grad_query_heads = from_items(grad_query_items, examples)
    grad_key_heads = from_items(grad_key_items, examples)
    grad_value_heads = from_items(grad_value_items, examples)
    grad_cross_q, grad_cross_k, grad_cross_v = (
        lax.all_to_all(
            grad_query_heads.astype(jnp.bfloat16), "narrow", split_axis=1, concat_axis=2, tiled=True
        ),
        lax.all_to_all(
            grad_key_heads.astype(jnp.bfloat16), "narrow", split_axis=1, concat_axis=2, tiled=True
        ),
        lax.all_to_all(
            grad_value_heads.astype(jnp.bfloat16), "narrow", split_axis=1, concat_axis=2, tiled=True
        ),
    )
    grad_memory_query = weight_grad(normed_two, grad_cross_q)
    grad_memory_key = weight_grad(enc_out, grad_cross_k)
    grad_memory_value = weight_grad(enc_out, grad_cross_v)
    enc_grad = (
        project_back(grad_cross_k, memory_key) + project_back(grad_cross_v, memory_value)
    ).astype(jnp.bfloat16)
    grad_normed_two = project_back(grad_cross_q, memory_query)
    unused, norm_pull_two = jax.vjp(root_norm, first, gain_two)
    grad_first_norm, grad_gain_two = norm_pull_two(grad_normed_two)
    grad_first = grad_second + grad_first_norm
    first_rounded = grad_first.astype(jnp.bfloat16)
    grad_output_matrix = weight_grad(mixed, first_rounded)
    grad_mixed_four = project_back(first_rounded, output_matrix).astype(jnp.bfloat16)
    grad_mixed_four = grad_mixed_four.reshape(examples, local_rows, head_count, HD)
    attention_scores = self_scores(query_four, key_four, relative_position_bias, causal)
    weights_back = jnp.exp(attention_scores - self_lse)
    grad_weights = jnp.einsum(
        "eqhd,ekhd->ehqk", grad_mixed_four, value_four, preferred_element_type=jnp.float32
    )
    inner_sum = jnp.sum(weights_back * grad_weights, axis=-1, keepdims=True)
    score_gradient = weights_back * (grad_weights - inner_sum)
    grad_table = jnp.einsum(
        "mji,yji->ym", jnp.sum(score_gradient, axis=0), bucket_indicator, precision=FULL_ACCURACY
    )
    scores_rounded = score_gradient.astype(jnp.bfloat16)
    grad_queries = jnp.einsum(
        "ehqk,ekhd->eqhd", scores_rounded, key_four, preferred_element_type=jnp.float32
    )
    grad_queries = grad_queries.reshape(examples, local_rows, model_width).astype(jnp.bfloat16)
    part_keys = jnp.einsum(
        "ehqk,eqhd->ekhd", scores_rounded, query_four, preferred_element_type=jnp.float32
    )
    part_values = jnp.einsum(
        "ehqk,eqhd->ekhd",
        weights_back.astype(jnp.bfloat16),
        grad_mixed_four,
        preferred_element_type=jnp.float32,
    )
    summed_keys, summed_values = (
        lax.psum_scatter(
            part_keys.reshape(examples, target_rows, model_width).astype(jnp.bfloat16),
            "narrow",
            scatter_dimension=1,
            tiled=True,
        ).astype(jnp.float32),
        lax.psum_scatter(
            part_values.reshape(examples, target_rows, model_width).astype(jnp.bfloat16),
            "narrow",
            scatter_dimension=1,
            tiled=True,
        ).astype(jnp.float32),
    )
    grad_keys = summed_keys.astype(jnp.bfloat16)
    grad_values = summed_values.astype(jnp.bfloat16)
    grad_query_matrix = weight_grad(normed_one, grad_queries)
    grad_key_matrix = weight_grad(normed_one, grad_keys)
    grad_value_matrix = weight_grad(normed_one, grad_values)
    grad_normed_one = (
        project_back(grad_queries, query_matrix)
        + project_back(grad_keys, key_matrix)
        + project_back(grad_values, value_matrix)
    )
    unused, norm_pull_one = jax.vjp(root_norm, residual, gain_one)
    grad_input_norm, grad_gain_one = norm_pull_one(grad_normed_one)
    input_grad = (grad_first + grad_input_norm).astype(jnp.bfloat16)
    table_grad_flat = grad_table.reshape(-1)
    reduced = (
        lax.psum_scatter(grad_query_matrix, "wide", scatter_dimension=0, tiled=True),
        lax.psum_scatter(grad_key_matrix, "wide", scatter_dimension=0, tiled=True),
        lax.psum_scatter(grad_value_matrix, "wide", scatter_dimension=0, tiled=True),
        lax.psum_scatter(grad_output_matrix, "wide", scatter_dimension=0, tiled=True),
        lax.psum_scatter(grad_memory_query, "wide", scatter_dimension=0, tiled=True),
        lax.psum_scatter(grad_memory_key, "wide", scatter_dimension=0, tiled=True),
        lax.psum_scatter(grad_memory_value, "wide", scatter_dimension=0, tiled=True),
        lax.psum_scatter(grad_memory_output, "wide", scatter_dimension=0, tiled=True),
        lax.psum_scatter(grad_gate, "wide", scatter_dimension=0, tiled=True),
        lax.psum_scatter(grad_up, "wide", scatter_dimension=0, tiled=True),
        lax.psum_scatter(grad_down, "wide", scatter_dimension=0, tiled=True),
        lax.psum_scatter(grad_gain_one, "wide", scatter_dimension=0, tiled=True),
        lax.psum_scatter(grad_gain_two, "wide", scatter_dimension=0, tiled=True),
        lax.psum_scatter(grad_gain_three, "wide", scatter_dimension=0, tiled=True),
        lax.psum_scatter(table_grad_flat, "wide", scatter_dimension=0, tiled=True),
    )
    totals = (
        lax.psum(reduced[0].astype(jnp.bfloat16), "narrow").astype(jnp.float32),
        lax.psum(reduced[1].astype(jnp.bfloat16), "narrow").astype(jnp.float32),
        lax.psum(reduced[2].astype(jnp.bfloat16), "narrow").astype(jnp.float32),
        lax.psum(reduced[3].astype(jnp.bfloat16), "narrow").astype(jnp.float32),
        lax.psum(reduced[4].astype(jnp.bfloat16), "narrow").astype(jnp.float32),
        lax.psum(reduced[5].astype(jnp.bfloat16), "narrow").astype(jnp.float32),
        lax.psum(reduced[6].astype(jnp.bfloat16), "narrow").astype(jnp.float32),
        lax.psum(reduced[7].astype(jnp.bfloat16), "narrow").astype(jnp.float32),
        lax.psum(reduced[8].astype(jnp.bfloat16), "narrow").astype(jnp.float32),
        lax.psum(reduced[9].astype(jnp.bfloat16), "narrow").astype(jnp.float32),
        lax.psum(reduced[10].astype(jnp.bfloat16), "narrow").astype(jnp.float32),
        lax.psum(reduced[11].astype(jnp.bfloat16), "narrow").astype(jnp.float32),
        lax.psum(reduced[12].astype(jnp.bfloat16), "narrow").astype(jnp.float32),
        lax.psum(reduced[13].astype(jnp.bfloat16), "narrow").astype(jnp.float32),
        lax.psum(reduced[14].astype(jnp.bfloat16), "narrow").astype(jnp.float32),
    )
    return (
        layer_out,
        input_grad,
        enc_grad,
        totals[0],
        totals[1],
        totals[2],
        totals[3],
        totals[4],
        totals[5],
        totals[6],
        totals[7],
        totals[8],
        totals[9],
        totals[10],
        totals[11],
        totals[12],
        totals[13],
        totals[14],
    )


def solution(mesh):
    placed = (
        P("wide", "narrow", None),
        P("wide", "narrow", None),
        P("wide"),
        P("wide", "narrow", None),
        P("wide", None),
        P("wide", None),
        P("wide", None),
        P("wide", None),
        P("wide", None),
        P("wide", None),
        P("wide", None),
        P("wide", None),
        P("wide", None),
        P("wide", None),
        P("wide", None),
        P("wide"),
        P("wide"),
        P("wide"),
        P("wide"),
    )
    return jax.shard_map(
        local,
        mesh=mesh,
        in_specs=placed,
        out_specs=(
            P("wide", "narrow", None),
            P("wide", "narrow", None),
            P("wide", "narrow", None),
            P("wide", None),
            P("wide", None),
            P("wide", None),
            P("wide", None),
            P("wide", None),
            P("wide", None),
            P("wide", None),
            P("wide", None),
            P("wide", None),
            P("wide", None),
            P("wide", None),
            P("wide"),
            P("wide"),
            P("wide"),
            P("wide"),
        ),
        check_vma=False,
    )
```

profile of v0, /device:TPU:9, one launch (start us, length us, event | category | flops | bytes accessed | tf_op | source)
XLA Modules:
  0.0 2031.9 jit_solution(5578772597171063474)
XLA Ops:
  17.9 16.3 all-reduce.9
  34.4 17.4 all-gather.14.cloned.1.call-done
  54.7 39.8 %all-gather.20.cloned.1.call-done = bf16[768,768]{1,0:T(8,128)(2,1)} async-done(((bf16[96,768]{1,0:T(8,128)(2,1)}), bf16[768,768]{1,0:T(8,128)(2,1)}) %all-gather.20.cloned.1.call-update) | async-done | bytes 1179664 | tf_op jit(solution)/shard_map/all_gather | solution.py:189
  100.4 36.7 %all-gather.30.cloned.1.call-done = bf16[768,768]{1,0:T(8,128)(2,1)} async-done(((bf16[96,768]{1,0:T(8,128)(2,1)}), bf16[768,768]{1,0:T(8,128)(2,1)}) %all-gather.30.cloned.1.call-update) | async-done | bytes 1179664 | tf_op jit(solution)/shard_map/all_gather | solution.py:194
  145.8 11.1 copy.176
  167.0 37.3 %copy.165 = pred[32,128,512]{2,0,1:T(32,128)(4,1)S(1)} copy(pred[32,128,512]{1,0,2:T(32,128)(4,1)S(1)} %iota_compare_fusion.2) | data formatting | bytes 4194304 | tf_op jit(solution)/shard_map/eq | solution.py:227
  218.5 11.1 copy.172
  242.2 11.0 all-gather.16.cloned.1.call-done
  257.6 36.6 %all-gather.22.cloned.1.call-done = bf16[3,512,768]{2,1,0:T(8,128)(2,1)} async-done(((bf16[3,128,768]{2,1,0:T(8,128)(2,1)}), bf16[3,512,768]{2,1,0:T(8,128)(2,1)}) %all-gather.22.cloned.1.call-update) | async-done | bytes 2359312 | tf_op jit(solution)/shard_map/all_gather | solution.py:218
  309.2 27.0 %all-gather.24.cloned.1.call-done = bf16[768,768]{1,0:T(8,128)(2,1)} async-done(((bf16[96,768]{1,0:T(8,128)(2,1)}), bf16[768,768]{1,0:T(8,128)(2,1)}) %all-gather.24.cloned.1.call-update) | async-done | bytes 1179664 | tf_op jit(solution)/shard_map/all_gather | solution.py:191
  338.3 40.6 %all-gather.26.cloned.1.call-done = bf16[768,768]{1,0:T(8,128)(2,1)} async-done(((bf16[96,768]{1,0:T(8,128)(2,1)}), bf16[768,768]{1,0:T(8,128)(2,1)}) %all-gather.26.cloned.1.call-update) | async-done | bytes 1179664 | tf_op jit(solution)/shard_map/all_gather | solution.py:192
  458.0 79.9 %while.26 = (s32[]{:T(128)}, bf16[9,1,512,64]{2,3,1,0:T(8,128)(2,1)S(1)}, f32[9,1,512]{2,1,0:T(1,128)S(1)}, s32[9,1]{0,1:T(1,128)S(1)}, bf16[9,1,512,64]{3,2,1,0...) while((s32[]{:T(128)}, ...), condition=%wide.region_7.8_spmd, body=%wide.region_4.7_spmd.sunk | while | flops 555748864 | bytes 27564144 | solution.py:105
  571.1 34.2 %all-gather.34.cloned.1.call-done = bf16[768,2048]{1,0:T(8,128)(2,1)} async-done(((bf16[96,2048]{1,0:T(8,128)(2,1)}), bf16[768,2048]{1,0:T(8,128)(2,1)}) %all-gather.34.cloned.1.call-update) | async-done | bytes 3145744 | tf_op jit(solution)/shard_map/all_gather | solution.py:196
  627.3 10.7 all-to-all-done.4
  638.9 268.3 %while.27 = (s32[]{:T(128)}, bf16[9,1,512,64]{2,3,1,0:T(8,128)(2,1)S(1)}, bf16[9,1,4096,64]{2,3,1,0:T(8,128)(2,1)}, bf16[9,1,4096,64]{2,3,1,0:T(8,128)(2,1)}, s3...) while((s32[]{:T(128)}, ...), condition=%wide.region_12.13_spmd, body=%wide.region_10.12_spmd.sunk | while | flops 1358958080 | bytes 102259872 | solution.py:140
  913.8 13.7 all-to-all-done.5
  989.0 13.3 copy.211
  1002.2 100.7 %all_to_all.132 = bf16[3,4096,192]{2,0,1:T(4,128)(2,1)} all-to-all(bf16[3,4096,192]{2,0,1:T(4,128)(2,1)} %copy.211), channel_id=1, replica_groups=mesh['wide'=8,'narrow'=4] {'narrow'}, dimensions={1} | all-to-all | bytes 9437184 | tf_op jit(solution)/shard_map/all_to_all | solution.py:338
  1102.9 12.8 copy.213
  1130.2 12.7 copy.206
  1142.9 100.8 %all_to_all.133 = bf16[3,4096,192]{2,0,1:T(4,128)(2,1)} all-to-all(bf16[3,4096,192]{2,0,1:T(4,128)(2,1)} %copy.206), channel_id=1, replica_groups=mesh['wide'=8,'narrow'=4] {'narrow'}, dimensions={1} | all-to-all | bytes 9437184 | tf_op jit(solution)/shard_map/all_to_all | solution.py:335
  1243.7 12.8 copy.208
  1326.9 44.0 %reduce-scatter.42.cloned.1.call-done = f32[96,768]{1,0:T(8,128)} async-done(((f32[768,768]{1,0:T(8,128)}), f32[96,768]{1,0:T(8,128)}) %reduce-scatter.42.cloned.1.call-update) | async-done | bytes 294928
  1372.6 69.8 %reduce-scatter.40.cloned.1.call-done = f32[96,768]{1,0:T(8,128)} async-done(((f32[768,768]{1,0:T(8,128)}), f32[96,768]{1,0:T(8,128)}) %reduce-scatter.40.cloned.1.call-update) | async-done | bytes 294928
  1444.1 69.7 %reduce-scatter.26.cloned.1.call-done = f32[96,768]{1,0:T(8,128)} async-done(((f32[768,768]{1,0:T(8,128)}), f32[96,768]{1,0:T(8,128)}) %reduce-scatter.26.cloned.1.call-update) | async-done | bytes 294928 | tf_op jit(solution)/shard_map/reduce_scatter | solution.py:411
  1515.5 69.9 %reduce-scatter.24.cloned.1.call-done = f32[96,768]{1,0:T(8,128)} async-done(((f32[768,768]{1,0:T(8,128)}), f32[96,768]{1,0:T(8,128)}) %reduce-scatter.24.cloned.1.call-update) | async-done | bytes 294928 | tf_op jit(solution)/shard_map/reduce_scatter | solution.py:410
  1587.0 119.8 %reduce-scatter.38.cloned.1.call-done = f32[256,768]{1,0:T(8,128)} async-done(((f32[2048,768]{1,0:T(8,128)}), f32[256,768]{1,0:T(8,128)}) %reduce-scatter.38.cloned.1.call-update) | async-done | bytes 786448 | tf_op jit(solution)/shard_map/reduce_scatter | solution.py:419
  1708.7 118.8 %reduce-scatter.34.cloned.1.call-done = f32[96,2048]{1,0:T(8,128)} async-done(((f32[768,2048]{1,0:T(8,128)}), f32[96,2048]{1,0:T(8,128)}) %reduce-scatter.34.cloned.1.call-update) | async-done | bytes 786448 | tf_op jit(solution)/shard_map/reduce_scatter | solution.py:417
  1829.4 118.6 %reduce-scatter.36.cloned.1.call-done = f32[96,2048]{1,0:T(8,128)} async-done(((f32[768,2048]{1,0:T(8,128)}), f32[96,2048]{1,0:T(8,128)}) %reduce-scatter.36.cloned.1.call-update) | async-done | bytes 786448 | tf_op jit(solution)/shard_map/reduce_scatter | solution.py:418
  1953.1 26.9 %all-reduce.8 = (bf16[768]{0:T(1024)(128)(2,1)S(1)}, bf16[768]{0:T(1024)(128)(2,1)S(1)}, bf16[768]{0:T(1024)(128)(2,1)S(1)}, bf16[384]{0:T(512)(128)(2,1)S(1)}) all-reduce(f32[768]{0:T(1024)S(1)} %get-tuple-element.225, f32[768]{0:T(1024)S(1)} %get-tuple-element.223, ...), channel_id=15, replica_groups=mesh['wide'=8,'narrow'=4] {'wide'}, use_global_device_ids=true, to_apply=%region_41.42.clone | all-reduce | flops 2688 | bytes 16128
  1980.3 12.3 all-reduce.10
  1995.8 15.4 all-reduce.14.cloned.1.call-done
  (567 shorter events, 750.7 us)
Async XLA Ops:
  7.3 44.6 %all-gather.14.cloned.1.call-start = ((), (), s32[]{:S(2)}) async-start(), calls=%async_computation.21 | async-start | bytes 1327104 | tf_op jit(solution)/shard_map/all_gather | solution.py:190
  9.0 85.4 %all-gather.20.cloned.1.call-start = ((), (), s32[]{:S(2)}) async-start(), calls=%async_computation.24 | async-start | bytes 1327104 | tf_op jit(solution)/shard_map/all_gather | solution.py:189
  10.8 126.3 %all-gather.30.cloned.1.call-start = ((), (), s32[]{:S(2)}) async-start(), calls=%async_computation.29 | async-start | bytes 1327104 | tf_op jit(solution)/shard_map/all_gather | solution.py:194
  12.5 197.3 %all-gather.28.cloned.1.call-start = ((), (), s32[]{:S(2)}) async-start(), calls=%async_computation.28 | async-start | bytes 1327104 | tf_op jit(solution)/shard_map/all_gather | solution.py:193
  14.2 225.7 %all-gather.18.cloned.1.call-start = ((), (), s32[]{:S(2)}) async-start(), calls=%async_computation.23 | async-start | bytes 1327104 | tf_op jit(solution)/shard_map/all_gather | solution.py:188
  14.9 238.3 %all-gather.16.cloned.1.call-start = ((), (), s32[]{:S(2)}) async-start(), calls=%async_computation.22 | async-start | bytes 2949120 | tf_op jit(solution)/shard_map/all_gather | solution.py:219
  54.7 239.5 %all-gather.22.cloned.1.call-start = ((), (), s32[]{:S(2)}) async-start(), calls=%async_computation.25 | async-start | bytes 2949120 | tf_op jit(solution)/shard_map/all_gather | solution.py:218
  97.3 238.9 %all-gather.24.cloned.1.call-start = ((), (), s32[]{:S(2)}) async-start(), calls=%async_computation.26 | async-start | bytes 1327104 | tf_op jit(solution)/shard_map/all_gather | solution.py:191
  98.0 280.8 %all-gather.26.cloned.1.call-start = ((), (), s32[]{:S(2)}) async-start(), calls=%async_computation.27 | async-start | bytes 1327104 | tf_op jit(solution)/shard_map/all_gather | solution.py:192
  98.8 449.3 %all-gather.38.cloned.1.call-start = ((), (), s32[]{:S(2)}) async-start(), calls=%async_computation.33 | async-start | bytes 3538944 | tf_op jit(solution)/shard_map/all_gather | solution.py:198
  99.6 463.7 %all-gather.32.cloned.1.call-start = ((), (), s32[]{:S(2)}) async-start(), calls=%async_computation.30 | async-start | bytes 1327104 | tf_op jit(solution)/shard_map/all_gather | solution.py:195
  156.9 76.7 %all-to-all-start.2 = ((bf16[3,1024,768]{1,0,2:T(4,128)(2,1)}), bf16[3,1024,768]{1,0,2:T(4,128)(2,1)}, u32[]{:S(2)}, u32[]{:S(2)}) async-start(bf16[3,1024,768]{1,0,2:T(4,128)(2,1)} %copy.176), calls=%async_computation.2 | async-start | bytes 12582912 | tf_op jit(solution)/shard_map/all_to_all | solution.py:253
  163.8 402.0 %all-gather.36.cloned.1.call-start = ((), (), s32[]{:S(2)}) async-start(), calls=%async_computation.32 | async-start | bytes 3538944 | tf_op jit(solution)/shard_map/all_gather | solution.py:197
  233.6 148.5 %all-to-all-start.1 = ((bf16[3,1024,768]{1,0,2:T(4,128)(2,1)}), bf16[3,1024,768]{1,0,2:T(4,128)(2,1)}, u32[]{:S(2)}, u32[]{:S(2)}) async-start(bf16[3,1024,768]{1,0,2:T(4,128)(2,1)} %copy.172), calls=%async_computation.1 | async-start | bytes 12582912 | tf_op jit(solution)/shard_map/all_to_all | solution.py:252
  382.2 74.2 %all-to-all-start = ((bf16[3,128,768]{1,0,2:T(4,128)(2,1)}), bf16[3,128,768]{1,0,2:T(4,128)(2,1)S(1)}, u32[]{:S(2)}, u32[]{:S(2)}) async-start(bf16[3,128,768]{1,0,2:T(4,128)(2,1)} %copy.168), calls=%async_computation | async-start | bytes 1572864 | tf_op jit(solution)/shard_map/all_to_all | solution.py:251
  387.2 218.2 %all-gather.34.cloned.1.call-start = ((), (), s32[]{:S(2)}) async-start(), calls=%async_computation.31 | async-start | bytes 3538944 | tf_op jit(solution)/shard_map/all_gather | solution.py:196
  543.1 18.6 all-to-all-start.3
  908.7 18.8 all-to-all-start.5
  913.8 351.9 %reduce-scatter.20.cloned.1.call-start = ((), (), s32[]{:S(2)}) async-start(), calls=%async_computation.35 | async-start | bytes 2949120 | tf_op jit(solution)/shard_map/reduce_scatter | solution.py:387
  946.3 323.0 %reduce-scatter.18.cloned.1.call-start = ((), (), s32[]{:S(2)}) async-start(), calls=%async_computation.34 | async-start | bytes 2949120 | tf_op jit(solution)/shard_map/reduce_scatter | solution.py:381
  967.5 352.7 %reduce-scatter.32.cloned.1.call-start = ((), (), s32[]{:S(2)}) async-start(), calls=%async_computation.41 | async-start | bytes 2654208 | tf_op jit(solution)/shard_map/reduce_scatter | solution.py:416
  971.3 350.6 %reduce-scatter.30.cloned.1.call-start = ((), (), s32[]{:S(2)}) async-start(), calls=%async_computation.40 | async-start | bytes 2654208 | tf_op jit(solution)/shard_map/reduce_scatter | solution.py:413
  973.7 349.9 %reduce-scatter.28.cloned.1.call-start = ((), (), s32[]{:S(2)}) async-start(), calls=%async_computation.39 | async-start | bytes 2654208 | tf_op jit(solution)/shard_map/reduce_scatter | solution.py:412
  977.2 348.0 %reduce-scatter.22.cloned.1.call-start = ((), (), s32[]{:S(2)}) async-start(), calls=%async_computation.36 | async-start | bytes 2654208 | tf_op jit(solution)/shard_map/reduce_scatter | solution.py:409
  983.7 387.1 %reduce-scatter.42.cloned.1.call-start = ((), (), s32[]{:S(2)}) async-start(), calls=%async_computation.46 | async-start | bytes 2654208
  1124.9 317.4 %reduce-scatter.40.cloned.1.call-start = ((), (), s32[]{:S(2)}) async-start(), calls=%async_computation.45 | async-start | bytes 2654208
  1265.6 248.2 %reduce-scatter.26.cloned.1.call-start = ((), (), s32[]{:S(2)}) async-start(), calls=%async_computation.38 | async-start | bytes 2654208 | tf_op jit(solution)/shard_map/reduce_scatter | solution.py:411
  1269.1 316.2 %reduce-scatter.24.cloned.1.call-start = ((), (), s32[]{:S(2)}) async-start(), calls=%async_computation.37 | async-start | bytes 2654208 | tf_op jit(solution)/shard_map/reduce_scatter | solution.py:410
  1272.8 434.0 %reduce-scatter.38.cloned.1.call-start = ((), (), s32[]{:S(2)}) async-start(), calls=%async_computation.44 | async-start | bytes 7077888 | tf_op jit(solution)/shard_map/reduce_scatter | solution.py:419
  1277.3 550.2 %reduce-scatter.34.cloned.1.call-start = ((), (), s32[]{:S(2)}) async-start(), calls=%async_computation.42 | async-start | bytes 7077888 | tf_op jit(solution)/shard_map/reduce_scatter | solution.py:417
  1283.4 664.6 %reduce-scatter.36.cloned.1.call-start = ((), (), s32[]{:S(2)}) async-start(), calls=%async_computation.43 | async-start | bytes 7077888 | tf_op jit(solution)/shard_map/reduce_scatter | solution.py:418
  1289.3 721.9 %all-reduce.14.cloned.1.call-start = ((), (), s32[]{:S(2)}) async-start(), calls=%async_computation.47 | async-start | bytes 4915200 | tf_op jit(solution)/shard_map/psum | solution.py:431
  (92 other events, 2010.3 us)
Sparse Core Ops, SparseCore 0:
  10.9 40.9 all-gather.13
  54.6 39.8 all-gather.19
  97.2 39.8 all-gather.29
  139.7 39.8 all-gather.27
  182.1 39.8 all-gather.17
  224.1 29.1 all-gather.15
  255.4 38.7 all-gather.21
  296.9 39.2 all-gather.23
  339.0 39.8 all-gather.25
  380.9 59.3 all-gather.37
  443.0 39.5 all-gather.31
  484.6 59.4 all-gather.35
  546.3 59.0 all-gather.33
  946.4 31.0 reduce-scatter.19
  980.0 33.0 reduce-scatter.17
  1016.5 68.5 reduce-scatter.31
  1088.4 68.0 reduce-scatter.29
  1159.8 68.0 reduce-scatter.27
  1231.4 68.0 reduce-scatter.21
  1302.8 68.0 reduce-scatter.41
  1374.3 67.9 reduce-scatter.39
  1445.8 67.9 reduce-scatter.25
  1517.3 67.9 reduce-scatter.23
  1588.8 117.9 reduce-scatter.37
  1710.4 117.0 reduce-scatter.33
  1830.9 117.0 reduce-scatter.35
  1952.3 58.8 all-reduce.13
where the time goes:
time: 2050 us; the launch traced here: 2030 us
  waiting for transfers between devices  907 us (44%)
  matrix products  397 us (19%)
  local copies, waits for them, and re-layouts  264 us (13%)
  blocking collectives  257 us (13%)
  other arithmetic  152 us (7%)
  starting transfers between devices  35.4 us (2%)
    reduce_scatter x1, waiting for transfers between devices, local(): lax.psum_scatter(grad_down, 'wide', scatter_dimension=0, tiled=True)  120 us
    reduce_scatter x1, waiting for transfers between devices, local(): lax.psum_scatter(grad_gate, 'wide', scatter_dimension=0, tiled=True)  119 us
    reduce_scatter x1, waiting for transfers between devices, local(): lax.psum_scatter(grad_up, 'wide', scatter_dimension=0, tiled=True)  119 us
    unnamed x29, waiting for transfers between devices  114 us
    all_to_all x1, blocking collectives, local(): lax.all_to_all(grad_key_heads.astype(jnp.bfloat16), 'narrow', split_axis=...  101 us
    all_to_all x1, blocking collectives, local(): lax.all_to_all(grad_value_heads.astype(jnp.bfloat16), 'narrow', split_axi...  101 us
    dot_general x18, matrix products, cross_scores(): jnp.einsum('xug,xwg->xuw', query_heads_all, key_heads_all, preferred_elem...  93.5 us
    convert_element_type x9, other arithmetic, one_item(): (attention_weight * (grad_weights - inner_sum)).astype(jnp.bfloat16)  71.4 us
  transfers between devices with their start and end apart: 33, of which 20 were waited for; matrix products, arithmetic and copies ran while one was open for 24% of the time, Pallas kernels for 0%

commit v1 on v0

v1 whole, which is shorter than its diff:
```python
import functools
import math

import jax
import jax.numpy as jnp
import numpy as np
from jax import lax
from jax.experimental import pallas as pl
from jax.experimental.pallas import tpu as pltpu
from jax.sharding import PartitionSpec as P

HD = 64
BUCKETS = 32
MAXDIST = 128
NORM_EPS = 1e-06
MASKED = -1e30
LANES = 128
ROW_BLOCK = 512
FULL_ACCURACY = lax.Precision.HIGHEST
F32 = jnp.float32
BF16 = jnp.bfloat16

PAIR = ((0, 1), (1, 0), (2, 3), (3, 2))
ACROSS = ((0, 2), (2, 0), (1, 3), (3, 1))


def bucket_table(length):
    exact = BUCKETS // 2
    hot = np.zeros((BUCKETS, length), np.float32)
    for distance in range(length):
        bucket = distance
        if distance >= exact:
            scaled = math.log(distance / exact) / math.log(MAXDIST / exact) * (BUCKETS - exact)
            bucket = min(exact + math.floor(scaled), BUCKETS - 1)
        hot[bucket, distance] = 1.0
    return hot


def dot(left, right, contract=(1, 0)):
    return lax.dot_general(
        left, right, (((contract[0],), (contract[1],)), ((), ())), preferred_element_type=F32
    )


def root_norm(values, gain):
    return values * lax.rsqrt(jnp.mean(values * values, axis=-1, keepdims=True) + NORM_EPS) * gain


def pair_swap(value):
    return lax.ppermute(value, "narrow", PAIR)


def across_swap(value):
    return lax.ppermute(value, "narrow", ACROSS)


def in_order(flag, mine, other):
    first = flag == 0
    return jnp.where(first, mine, other), jnp.where(first, other, mine)


def narrow_gather(value, axis, row, core):
    low, high = in_order(row, value, across_swap(value))
    column = jnp.stack([low, high], axis)
    low, high = in_order(core, column, pair_swap(column))
    full = jnp.stack([low, high], axis + 1)
    shape = list(value.shape)
    shape[axis] *= 4
    return full.reshape(shape)


def part_of(value, index, parts, axis):
    size = value.shape[axis] // parts
    return lax.dynamic_slice_in_dim(value, index * size, size, axis)


def transpose_chunks(chunks_ref, out_ref):
    for i in range(chunks_ref.shape[0]):
        out_ref[LANES * i : LANES * (i + 1), :] = chunks_ref[i].T


def position_bias(vec_ref, bias_ref):
    heads, size, _ = bias_ref.shape
    key = lax.broadcasted_iota(jnp.int32, (size, size), 0)
    query = lax.broadcasted_iota(jnp.int32, (size, size), 1)
    for h in range(heads):
        rows = jnp.broadcast_to(vec_ref[h : h + 1, :], (size, size))
        rolled = pltpu.roll(rows, 0, 1, stride=1, stride_axis=0)
        bias_ref[h] = jnp.where(key <= query, rolled, MASKED)


def self_forward_kernel(
    x_ref, gain_ref, chunks_ref, vec_ref, n1_ref, qkv_ref, out_ref, lse_ref, wt_ref, bias_ref
):
    heads = bias_ref.shape[0]
    width = heads * HD

    @pl.when(pl.program_id(0) == 0)
    def _():
        transpose_chunks(chunks_ref, wt_ref)
        position_bias(vec_ref, bias_ref)

    normed = root_norm(x_ref[0].astype(F32), gain_ref[...]).astype(BF16)
    n1_ref[0] = normed
    qkv = dot(wt_ref[...], normed, (1, 1)).astype(BF16)
    qkv_ref[0] = qkv
    lse_ref[...] = jnp.zeros_like(lse_ref)
    for h in range(heads):
        q, k, v = (qkv[width * part + HD * h : width * part + HD * (h + 1)] for part in range(3))
        s = dot(k, q, (0, 0)) + bias_ref[h]
        peak = jnp.max(s, axis=0, keepdims=True)
        raised = jnp.exp(s - peak)
        total = jnp.sum(raised, axis=0, keepdims=True)
        weight = (raised * (1.0 / total)).astype(BF16)
        out_ref[0, HD * h : HD * (h + 1), :] = dot(v, weight).astype(BF16)
        lse_ref[0, h : h + 1, :] = peak + jnp.log(total)


def self_forward(x, gain, chunks, vec, heads):
    examples, length, model = x.shape
    feats = chunks.shape[0] * LANES
    whole = lambda *shape: pl.BlockSpec(shape, lambda e: (0,) * len(shape))
    per = lambda *shape: pl.BlockSpec((1, *shape), lambda e: (e, 0, 0))
    return pl.pallas_call(
        self_forward_kernel,
        grid=(examples,),
        in_specs=[
            per(length, model),
            whole(1, model),
            whole(*chunks.shape),
            whole(*vec.shape),
        ],
        out_specs=[
            per(length, model),
            per(feats, length),
            per(heads * HD, length),
            per(8, length),
        ],
        out_shape=[
            jax.ShapeDtypeStruct((examples, length, model), BF16),
            jax.ShapeDtypeStruct((examples, feats, length), BF16),
            jax.ShapeDtypeStruct((examples, heads * HD, length), BF16),
            jax.ShapeDtypeStruct((examples, 8, length), F32),
        ],
        scratch_shapes=[
            pltpu.VMEM((feats, model), BF16),
            pltpu.VMEM((heads, length, length), F32),
        ],
        compiler_params=pltpu.CompilerParams(vmem_limit_bytes=48 << 20),
        name="self_forward",
    )(x, gain, chunks, vec)


def self_backward_kernel(
    n1_ref, qkv_ref, do_ref, lse_ref, chunks_ref, vec_ref,
    dn_ref, gw_ref, dvec_ref,
    wt_ref, bias_ref, dsum_ref, dqkv_ref,
):
    heads, size, _ = bias_ref.shape
    width = heads * HD
    e = pl.program_id(0)

    @pl.when(e == 0)
    def _():
        transpose_chunks(chunks_ref, wt_ref)
        position_bias(vec_ref, bias_ref)
        dsum_ref[...] = jnp.zeros_like(dsum_ref)
        gw_ref[...] = jnp.zeros_like(gw_ref)
        dqkv_ref[...] = jnp.zeros_like(dqkv_ref)

    for h in range(heads):
        q, k, v = (
            qkv_ref[0, width * part + HD * h : width * part + HD * (h + 1), :] for part in range(3)
        )
        do = do_ref[0, HD * h : HD * (h + 1), :]
        s = dot(k, q, (0, 0)) + bias_ref[h]
        p = jnp.exp(s - lse_ref[0, h : h + 1, :])
        dp = dot(v, do, (0, 0))
        inner = jnp.sum(p * dp, axis=0, keepdims=True)
        ds = p * (dp - inner)
        dsum_ref[h] += ds
        ds = ds.astype(BF16)
        at = lambda part: slice(width * part + HD * h, width * part + HD * (h + 1))
        dqkv_ref[:, at(0)] = dot(k, ds).T.astype(BF16)
        dqkv_ref[:, at(1)] = dot(ds, q, (1, 1)).astype(BF16)
        dqkv_ref[:, at(2)] = dot(p.astype(BF16), do, (1, 1)).astype(BF16)
    dqkv = dqkv_ref[...]
    dn_ref[0] = dot(dqkv, wt_ref[...])
    gw_ref[...] += dot(n1_ref[0], dqkv, (0, 0))

    @pl.when(e == pl.num_programs(0) - 1)
    def _():
        dvec_ref[...] = jnp.zeros_like(dvec_ref)
        for h in range(heads):
            back, count = dsum_ref[h], size
            while count > 8:
                count //= 2
                back = back[:count] + pltpu.roll(back[count:], size - count, 1)
            total = back[:1]
            for r in range(1, count):
                total = total + pltpu.roll(back[r : r + 1], size - r, 1)
            dvec_ref[h : h + 1, :] = total


def self_backward(n1, qkv, do, lse, chunks, vec, heads):
    examples, length, model = n1.shape
    feats = chunks.shape[0] * LANES
    whole = lambda *shape: pl.BlockSpec(shape, lambda e: (0,) * len(shape))
    per = lambda *shape: pl.BlockSpec((1, *shape), lambda e: (e, 0, 0))
    return pl.pallas_call(
        self_backward_kernel,
        grid=(examples,),
        in_specs=[
            per(length, model),
            per(feats, length),
            per(heads * HD, length),
            per(8, length),
            whole(*chunks.shape),
            whole(*vec.shape),
        ],
        out_specs=[per(length, model), whole(model, feats), whole(8, length)],
        out_shape=[
            jax.ShapeDtypeStruct((examples, length, model), F32),
            jax.ShapeDtypeStruct((model, feats), F32),
            jax.ShapeDtypeStruct((8, length), F32),
        ],
        scratch_shapes=[
            pltpu.VMEM((feats, model), BF16),
            pltpu.VMEM((heads, length, length), F32),
            pltpu.VMEM((heads, length, length), F32),
            pltpu.VMEM((length, feats), BF16),
        ],
        compiler_params=pltpu.CompilerParams(vmem_limit_bytes=48 << 20),
        name="self_backward",
    )(n1, qkv, do, lse, chunks, vec)


def memory_project_kernel(live_ref, own_ref, other_ref, chunks_ref, k_ref, v_ref, wt_ref):
    e, j = pl.program_id(0), pl.program_id(1)
    blocks = pl.num_programs(1)
    half = wt_ref.shape[0] // 2

    @pl.when((e == 0) & (j == 0))
    def _():
        transpose_chunks(chunks_ref, wt_ref)

    def project(rows):
        both = dot(wt_ref[...], rows, (1, 1)).astype(BF16)
        k_ref[0] = both[:half]
        v_ref[0] = both[half:]

    @pl.when((live_ref[e, j] > 0) & (j < blocks // 2))
    def _():
        project(own_ref[0])

    @pl.when((live_ref[e, j] > 0) & (j >= blocks // 2))
    def _():
        project(other_ref[0])


def memory_project(live, own, other, chunks):
    examples, rows, model = own.shape
    half = rows // ROW_BLOCK
    feats = chunks.shape[0] * LANES // 2
    row_spec = lambda first: pl.BlockSpec(
        (1, ROW_BLOCK, model), lambda e, j, live: (e, jnp.clip(j - first, 0, half - 1), 0)
    )
    out_spec = pl.BlockSpec((1, feats, ROW_BLOCK), lambda e, j, live: (e, 0, j))
    out = jax.ShapeDtypeStruct((examples, feats, 2 * rows), BF16)
    return pl.pallas_call(
        memory_project_kernel,
        grid_spec=pltpu.PrefetchScalarGridSpec(
            num_scalar_prefetch=1,
            grid=(examples, 2 * half),
            in_specs=[
                row_spec(0),
                row_spec(half),
                pl.BlockSpec(chunks.shape, lambda e, j, live: (0, 0, 0)),
            ],
            out_specs=[out_spec, out_spec],
            scratch_shapes=[pltpu.VMEM((2 * feats, model), BF16)],
        ),
        out_shape=[out, out],
        compiler_params=pltpu.CompilerParams(vmem_limit_bytes=48 << 20),
        name="memory_project",
    )(live, own, other, chunks)


def cross_forward_kernel(live_ref, q_ref, k_ref, v_ref, o_ref, lse_ref, peak_ref, total_ref, acc_ref):
    e, j = pl.program_id(0), pl.program_id(1)
    heads = acc_ref.shape[0] // HD
    live = live_ref[e, j]

    @pl.when(j == 0)
    def _():
        peak_ref[...] = jnp.full_like(peak_ref, MASKED)
        total_ref[...] = jnp.zeros_like(total_ref)
        acc_ref[...] = jnp.zeros_like(acc_ref)

    def block(partial):
        for h in range(heads):
            at = slice(HD * h, HD * (h + 1))
            s = dot(k_ref[0, at, :], q_ref[0, at, :], (0, 0))
            if partial:
                s = jnp.where(lax.broadcasted_iota(jnp.int32, s.shape, 0) < live, s, MASKED)
            before = peak_ref[h : h + 1, :]
            peak = jnp.maximum(before, jnp.max(s, axis=0, keepdims=True))
            p = jnp.exp(s - peak)
            shrink = jnp.exp(before - peak)
            peak_ref[h : h + 1, :] = peak
            total_ref[h : h + 1, :] = total_ref[h : h + 1, :] * shrink + jnp.sum(p, axis=0, keepdims=True)
            acc_ref[at, :] = acc_ref[at, :] * shrink + dot(v_ref[0, at, :], p.astype(BF16))

    @pl.when(live == ROW_BLOCK)
    def _():
        block(False)

    @pl.when((live > 0) & (live < ROW_BLOCK))
    def _():
        block(True)

    @pl.when(j == pl.num_programs(1) - 1)
    def _():
        total = total_ref[...]
        some = total > 0
        inverse = jnp.where(some, 1.0 / jnp.where(some, total, 1.0), 0.0)
        lse_ref[0] = jnp.where(some, peak_ref[...] + jnp.log(jnp.where(some, total, 1.0)), MASKED)
        for h in range(heads):
            at = slice(HD * h, HD * (h + 1))
            o_ref[0, at, :] = (acc_ref[at, :] * inverse[h : h + 1, :]).astype(o_ref.dtype)


def cross_forward(live, q, k, v):
    examples, feats, length = q.shape
    rows = k.shape[2]
    q_spec = pl.BlockSpec((1, feats, length), lambda e, j, live: (e, 0, 0))
    k_spec = pl.BlockSpec((1, feats, ROW_BLOCK), lambda e, j, live: (e, 0, j))
    l_spec = pl.BlockSpec((1, 8, length), lambda e, j, live: (e, 0, 0))
    return pl.pallas_call(
        cross_forward_kernel,
        grid_spec=pltpu.PrefetchScalarGridSpec(
            num_scalar_prefetch=1,
            grid=(examples, rows // ROW_BLOCK),
            in_specs=[q_spec, k_spec, k_spec],
            out_specs=[q_spec, l_spec],
            scratch_shapes=[
                pltpu.VMEM((8, length), F32),
                pltpu.VMEM((8, length), F32),
                pltpu.VMEM((feats, length), F32),
            ],
        ),
        out_shape=[
            jax.ShapeDtypeStruct((examples, feats, length), F32),
            jax.ShapeDtypeStruct((examples, 8, length), F32),
        ],
        compiler_params=pltpu.CompilerParams(vmem_limit_bytes=48 << 20),
        name="cross_forward",
    )(live, q, k, v)


def cross_backward_kernel(
    live_ref, q_ref, do_ref, lse_ref, inner_ref, k_ref, v_ref, dq_ref, dk_ref, dv_ref, acc_ref
):
    e, j = pl.program_id(0), pl.program_id(1)
    heads = acc_ref.shape[0] // HD
    live = live_ref[e, j]

    @pl.when(j == 0)
    def _():
        acc_ref[...] = jnp.zeros_like(acc_ref)

    def block(partial):
        for h in range(heads):
            at = slice(HD * h, HD * (h + 1))
            q, do, k, v = q_ref[0, at, :], do_ref[0, at, :], k_ref[0, at, :], v_ref[0, at, :]
            s = dot(k, q, (0, 0))
            p = jnp.exp(s - lse_ref[0, h : h + 1, :])
            if partial:
                p = jnp.where(lax.broadcasted_iota(jnp.int32, s.shape, 0) < live, p, 0.0)
            dp = dot(v, do, (0, 0))
            ds = (p * (dp - inner_ref[0, h : h + 1, :])).astype(BF16)
            acc_ref[at, :] += dot(k, ds)
            dk_ref[0, :, at] = dot(ds, q, (1, 1)).astype(BF16)
            dv_ref[0, :, at] = dot(p.astype(BF16), do, (1, 1)).astype(BF16)

    @pl.when(live == ROW_BLOCK)
    def _():
        block(False)

    @pl.when((live > 0) & (live < ROW_BLOCK))
    def _():
        block(True)

    @pl.when(j == pl.num_programs(1) - 1)
    def _():
        dq_ref[0] = acc_ref[...].T


def cross_backward(live, q, do, lse, inner, k, v):
    examples, feats, length = q.shape
    rows = k.shape[2]
    q_spec = pl.BlockSpec((1, feats, length), lambda e, j, live: (e, 0, 0))
    k_spec = pl.BlockSpec((1, feats, ROW_BLOCK), lambda e, j, live: (e, 0, j))
    l_spec = pl.BlockSpec((1, 8, length), lambda e, j, live: (e, 0, 0))
    d_spec = pl.BlockSpec((1, ROW_BLOCK, feats), lambda e, j, live: (e, j, 0))
    return pl.pallas_call(
        cross_backward_kernel,
        grid_spec=pltpu.PrefetchScalarGridSpec(
            num_scalar_prefetch=1,
            grid=(examples, rows // ROW_BLOCK),
            in_specs=[q_spec, q_spec, l_spec, l_spec, k_spec, k_spec],
            out_specs=[
                pl.BlockSpec((1, length, feats), lambda e, j, live: (e, 0, 0)),
                d_spec,
                d_spec,
            ],
            scratch_shapes=[pltpu.VMEM((feats, length), F32)],
        ),
        out_shape=[
            jax.ShapeDtypeStruct((examples, length, feats), F32),
            jax.ShapeDtypeStruct((examples, rows, feats), BF16),
            jax.ShapeDtypeStruct((examples, rows, feats), BF16),
        ],
        compiler_params=pltpu.CompilerParams(vmem_limit_bytes=48 << 20),
        name="cross_backward",
    )(live, q, do, lse, inner, k, v)


def memory_backward_kernel(live_ref, rows_ref, dk_ref, dv_ref, chunks_ref, *refs):
    *add_ref, out_ref, gk_ref, gv_ref, wt_ref = refs
    e, j = pl.program_id(0), pl.program_id(1)
    half = wt_ref.shape[0] // 2

    @pl.when((e == 0) & (j == 0))
    def _():
        transpose_chunks(chunks_ref, wt_ref)
        gk_ref[...] = jnp.zeros_like(gk_ref)
        gv_ref[...] = jnp.zeros_like(gv_ref)

    @pl.when(live_ref[e, j] > 0)
    def _():
        rows, dk, dv = rows_ref[0], dk_ref[0], dv_ref[0]
        gk_ref[...] += dot(rows, dk, (0, 0))
        gv_ref[...] += dot(rows, dv, (0, 0))
        back = dot(dk, wt_ref[:half]) + dot(dv, wt_ref[half:])
        if add_ref:
            back = back + add_ref[0][0].astype(F32)
        out_ref[0] = back.astype(BF16)

    @pl.when(live_ref[e, j] == 0)
    def _():
        out_ref[0] = jnp.zeros_like(out_ref[0])


def memory_backward(live, rows, dk, dv, first, chunks, add=None):
    examples, count, model = rows.shape
    feats = dk.shape[2]
    row_spec = pl.BlockSpec((1, ROW_BLOCK, model), lambda e, j, live: (e, j, 0))
    d_spec = pl.BlockSpec((1, ROW_BLOCK, feats), lambda e, j, live: (e, j + first, 0))
    g_spec = pl.BlockSpec((model, feats), lambda e, j, live: (0, 0))
    grad = jax.ShapeDtypeStruct((model, feats), F32)
    extra = () if add is None else (add,)
    return pl.pallas_call(
        memory_backward_kernel,
        grid_spec=pltpu.PrefetchScalarGridSpec(
            num_scalar_prefetch=1,
            grid=(examples, count // ROW_BLOCK),
            in_specs=[
                row_spec,
                d_spec,
                d_spec,
                pl.BlockSpec(chunks.shape, lambda e, j, live: (0, 0, 0)),
            ]
            + [row_spec] * len(extra),
            out_specs=[row_spec, g_spec, g_spec],
            scratch_shapes=[pltpu.VMEM((2 * feats, model), BF16)],
        ),
        out_shape=[jax.ShapeDtypeStruct(rows.shape, BF16), grad, grad],
        compiler_params=pltpu.CompilerParams(vmem_limit_bytes=48 << 20),
        name="memory_backward",
    )(live, rows, dk, dv, chunks, *extra)


def to_chunks(rows):
    count, width = rows.shape
    return jnp.transpose(rows.reshape(count, width // LANES, LANES), (1, 0, 2))


def from_chunks(chunks):
    count, rows, lanes = chunks.shape
    return jnp.transpose(chunks, (1, 0, 2)).reshape(rows, count * lanes)


def norm_pull(values, gain, grad):
    unused, pull = jax.vjp(root_norm, values, gain)
    return pull(grad)


def local(
    dec_input,
    enc_out,
    enc_len,
    cotangent,
    self_query,
    self_key,
    self_value,
    self_output,
    cross_query,
    cross_key,
    cross_value,
    cross_output,
    ffn_gate,
    ffn_up,
    ffn_down,
    self_gain,
    cross_gain,
    ffn_gain,
    bias_table,
):
    place = lax.axis_index("narrow")
    row, core = place // 2, place % 2
    wide = lax.axis_size("wide")
    examples, own, model = dec_input.shape
    length = 4 * own
    heads = model // HD
    own_heads = heads // 4
    memory_rows = enc_out.shape[1]
    share = self_query.shape[0]

    own_qkv = jnp.concatenate(
        [part_of(w.astype(BF16), place, 4, 1) for w in (self_query, self_key, self_value)], 1
    )
    own_qkv = jnp.pad(own_qkv, ((0, 0), (0, -own_qkv.shape[1] % LANES)))
    pair_qkv = [part_of(w.astype(BF16), core, 2, 1) for w in (cross_query, cross_key, cross_value)]
    small = jnp.stack([self_gain, cross_gain, ffn_gain, jnp.pad(bias_table, (0, share - bias_table.shape[0]))], 1)
    small = jnp.pad(small.astype(BF16), ((0, 0), (0, LANES - 4)))
    packed = [own_qkv, *pair_qkv, self_output.astype(BF16), cross_output.astype(BF16), small]
    counts = [p.shape[1] // LANES for p in packed]
    gathered = lax.all_gather(jnp.concatenate([to_chunks(p) for p in packed], 0), "wide", axis=1, tiled=True)
    bounds = np.cumsum([0, *counts])
    c_self, c_query, c_key, c_value, c_so, c_co, c_small = (
        gathered[a:b] for a, b in zip(bounds[:-1], bounds[1:])
    )
    c_memory = gathered[bounds[2] : bounds[4]]
    self_out_w, cross_out_w, cross_query_w = from_chunks(c_so), from_chunks(c_co), from_chunks(c_query)
    small_rows = c_small[0, :, :4].astype(F32).T
    gain_one, gain_two, gain_three = (small_rows[i : i + 1] for i in range(3))
    table = small_rows[3].reshape(wide, share)[:, : bias_table.shape[0]].reshape(BUCKETS, heads)

    both = ("wide", "narrow")
    quarter = lambda w: part_of(w.astype(BF16), place, 4, 0)
    gate_up = lax.all_gather(jnp.stack([quarter(ffn_gate), quarter(ffn_up)]), both, axis=1, tiled=True)
    gate_w, up_w = gate_up[0], gate_up[1]
    down_w = lax.all_gather(quarter(ffn_down), both, axis=0, tiled=True)

    enc_other = pair_swap(enc_out)
    starts = (place * memory_rows + np.arange(memory_rows // ROW_BLOCK) * ROW_BLOCK).astype(jnp.int32)
    other_starts = starts + (1 - 2 * core) * memory_rows
    block_starts = jnp.concatenate([starts, other_starts])
    live = jnp.clip(enc_len[:, None] - block_starts[None, :], 0, ROW_BLOCK)

    x_all = narrow_gather(dec_input, 1, row, core)
    hot = jnp.asarray(bucket_table(length))
    distance_bias = jnp.dot(table.T, hot, precision=FULL_ACCURACY)
    vec = jnp.pad(part_of(distance_bias, place, 4, 0), ((0, 8 - own_heads), (0, 0)))
    n1, qkv, self_o, self_lse = self_forward(x_all, gain_one, c_self, vec, own_heads)
    self_o_all = narrow_gather(self_o, 1, row, core)
    x1_all = x_all.astype(F32) + jnp.einsum("eft,fd->etd", self_o_all, self_out_w, preferred_element_type=F32)
    n2_all = root_norm(x1_all, gain_two[0]).astype(BF16)
    cross_q = jnp.einsum("df,etd->eft", cross_query_w, n2_all, preferred_element_type=F32).astype(BF16)

    keys, values = memory_project(live, enc_out, enc_other, c_memory)
    part_o, part_lse = cross_forward(live, cross_q, keys, values)
    other_lse = across_swap(part_lse)
    lse = jnp.logaddexp(part_lse, other_lse)
    feats = part_o.shape[1]

    def spread(per_head):
        pieces = per_head[:, : feats // HD, None, :]
        return jnp.broadcast_to(pieces, (examples, feats // HD, HD, per_head.shape[2])).reshape(
            examples, feats, per_head.shape[2]
        )

    sent = part_of(part_o, 1 - row, 2, 2).astype(BF16)
    came = across_swap(sent).astype(F32)
    kept = part_of(part_o, row, 2, 2)
    chip_lse = part_of(lse, row, 2, 2)
    own_weight = jnp.exp(part_of(part_lse, row, 2, 2) - chip_lse)
    other_weight = jnp.exp(part_of(other_lse, row, 2, 2) - chip_lse)
    chip_o = (kept * spread(own_weight) + came * spread(other_weight)).astype(BF16)
    low, high = in_order(core, part_of(chip_o, core, 2, 2), pair_swap(part_of(chip_o, 1 - core, 2, 2)))
    oc = jnp.concatenate([low, high], 1)

    x1 = part_of(x1_all, place, 4, 1)
    x2 = x1 + jnp.einsum("eft,fd->etd", oc, cross_out_w, preferred_element_type=F32)
    n3 = root_norm(x2, gain_three[0]).astype(BF16)
    project = lambda a, w: jnp.einsum("etd,df->etf", a, w, preferred_element_type=F32)
    project_back = lambda a, w: jnp.einsum("etf,df->etd", a, w, preferred_element_type=F32)
    weight_grad = lambda a, g: jnp.einsum("etd,etf->df", a, g, preferred_element_type=F32)
    gate_pre = project(n3, gate_w)
    up_pre = project(n3, up_w)
    gated = lambda a, u: jax.nn.gelu(a, approximate=True) * u
    hidden, gated_pull = jax.vjp(gated, gate_pre, up_pre)
    hidden = hidden.astype(BF16)
    layer_out = (x2 + project(hidden, down_w)).astype(BF16)
    dy = cotangent.astype(F32)
    grad_down = weight_grad(hidden, cotangent)
    da, du = gated_pull(project_back(cotangent, down_w))
    da, du = da.astype(BF16), du.astype(BF16)
    grad_gate = weight_grad(n3, da)
    grad_up = weight_grad(n3, du)
    dn3 = project_back(da, gate_w) + project_back(du, up_w)
    dx2, grad_gain_three = norm_pull(x2, gain_three[0], dn3)
    dx2 = dx2 + dy
    dx2r = dx2.astype(BF16)
    grad_cross_output = jnp.einsum("eft,etd->fd", oc, dx2r, preferred_element_type=F32)

    doc = jnp.einsum("fd,etd->eft", cross_out_w, dx2r, preferred_element_type=F32).astype(BF16)
    inner = jnp.sum(
        (doc.astype(F32) * oc.astype(F32)).reshape(examples, heads, HD, own), axis=2
    )

    def to_heads(value):
        low, high = in_order(core, part_of(value, core, 2, 1), pair_swap(part_of(value, 1 - core, 2, 1)))
        chip = jnp.concatenate([low, high], 2)
        low, high = in_order(row, chip, across_swap(chip))
        return jnp.concatenate([low, high], 2)

    doc_heads = to_heads(doc)
    inner_heads = jnp.pad(to_heads(inner), ((0, 0), (0, 8 - heads // 2), (0, 0)))
    part_dq, dk, dv = cross_backward(live, cross_q, doc_heads, lse, inner_heads, keys, values)
    half_blocks = memory_rows // ROW_BLOCK
    other_grad, gk_other, gv_other = memory_backward(
        live[:, half_blocks:], enc_other, dk, dv, half_blocks, c_memory
    )
    enc_grad, gk_own, gv_own = memory_backward(
        live[:, :half_blocks], enc_out, dk, dv, 0, c_memory, pair_swap(other_grad)
    )
    grad_cross_key, grad_cross_value = gk_own + gk_other, gv_own + gv_other
    grad_cross_query = jnp.einsum("etd,etf->df", n2_all, part_dq.astype(BF16), preferred_element_type=F32)
    chip_dq = part_of(part_dq, row, 2, 1) + across_swap(
        part_of(part_dq, 1 - row, 2, 1).astype(BF16)
    ).astype(F32)
    chip_dn2 = project_back(chip_dq.astype(BF16), cross_query_w)
    dn2 = part_of(chip_dn2, core, 2, 1) + pair_swap(
        part_of(chip_dn2, 1 - core, 2, 1).astype(BF16)
    ).astype(F32)
    dx1, grad_gain_two = norm_pull(x1, gain_two[0], dn2)
    dx1 = dx1 + dx2
    dx1r = dx1.astype(BF16)
    own_o = part_of(self_o_all, place, 4, 2)
    grad_self_output = jnp.einsum("eft,etd->fd", own_o, dx1r, preferred_element_type=F32)

    do = jnp.einsum("fd,etd->eft", self_out_w, dx1r, preferred_element_type=F32).astype(BF16)
    low, high = in_order(row, part_of(do, row, 2, 1), across_swap(part_of(do, 1 - row, 2, 1)))
    column = jnp.stack([low, high], 2)
    low, high = in_order(core, part_of(column, core, 2, 1), pair_swap(part_of(column, 1 - core, 2, 1)))
    do_heads = jnp.stack([low, high], 3).reshape(examples, own_heads * HD, length)
    part_dn1, grad_self, dvec = self_backward(n1, qkv, do_heads, self_lse, c_self, vec, own_heads)
    by_core = part_dn1.reshape(examples, 2, 2, own, model)
    column = part_of(by_core, core, 2, 2) + pair_swap(part_of(by_core, 1 - core, 2, 2).astype(BF16)).astype(F32)
    dn1 = part_of(column, row, 2, 1) + across_swap(part_of(column, 1 - row, 2, 1).astype(BF16)).astype(F32)
    dn1 = dn1.reshape(examples, own, model)
    grad_in, grad_gain_one = norm_pull(dec_input.astype(F32), gain_one[0], dn1)
    input_grad = (dx1 + grad_in).astype(BF16)

    own_table = jnp.dot(hot, dvec[:own_heads].T, precision=FULL_ACCURACY)
    grad_table = lax.dynamic_update_slice_in_dim(
        jnp.zeros((BUCKETS, heads), F32), own_table, place * own_heads, 1
    )
    table_rows = jnp.pad(
        grad_table.reshape(wide, bias_table.shape[0]), ((0, 0), (0, share - bias_table.shape[0]))
    ).reshape(-1)
    small = jnp.stack([grad_gain_one, grad_gain_two, grad_gain_three, table_rows], 1)
    small = jnp.pad(small, ((0, 0), (0, LANES - 4)))
    scatter = functools.partial(lax.psum_scatter, scatter_dimension=0, tiled=True)
    shared = [grad_gate, grad_up, grad_self_output, grad_cross_output, small]
    shared_sum = scatter(jnp.concatenate([g.astype(BF16) for g in shared], 1), both)
    down_sum = scatter(grad_down.astype(BF16), both)
    columns_sum = scatter(
        jnp.concatenate([g.astype(BF16) for g in (grad_self, grad_cross_query, grad_cross_key, grad_cross_value)], 1),
        "wide",
    )
    shared_sum = narrow_gather(shared_sum, 0, row, core).astype(F32)
    down_sum = narrow_gather(down_sum, 0, row, core).astype(F32)
    bounds = np.cumsum([0, *(g.shape[1] for g in shared)])
    gate_sum, up_sum, so_sum, co_sum, small_sum = (
        shared_sum[:, a:b] for a, b in zip(bounds[:-1], bounds[1:])
    )
    self_width = grad_self.shape[1]
    self_sum = narrow_gather(columns_sum[None, :, :self_width], 0, row, core)
    q_sum, k_sum, v_sum = (
        jnp.concatenate([self_sum[i, :, own_heads * HD * part : own_heads * HD * (part + 1)] for i in range(4)], 1)
        for part in range(3)
    )
    cross_sum = columns_sum[:, self_width:].astype(F32)
    cross_sum = (cross_sum + across_swap(columns_sum[:, self_width:]).astype(F32)).astype(BF16)
    low, high = in_order(core, cross_sum, pair_swap(cross_sum))
    cq_sum, ck_sum, cv_sum = (
        jnp.concatenate([part[:, feats * i : feats * (i + 1)] for part in (low, high)], 1) for i in range(3)
    )
    f = lambda a: a.astype(F32)
    return (
        layer_out,
        input_grad,
        enc_grad,
        f(q_sum),
        f(k_sum),
        f(v_sum),
        so_sum,
        f(cq_sum),
        f(ck_sum),
        f(cv_sum),
        co_sum,
        gate_sum,
        up_sum,
        down_sum,
        small_sum[:, 0],
        small_sum[:, 1],
        small_sum[:, 2],
        small_sum[: bias_table.shape[0], 3],
    )


def solution(mesh):
    rows = P("wide", "narrow", None)
    weight, vector = P("wide", None), P("wide")
    return jax.shard_map(
        local,
        mesh=mesh,
        in_specs=(rows, rows, vector, rows, *[weight] * 11, *[vector] * 4),
        out_specs=(rows, rows, rows, *[weight] * 11, *[vector] * 4),
        check_vma=False,
    )
```

time: 2050 us -> 703 us (0.34)
  waiting for transfers between devices: 907 us -> 320 us
  matrix products: 397 us -> 57.8 us
  blocking collectives: 257 us -> 0 us
  local copies, waits for them, and re-layouts: 264 us -> 63.6 us
  Pallas kernels: 0 us -> 164 us
  other arithmetic: 152 us -> 41.1 us
    reduce_scatter x11 -> x2, waiting for transfers between devices: 497 us -> 51.5 us  [the longest x1 51.5 us: local(): scatter(jnp.concatenate([g.astype(BF16) for g in (grad_self, grad_cross_q...]
    dot_general x104 -> x20, matrix products: 397 us -> 57.8 us  [the longest x4 18.8 us: local(): jnp.einsum('etf,df->etd', a, w, preferred_element_type=F32)]
    all_to_all x2 -> x0, blocking collectives: 201 us -> none  [the longest x1 101 us: local(): lax.all_to_all(grad_key_heads.astype(jnp.bfloat16), 'narrow', split_axis=...]
    all_gather x13 -> x3, waiting for transfers between devices: 243 us -> 61.3 us  [the longest x1 61.3 us: local(): lax.all_gather(jnp.concatenate([to_chunks(p) for p in packed], 0), 'wide'...]
    pallas_call x0 -> x7, Pallas kernels: none -> 164 us  [the longest x1 54.1 us: cross_backward(): pl.pallas_call(cross_backward_kernel, grid_spec=pltpu.PrefetchScalarGridS...]
    convert_element_type x51 -> x15, other arithmetic: 112 us -> 10.4 us  [the longest x6 4.66 us: local(): f = lambda a: a.astype(F32)]
    ppermute x0 -> x27, waiting for transfers between devices: none -> 92.9 us  [the longest x13 89.2 us: across_swap(): return lax.ppermute(value, 'narrow', ACROSS)]
    convert_element_type x16 -> x8, local copies, waits for them, and re-layouts: 77 us -> 7.82 us  [the longest x2 2.22 us: local(): w.astype(BF16)]
  transfers between devices with their start and end apart: 33 -> 33, of which waited for: 20 -> 15; matrix products, arithmetic and copies ran while one was open for 24% -> 16% of each run, Pallas kernels for 0% -> 14%
where the time goes in v1:
time: 703 us; the launch traced here: 695 us
  waiting for transfers between devices  320 us (46%)
  Pallas kernels  164 us (23%)
  local copies, waits for them, and re-layouts  63.6 us (9%)
  matrix products  57.8 us (8%)
  other arithmetic  41.1 us (6%)
  starting transfers between devices  31.6 us (4%)
  between operations  15.8 us (2%)
    unnamed x7, waiting for transfers between devices  115 us
    ppermute x13, waiting for transfers between devices, across_swap(): return lax.ppermute(value, 'narrow', ACROSS)  89.2 us
    all_gather x1, waiting for transfers between devices, local(): lax.all_gather(jnp.concatenate([to_chunks(p) for p in packed], 0), 'wide'...  61.3 us
    pallas_call x1, Pallas kernels, cross_backward(): pl.pallas_call(cross_backward_kernel, grid_spec=pltpu.PrefetchScalarGridS...  54.1 us
    reduce_scatter x1, waiting for transfers between devices, local(): scatter(jnp.concatenate([g.astype(BF16) for g in (grad_self, grad_cross_q...  51.5 us
    pallas_call x1, Pallas kernels, cross_forward(): pl.pallas_call(cross_forward_kernel, grid_spec=pltpu.PrefetchScalarGridSp...  37 us
    pallas_call x2, Pallas kernels, memory_backward(): pl.pallas_call(memory_backward_kernel, grid_spec=pltpu.PrefetchScalarGrid...  31.4 us
    unnamed x147, local copies, waits for them, and re-layouts  25.3 us
  transfers between devices with their start and end apart: 33, of which 15 were waited for; matrix products, arithmetic and copies ran while one was open for 16% of the time, Pallas kernels for 14%

profile of v1, /device:TPU:9, one launch (start us, length us, event | category | flops | bytes accessed | tf_op | source)
XLA Modules:
  0.0 694.9 jit_solution(3374282271263858038)
XLA Ops:
  16.4 13.1 %collective-permute-done = bf16[3,128,768]{2,1,0:T(8,128)(2,1)S(1)} collective-permute-done((bf16[3,128,768]{2,1,0:T(8,128)(2,1)S(1)}, bf16[3,128,768]{2,1,0:T(8,128)(2,1)S(1)}, u32[]{:S(2)}, u32[]{:S(2)}) %collective-permute-start) | collective-permute-done | bytes 589856 | tf_op jit(solution)/shard_map/ppermute | solution.py:54
  38.3 61.3 %all-gather.4.cloned.1.call-done = bf16[27,768,128]{2,1,0:T(8,128)(2,1)} async-done(((bf16[27,96,128]{2,1,0:T(8,128)(2,1)}), bf16[27,768,128]{2,1,0:T(8,128)(2,1)}) %all-gather.4.cloned.1.call-update) | async-done | bytes 5308432 | tf_op jit(solution)/shard_map/all_gather | solution.py:539
  103.2 9.5 %self_forward.1 = (bf16[3,512,768]{2,1,0:T(8,128)(2,1)S(1)}, bf16[3,640,512]{2,1,0:T(8,128)(2,1)S(1)}, bf16[3,192,512]{2,1,0:T(8,128)(2,1)S(1)}, f32[3,8,512]{2,1,0:T(8,128)S(1)}) custom-call(bf16[3,512,768]{2,1,0:T(8,128)(2,1)} %bitcast.308, f32[1,768]{1,0:T(1,128)S(1)} %copy.128.gain_ref, bf16[5,768,128]{2,1,0:T(8,128)(2,1)S(1)} %slice.194.chunks_ref, ...), custom_call_target="tpu_custom_call" | custom-call | tf_op jit(solution)/shard_map/self_forward/pallas_call | solution.py:124
  117.3 11.3 %collective-permute-done.2 = bf16[3,192,512]{2,1,0:T(8,128)(2,1)} collective-permute-done((bf16[3,192,512]{2,1,0:T(8,128)(2,1)S(1)}, bf16[3,192,512]{2,1,0:T(8,128)(2,1)}, u32[]{:S(2)}, u32[]{:S(2)}) %collective-permute-start.2) | collective-permute-done | bytes 589856 | tf_op jit(solution)/shard_map/ppermute | solution.py:54
  136.7 3.7 fusion.74
  143.0 15.0 %memory_project.1 = (bf16[3,384,2048]{2,1,0:T(8,128)(2,1)S(1)}, bf16[3,384,2048]{2,1,0:T(8,128)(2,1)}) custom-call(s32[3,4]{1,0:T(4,128)S(1)} %subtract_clamp_fusion.live_ref, bf16[3,1024,768]{2,1,0:T(8,128)(2,1)} %rows_ref.1, bf16[3,1024,768]{2,1,0:T(8,128)(2,1)} %collective-permute-done.4.other_ref.rows_ref, ...), custom_call_target="tpu_custom_call" | custom-call | tf_op jit(solution)/shard_map/memory_project/pallas_call | solution.py:270
  168.0 37.0 %cross_forward.1 = (f32[3,384,512]{2,1,0:T(8,128)}, f32[3,8,512]{2,1,0:T(8,128)S(1)}) custom-call(s32[3,4]{1,0:T(4,128)S(1)} %subtract_clamp_fusion.live_ref, bf16[3,384,512]{2,1,0:T(8,128)(2,1)S(1)} %fusion.20.q_ref, bf16[3,384,2048]{2,1,0:T(8,128)(2,1)} %copy-done.2, bf16[3,384,2048]{2,1,0:T(8,128)(2,1)} %get-tuple-element.40.v_ref), custom_call_target="tpu_custom_call" | custom-call | tf_op jit(solution)/shard_map/cross_forward/pallas_call | solution.py:339
  208.6 15.8 %collective-permute-done.5 = f32[3,8,512]{2,1,0:T(8,128)} collective-permute-done((f32[3,8,512]{2,1,0:T(8,128)S(1)}, f32[3,8,512]{2,1,0:T(8,128)}, u32[]{:S(2)}, u32[]{:S(2)}) %collective-permute-start.5) | collective-permute-done | bytes 49184 | tf_op jit(solution)/shard_map/ppermute | solution.py:54
  229.3 5.4 collective-permute-start.7
  243.2 5.3 fusion.15
  248.5 3.0 fusion.17
  251.5 8.4 %fusion.9 = (bf16[3,128,2048]{2,1,0:T(8,128)(2,1)S(1)}, bf16[3,128,2048]{2,1,0:T(8,128)(2,1)S(1)}, bf16[3,128,2048]{2,1,0:T(8,128)(2,1)}) fusion(f32[3,128,2048]{2,1,0:T(8,128)} %fusion.15, f32[3,128,2048]{2,1,0:T(8,128)} %fusion.17, bf16[3,128,768]{2,1,0:T(8,128)(2,1)} %param.24, bf16[2048,768]{1,0:T(8,128)(2,1)} %all-gather.8.cloned.1.call-done), kind=kOutput, calls=%fused_computation.21 | convolution fusion | flops 1228406784 | bytes 14745600 | tf_op jit(solution)/shard_map/etf,df->etd/dot_general | solution.py:598
  259.9 4.5 fusion.14
  264.4 3.6 multiply_reduce_fusion.1
  278.6 13.6 %collective-permute-done.11 = f32[3,6,256]{2,1,0:T(8,128)S(1)} collective-permute-done((f32[3,6,256]{2,1,0:T(8,128)S(1)}, f32[3,6,256]{2,1,0:T(8,128)S(1)}, u32[]{:S(2)}, u32[]{:S(2)}) %collective-permute-start.11) | collective-permute-done | bytes 18464 | tf_op jit(solution)/shard_map/ppermute | solution.py:54
  292.5 54.1 %cross_backward.1 = (f32[3,512,384]{2,1,0:T(8,128)S(1)}, bf16[3,2048,384]{2,1,0:T(8,128)(2,1)}, bf16[3,2048,384]{2,1,0:T(8,128)(2,1)}) custom-call(s32[3,4]{1,0:T(4,128)S(1)} %subtract_clamp_fusion.live_ref, bf16[3,384,512]{2,1,0:T(8,128)(2,1)S(1)} %fusion.20.q_ref, bf16[3,384,512]{2,1,0:T(8,128)(2,1)S(1)} %pad_maximum_fusion.5.do_ref, ...), custom_call_target="tpu_custom_call" | custom-call | tf_op jit(solution)/shard_map/cross_backward/pallas_call | solution.py:406
  346.6 15.8 %memory_backward.2 = (bf16[3,1024,768]{2,1,0:T(8,128)(2,1)}, f32[768,384]{1,0:T(8,128)S(1)}, f32[768,384]{1,0:T(8,128)S(1)}) custom-call(s32[3,2]{1,0:T(4,128)S(1)} %get-tuple-element.137.live_ref, bf16[3,1024,768]{2,1,0:T(8,128)(2,1)} %collective-permute-done.4.other_ref.rows_ref, bf16[3,2048,384]{2,1,0:T(8,128)(2,1)} %get-tuple-element.48.dk_ref, ...), custom_call_target="tpu_custom_call" | custom-call | tf_op jit(solution)/shard_map/memory_backward/pallas_call | solution.py:463
  364.0 3.5 bitcast_convert_fusion
  367.5 11.5 %collective-permute-done.12 = bf16[3,256,384]{2,1,0:T(8,128)(2,1)} collective-permute-done((bf16[3,256,384]{2,1,0:T(8,128)(2,1)}, bf16[3,256,384]{2,1,0:T(8,128)(2,1)}, u32[]{:S(2)}, u32[]{:S(2)}) %collective-permute-start.12) | collective-permute-done | bytes 589856 | tf_op jit(solution)/shard_map/ppermute | solution.py:54
  392.1 8.6 %collective-permute-done.14 = bf16[3,384,128]{1,2,0:T(8,128)(2,1)} collective-permute-done((bf16[3,384,128]{1,2,0:T(8,128)(2,1)}, bf16[3,384,128]{1,2,0:T(8,128)(2,1)}, u32[]{:S(2)}, u32[]{:S(2)}) %collective-permute-start.14) | collective-permute-done | bytes 294944 | tf_op jit(solution)/shard_map/ppermute | solution.py:54
  403.3 5.5 fusion.25
  414.5 17.4 %self_backward.1 = (f32[3,512,768]{2,1,0:T(8,128)}, f32[768,640]{1,0:T(8,128)S(1)}, f32[8,512]{1,0:T(8,128)S(1)}) custom-call(bf16[3,512,768]{2,1,0:T(8,128)(2,1)} %copy-done.4, bf16[3,640,512]{2,1,0:T(8,128)(2,1)S(1)} %copy-done.6, bf16[3,192,512]{2,1,0:T(8,128)(2,1)S(1)} %reshape.193.do_ref, f32[3,8,512]{2,1,0:T(8,128)S(1)} %get-tuple-element.46.lse_ref, ...), custom_call_target="tpu_custom_call" | custom-call | tf_op jit(solution)/shard_map/self_backward/pallas_call | solution.py:210
  432.0 15.6 %memory_backward.3 = (bf16[3,1024,768]{2,1,0:T(8,128)(2,1)}, f32[768,384]{1,0:T(8,128)S(1)}, f32[768,384]{1,0:T(8,128)S(1)}) custom-call(s32[3,2]{1,0:T(4,128)S(1)} %get-tuple-element.138.live_ref, bf16[3,1024,768]{2,1,0:T(8,128)(2,1)} %rows_ref.1, bf16[3,2048,384]{2,1,0:T(8,128)(2,1)} %get-tuple-element.48.dk_ref, ...), custom_call_target="tpu_custom_call" | custom-call | tf_op jit(solution)/shard_map/memory_backward/pallas_call | solution.py:463
  454.2 3.4 fusion
  466.1 3.3 copy-done.28
  469.9 7.6 %collective-permute-done.17 = bf16[3,1,1,128,768]{4,3,0,2,1:T(8,128)(2,1)} collective-permute-done((bf16[3,1,1,128,768]{4,3,0,2,1:T(8,128)(2,1)}, bf16[3,1,1,128,768]{4,3,0,2,1:T(8,128)(2,1)}, u32[]{:S(2)}, u32[]{:S(2)}) %collective-permute-start.17) | collective-permute-done | bytes 589856 | tf_op jit(solution)/shard_map/ppermute | solution.py:54
  481.8 4.7 fusion.26
  489.5 51.5 %reduce-scatter.6.cloned.1.call-done = bf16[96,1792]{1,0:T(8,128)(2,1)} async-done(((bf16[768,1792]{1,0:T(8,128)(2,1)}), bf16[96,1792]{1,0:T(8,128)(2,1)}) %reduce-scatter.6.cloned.1.call-update) | async-done | bytes 344080 | tf_op jit(solution)/shard_map/reduce_scatter | solution.py:680
  545.9 4.0 collective-permute-start.20
  556.3 114.7 %reduce-scatter.10.cloned.1.call-done = bf16[24,5760]{1,0:T(8,128)(2,1)} async-done(((bf16[768,5760]{1,0:T(8,128)(2,1)}), bf16[24,5760]{1,0:T(8,128)(2,1)}) %reduce-scatter.10.cloned.1.call-update) | async-done | bytes 276496
  671.9 4.7 collective-permute-done.21
  677.7 3.8 collective-permute-start.22
  (352 shorter events, 138.8 us)
Async XLA Ops:
  7.3 92.3 %all-gather.4.cloned.1.call-start = ((), (), s32[]{:S(2)}) async-start(), calls=%async_computation.3 | async-start | bytes 5971968 | tf_op jit(solution)/shard_map/all_gather | solution.py:539
  13.3 229.8 %all-gather.6.cloned.1.call-start = ((), (), s32[]{:S(2)}) async-start(), calls=%async_computation.4 | async-start | bytes 6488064 | tf_op jit(solution)/shard_map/all_gather | solution.py:552
  15.1 236.3 %all-gather.8.cloned.1.call-start = ((), (), s32[]{:S(2)}) async-start(), calls=%async_computation.5 | async-start | bytes 3244032 | tf_op jit(solution)/shard_map/all_gather | solution.py:554
  15.2 14.4 %collective-permute-start = (bf16[3,128,768]{2,1,0:T(8,128)(2,1)S(1)}, bf16[3,128,768]{2,1,0:T(8,128)(2,1)S(1)}, u32[]{:S(2)}, u32[]{:S(2)}) collective-permute-start(bf16[3,128,768]{2,1,0:T(8,128)(2,1)S(1)} %copy-done.25), channel_id=1, source_target_pairs={{0,2},{2,0},{1,3},{3,1},{4,6},{6,4},{5,7},{7,5},{8,10},{10,8},{9,1... | collective-permute-start | bytes 1769480 | tf_op jit(solution)/shard_map/ppermute | solution.py:54
  30.8 4.3 collective-permute-start.1
  32.2 110.8 %collective-permute-start.4 = (bf16[3,1024,768]{2,1,0:T(8,128)(2,1)}, bf16[3,1024,768]{2,1,0:T(8,128)(2,1)}, u32[]{:S(2)}, u32[]{:S(2)}) collective-permute-start(bf16[3,1024,768]{2,1,0:T(8,128)(2,1)} %rows_ref.1), channel_id=1, source_target_pairs={{0,1},{1,0},{2,3},{3,2},{4,5},{5,4},{6,7},{7,6},{8,9},{9,8},{10,11... | collective-permute-start | bytes 14155784 | tf_op jit(solution)/shard_map/ppermute | solution.py:50
  115.4 13.2 %collective-permute-start.2 = (bf16[3,192,512]{2,1,0:T(8,128)(2,1)S(1)}, bf16[3,192,512]{2,1,0:T(8,128)(2,1)}, u32[]{:S(2)}, u32[]{:S(2)}) collective-permute-start(bf16[3,192,512]{2,1,0:T(8,128)(2,1)S(1)} %get-tuple-element.38), channel_id=1, source_target_pairs={{0,2},{2,0},{1,3},{3,1},{4,6},{6,4},{5,7},{7,5},{8,10},{10,8},{9,1... | collective-permute-start | bytes 1769480 | tf_op jit(solution)/shard_map/ppermute | solution.py:54
  117.3 363.3 %reduce-scatter.8.cloned.1.call-start = ((), (), s32[]{:S(2)}) async-start(), calls=%async_computation.7 | async-start | bytes 3244032 | tf_op jit(solution)/shard_map/reduce_scatter | solution.py:679
  131.8 26.2 %collective-permute-start.3 = (bf16[3,2,192,512]{3,2,0,1:T(8,128)(2,1)}, bf16[3,2,192,512]{3,2,0,1:T(8,128)(2,1)}, u32[]{:S(2)}, u32[]{:S(2)}) collective-permute-start(bf16[3,2,192,512]{3,2,0,1:T(8,128)(2,1)} %pad_maximum_fusion.4), channel_id=1, source_target_pairs={{0,1},{1,0},{2,3},{3,2},{4,5},{5,4},{6,7},{7,6},{8,9},{9,8},{10,11... | collective-permute-start | bytes 3538952 | tf_op jit(solution)/shard_map/ppermute | solution.py:50
  207.1 18.9 %collective-permute-start.6 = (bf16[3,384,256]{2,1,0:T(8,128)(2,1)}, bf16[3,384,256]{2,1,0:T(8,128)(2,1)}, u32[]{:S(2)}, u32[]{:S(2)}) collective-permute-start(bf16[3,384,256]{2,1,0:T(8,128)(2,1)} %dynamic-slice_convert_fusion.3), channel_id=1, source_target_pairs={{0,2},{2,0},{1,3},{3,1},{4,6},{6,4},{5,7},{7,5},{8,10},{10,8},{9,1... | collective-permute-start | bytes 1769480 | tf_op jit(solution)/shard_map/ppermute | solution.py:54
  207.1 17.3 %collective-permute-start.5 = (f32[3,8,512]{2,1,0:T(8,128)S(1)}, f32[3,8,512]{2,1,0:T(8,128)}, u32[]{:S(2)}, u32[]{:S(2)}) collective-permute-start(f32[3,8,512]{2,1,0:T(8,128)S(1)} %get-tuple-element.42), channel_id=1, source_target_pairs={{0,2},{2,0},{1,3},{3,1},{4,6},{6,4},{5,7},{7,5},{8,10},{10,8},{9,1... | collective-permute-start | bytes 147464 | tf_op jit(solution)/shard_map/ppermute | solution.py:54
  229.3 8.0 %collective-permute-start.7 = (bf16[3,384,128]{2,1,0:T(8,128)(2,1)}, bf16[3,384,128]{2,1,0:T(8,128)(2,1)}, u32[]{:S(2)}, u32[]{:S(2)}) collective-permute-start(bf16[3,384,128]{2,1,0:T(8,128)(2,1)} %constant_dynamic-slice_fusion.3), channel_id=1, source_target_pairs={{0,1},{1,0},{2,3},{3,2},{4,5},{5,4},{6,7},{7,6},{8,9},{9,8},{10,11... | collective-permute-start | bytes 884744 | tf_op jit(solution)/shard_map/ppermute | solution.py:50
  272.9 2.8 collective-permute-start.8
  277.0 15.2 %collective-permute-start.9 = (bf16[3,384,256]{2,1,0:T(8,128)(2,1)S(1)}, bf16[3,384,256]{2,1,0:T(8,128)(2,1)S(1)}, u32[]{:S(2)}, u32[]{:S(2)}) collective-permute-start(bf16[3,384,256]{2,1,0:T(8,128)(2,1)S(1)} %pad_maximum_fusion.9), channel_id=1, source_target_pairs={{0,2},{2,0},{1,3},{3,1},{4,6},{6,4},{5,7},{7,5},{8,10},{10,8},{9,1... | collective-permute-start | bytes 1769480 | tf_op jit(solution)/shard_map/ppermute | solution.py:54
  277.1 15.1 %collective-permute-start.11 = (f32[3,6,256]{2,1,0:T(8,128)S(1)}, f32[3,6,256]{2,1,0:T(8,128)S(1)}, u32[]{:S(2)}, u32[]{:S(2)}) collective-permute-start(f32[3,6,256]{2,1,0:T(8,128)S(1)} %pad_maximum_fusion.18), channel_id=1, source_target_pairs={{0,2},{2,0},{1,3},{3,1},{4,6},{6,4},{5,7},{7,5},{8,10},{10,8},{9,1... | collective-permute-start | bytes 55304 | tf_op jit(solution)/shard_map/ppermute | solution.py:54
  362.4 69.6 %collective-permute-start.18 = (bf16[3,1024,768]{2,1,0:T(8,128)(2,1)}, bf16[3,1024,768]{2,1,0:T(8,128)(2,1)}, u32[]{:S(2)}, u32[]{:S(2)}) collective-permute-start(bf16[3,1024,768]{2,1,0:T(8,128)(2,1)} %get-tuple-element.50), channel_id=1, source_target_pairs={{0,1},{1,0},{2,3},{3,2},{4,5},{5,4},{6,7},{7,6},{8,9},{9,8},{10,11... | collective-permute-start | bytes 14155784 | tf_op jit(solution)/shard_map/ppermute | solution.py:50
  364.0 15.0 %collective-permute-start.12 = (bf16[3,256,384]{2,1,0:T(8,128)(2,1)}, bf16[3,256,384]{2,1,0:T(8,128)(2,1)}, u32[]{:S(2)}, u32[]{:S(2)}) collective-permute-start(bf16[3,256,384]{2,1,0:T(8,128)(2,1)} %dynamic-slice_convert_fusion.2), channel_id=1, source_target_pairs={{0,2},{2,0},{1,3},{3,1},{4,6},{6,4},{5,7},{7,5},{8,10},{10,8},{9,1... | collective-permute-start | bytes 1769480 | tf_op jit(solution)/shard_map/ppermute | solution.py:54
  367.5 173.5 %reduce-scatter.6.cloned.1.call-start = ((), (), s32[]{:S(2)}) async-start(), calls=%async_computation.6 | async-start | bytes 3096576 | tf_op jit(solution)/shard_map/reduce_scatter | solution.py:680
  382.8 2.7 collective-permute-start.13
  392.1 8.6 %collective-permute-start.14 = (bf16[3,384,128]{1,2,0:T(8,128)(2,1)}, bf16[3,384,128]{1,2,0:T(8,128)(2,1)}, u32[]{:S(2)}, u32[]{:S(2)}) collective-permute-start(bf16[3,384,128]{1,2,0:T(8,128)(2,1)} %dynamic-slice_bitcast_fusion), channel_id=1, source_target_pairs={{0,2},{2,0},{1,3},{3,1},{4,6},{6,4},{5,7},{7,5},{8,10},{10,8},{9,1... | collective-permute-start | bytes 884744 | tf_op jit(solution)/shard_map/ppermute | solution.py:54
  402.1 6.7 collective-permute-start.15
  450.8 220.2 %reduce-scatter.10.cloned.1.call-start = ((), (), s32[]{:S(2)}) async-start(), calls=%async_computation.8 | async-start | bytes 9123840
  453.0 6.5 collective-permute-start.16
  462.0 15.5 %collective-permute-start.17 = (bf16[3,1,1,128,768]{4,3,0,2,1:T(8,128)(2,1)}, bf16[3,1,1,128,768]{4,3,0,2,1:T(8,128)(2,1)}, u32[]{:S(2)}, u32[]{:S(2)}) collective-permute-start(bf16[3,1,1,128,768]{4,3,0,2,1:T(8,128)(2,1)} %dynamic-slice_convert_fusion), channel_id=1, source_target_pairs={{0,2},{2,0},{1,3},{3,1},{4,6},{6,4},{5,7},{7,5},{8,10},{10,8},{9,1... | collective-permute-start | bytes 1769480 | tf_op jit(solution)/shard_map/ppermute | solution.py:54
  480.6 6.0 collective-permute-start.25
  486.6 2.9 collective-permute-start.26
  542.0 3.8 collective-permute-start.19
  544.3 7.4 %collective-permute-start.23 = (bf16[96,1152]{1,0:T(8,128)(2,1)S(1)}, bf16[96,1152]{1,0:T(8,128)(2,1)S(1)}, u32[]{:S(2)}, u32[]{:S(2)}) collective-permute-start(bf16[96,1152]{1,0:T(8,128)(2,1)S(1)} %slice.218), channel_id=1, source_target_pairs={{0,2},{2,0},{1,3},{3,1},{4,6},{6,4},{5,7},{7,5},{8,10},{10,8},{9,1... | collective-permute-start | bytes 663560 | tf_op jit(solution)/shard_map/ppermute | solution.py:54
  545.9 7.6 %collective-permute-start.20 = (bf16[2,1,96,640]{3,2,0,1:T(8,128)(2,1)S(1)}, bf16[2,1,96,640]{3,2,0,1:T(8,128)(2,1)S(1)}, u32[]{:S(2)}, u32[]{:S(2)}) collective-permute-start(bf16[2,1,96,640]{3,2,0,1:T(8,128)(2,1)S(1)} %fusion.51), channel_id=1, source_target_pairs={{0,1},{1,0},{2,3},{3,2},{4,5},{5,4},{6,7},{7,6},{8,9},{9,8},{10,11... | collective-permute-start | bytes 737288 | tf_op jit(solution)/shard_map/ppermute | solution.py:50
  551.7 120.1 %collective-permute-start.24 = (bf16[96,1152]{1,0:T(8,128)(2,1)S(1)}, bf16[96,1152]{1,0:T(8,128)(2,1)S(1)}, u32[]{:S(2)}, u32[]{:S(2)}) collective-permute-start(bf16[96,1152]{1,0:T(8,128)(2,1)S(1)} %add_convert_fusion.4), channel_id=1, source_target_pairs={{0,1},{1,0},{2,3},{3,2},{4,5},{5,4},{6,7},{7,6},{8,9},{9,8},{10,11... | collective-permute-start | bytes 663560 | tf_op jit(solution)/shard_map/ppermute | solution.py:50
  671.1 5.6 collective-permute-start.21
  677.7 6.0 collective-permute-start.22
  (71 other events, 445.2 us)
Sparse Core Ops, SparseCore 0:
  13.4 86.0 all-gather.3
  103.0 70.3 all-gather.5
  176.9 58.6 all-gather.7
  367.6 99.4 reduce-scatter.7
  470.5 70.4 reduce-scatter.5
  547.0 123.9 reduce-scatter.9

commit v2 on v1

v2 whole, which is shorter than its diff:
```python
import functools
import math

import jax
import jax.numpy as jnp
import numpy as np
from jax import lax
from jax.experimental import pallas as pl
from jax.experimental.pallas import tpu as pltpu
from jax.sharding import PartitionSpec as P

HD = 64
BUCKETS = 32
MAXDIST = 128
NORM_EPS = 1e-06
MASKED = -1e30
LANES = 128
ROW_BLOCK = 512
PEAK_FLOPS = 1.15e15
FULL_ACCURACY = lax.Precision.HIGHEST
F32 = jnp.float32
BF16 = jnp.bfloat16

PAIR = ((0, 1), (1, 0), (2, 3), (3, 2))
ACROSS = ((0, 2), (2, 0), (1, 3), (3, 1))


def bucket_table(length):
    exact = BUCKETS // 2
    hot = np.zeros((BUCKETS, length), np.float32)
    for distance in range(length):
        bucket = distance
        if distance >= exact:
            scaled = math.log(distance / exact) / math.log(MAXDIST / exact) * (BUCKETS - exact)
            bucket = min(exact + math.floor(scaled), BUCKETS - 1)
        hot[bucket, distance] = 1.0
    return hot


def dot(left, right, contract=(1, 0)):
    return lax.dot_general(
        left, right, (((contract[0],), (contract[1],)), ((), ())), preferred_element_type=F32
    )


def root_norm(values, gain):
    return values * lax.rsqrt(jnp.mean(values * values, axis=-1, keepdims=True) + NORM_EPS) * gain


def pair_swap(value):
    return lax.ppermute(value, "narrow", PAIR)


def across_swap(value):
    return lax.ppermute(value, "narrow", ACROSS)


def in_order(flag, mine, other):
    first = flag == 0
    return jnp.where(first, mine, other), jnp.where(first, other, mine)


def narrow_gather(value, axis, row, core):
    low, high = in_order(row, value, across_swap(value))
    column = jnp.stack([low, high], axis)
    low, high = in_order(core, column, pair_swap(column))
    full = jnp.stack([low, high], axis + 1)
    shape = list(value.shape)
    shape[axis] *= 4
    return full.reshape(shape)


def plus(mine, came):
    return (mine.astype(F32) + came.astype(F32)).astype(mine.dtype)


def part_of(value, index, parts, axis):
    size = value.shape[axis] // parts
    return lax.dynamic_slice_in_dim(value, index * size, size, axis)


LINE = 4
BESIDE = tuple((i, i ^ 1) for i in range(2 * LINE))


def along(step):
    return [(2 * z + x, 2 * ((z + step) % LINE) + x) for z in range(LINE) for x in range(2)]


def by_planes():
    return lax.axis_size("wide") == 2 * LINE


def assemble_kernel(widths, order_ref, *refs):
    pieces, outs = refs[: 2 * LINE], refs[2 * LINE :]
    for i, piece in enumerate(pieces):
        at = 0
        for width, out in zip(widths, outs):
            out[order_ref[i]] = piece[:, at : at + width]
            at += width


def after(value, *others):
    return lax.optimization_barrier((value, *others))[0]


def wide_gather(block, widths, first=()):
    rows = block.shape[0]
    if not by_planes():
        full = lax.all_gather(block, "wide", axis=0, tiled=True)
        bounds = np.cumsum([0, *widths])
        return [full[:, a:b] for a, b in zip(bounds[:-1], bounds[1:])]
    z, x = lax.axis_index("wide") // 2, lax.axis_index("wide") % 2
    line = [block] + [lax.ppermute(block, "wide", along(step)) for step in range(1, LINE)]
    line = after(line, *first)
    pieces = line + [lax.ppermute(piece, "wide", BESIDE) for piece in line]
    places = (z - np.arange(LINE)) % LINE * 2
    order = jnp.concatenate([places + x, places + 1 - x]).astype(jnp.int32)
    outs = pl.pallas_call(
        functools.partial(assemble_kernel, widths),
        in_specs=[pl.BlockSpec(memory_space=pltpu.SMEM)] + [pl.BlockSpec(memory_space=pltpu.VMEM)] * len(pieces),
        out_specs=[pl.BlockSpec(memory_space=pltpu.VMEM)] * len(widths),
        out_shape=[jax.ShapeDtypeStruct((2 * LINE, rows, width), block.dtype) for width in widths],
        compiler_params=pltpu.CompilerParams(vmem_limit_bytes=16 << 20),
        name="assemble",
    )(order, *pieces)
    return [out.reshape(2 * LINE * rows, out.shape[2]) for out in outs]


def shared_gather(block, row, first=()):
    rows, width = block.shape
    (full,) = wide_gather(part_of(block, row, 2, 0), (width,), first)
    halves = full.reshape(-1, rows // 2, width)
    return jnp.stack(in_order(row, halves, across_swap(halves)), 1).reshape(-1, width)


def pick(value, index, axis):
    return lax.dynamic_index_in_dim(value, index, axis, keepdims=False)


def wide_scatter_x(blocks):
    if not by_planes():
        return blocks
    x = lax.axis_index("wide") % 2
    planes = blocks.reshape(LINE, 2, *blocks.shape[1:])
    return plus(pick(planes, x, 1), lax.ppermute(pick(planes, 1 - x, 1), "wide", BESIDE))


def wide_scatter_z(planes):
    if not by_planes():
        shape = planes.shape
        return lax.psum_scatter(
            planes.reshape(shape[0] * shape[1], *shape[2:]), "wide", scatter_dimension=0, tiled=True
        )
    z = lax.axis_index("wide") // 2
    total = pick(planes, z, 0).astype(F32)
    for step in range(1, LINE):
        sent = pick(planes, (z + step) % LINE, 0)
        total = total + lax.ppermute(sent, "wide", along(step)).astype(F32)
    return total.astype(planes.dtype)


def wide_scatter(blocks):
    return wide_scatter_z(wide_scatter_x(blocks))


def transpose_columns(weight_ref, out_ref):
    for i in range(0, weight_ref.shape[1], LANES):
        out_ref[i : i + LANES, :] = weight_ref[:, i : i + LANES].T


def cost(flops, moved):
    return pl.CostEstimate(flops=int(flops), bytes_accessed=int(moved), transcendentals=0)


def position_bias(vec_ref, bias_ref):
    heads, size, _ = bias_ref.shape
    key = lax.broadcasted_iota(jnp.int32, (size, size), 0)
    query = lax.broadcasted_iota(jnp.int32, (size, size), 1)
    for h in range(heads):
        rows = jnp.broadcast_to(vec_ref[h : h + 1, :], (size, size))
        rolled = pltpu.roll(rows, 0, 1, stride=1, stride_axis=0)
        bias_ref[h] = jnp.where(key <= query, rolled, MASKED)


def self_forward_kernel(
    x_ref, gain_ref, w_ref, vec_ref, n1_ref, qkv_ref, out_ref, lse_ref, wt_ref, bias_ref
):
    heads = bias_ref.shape[0]
    width = heads * HD

    @pl.when(pl.program_id(0) == 0)
    def _():
        transpose_columns(w_ref, wt_ref)
        position_bias(vec_ref, bias_ref)

    normed = root_norm(x_ref[0].astype(F32), gain_ref[...]).astype(BF16)
    n1_ref[0] = normed
    qkv = dot(wt_ref[...], normed, (1, 1)).astype(BF16)
    qkv_ref[0] = qkv
    lse_ref[...] = jnp.zeros_like(lse_ref)
    for h in range(heads):
        q, k, v = (qkv[width * part + HD * h : width * part + HD * (h + 1)] for part in range(3))
        s = dot(k, q, (0, 0)) + bias_ref[h]
        peak = jnp.max(s, axis=0, keepdims=True)
        raised = jnp.exp(s - peak)
        total = jnp.sum(raised, axis=0, keepdims=True)
        weight = (raised * (1.0 / total)).astype(BF16)
        out_ref[0, HD * h : HD * (h + 1), :] = dot(v, weight).astype(BF16)
        lse_ref[0, h : h + 1, :] = peak + jnp.log(total)


def self_forward(x, gain, weight, vec, heads):
    examples, length, model = x.shape
    feats = weight.shape[1]
    whole = lambda *shape: pl.BlockSpec(shape, lambda e: (0,) * len(shape))
    per = lambda *shape: pl.BlockSpec((1, *shape), lambda e: (e, 0, 0))
    return pl.pallas_call(
        self_forward_kernel,
        grid=(examples,),
        in_specs=[
            per(length, model),
            whole(1, model),
            whole(*weight.shape),
            whole(*vec.shape),
        ],
        out_specs=[
            per(length, model),
            per(feats, length),
            per(heads * HD, length),
            per(8, length),
            whole(feats, model),
        ],
        out_shape=[
            jax.ShapeDtypeStruct((examples, length, model), BF16),
            jax.ShapeDtypeStruct((examples, feats, length), BF16),
            jax.ShapeDtypeStruct((examples, heads * HD, length), BF16),
            jax.ShapeDtypeStruct((examples, 8, length), F32),
            jax.ShapeDtypeStruct((feats, model), BF16),
        ],
        scratch_shapes=[pltpu.VMEM((heads, length, length), F32)],
        compiler_params=pltpu.CompilerParams(vmem_limit_bytes=48 << 20),
        cost_estimate=cost(9e-6 * PEAK_FLOPS, 8e6),
        name="self_forward",
    )(x, gain, weight, vec)


def self_backward_kernel(
    n1_ref, qkv_ref, do_ref, lse_ref, wt_ref, vec_ref,
    dn_ref, gw_ref, dvec_ref,
    bias_ref, dsum_ref, dqkv_ref,
):
    heads, size, _ = bias_ref.shape
    width = heads * HD
    e = pl.program_id(0)

    @pl.when(e == 0)
    def _():
        position_bias(vec_ref, bias_ref)
        dsum_ref[...] = jnp.zeros_like(dsum_ref)
        gw_ref[...] = jnp.zeros_like(gw_ref)
        dqkv_ref[...] = jnp.zeros_like(dqkv_ref)

    for h in range(heads):
        q, k, v = (
            qkv_ref[0, width * part + HD * h : width * part + HD * (h + 1), :] for part in range(3)
        )
        do = do_ref[0, HD * h : HD * (h + 1), :]
        s = dot(k, q, (0, 0)) + bias_ref[h]
        p = jnp.exp(s - lse_ref[0, h : h + 1, :])
        dp = dot(v, do, (0, 0))
        inner = jnp.sum(p * dp, axis=0, keepdims=True)
        ds = p * (dp - inner)
        dsum_ref[h] += ds
        ds = ds.astype(BF16)
        at = lambda part: slice(width * part + HD * h, width * part + HD * (h + 1))
        dqkv_ref[:, at(0)] = dot(k, ds).T.astype(BF16)
        dqkv_ref[:, at(1)] = dot(ds, q, (1, 1)).astype(BF16)
        dqkv_ref[:, at(2)] = dot(p.astype(BF16), do, (1, 1)).astype(BF16)
    dqkv = dqkv_ref[...]
    dn_ref[0] = dot(dqkv, wt_ref[...])
    gw_ref[...] += dot(n1_ref[0], dqkv, (0, 0))

    @pl.when(e == pl.num_programs(0) - 1)
    def _():
        dvec_ref[...] = jnp.zeros_like(dvec_ref)
        for h in range(heads):
            back, count = dsum_ref[h], size
            while count > 8:
                count //= 2
                back = back[:count] + pltpu.roll(back[count:], size - count, 1)
            total = back[:1]
            for r in range(1, count):
                total = total + pltpu.roll(back[r : r + 1], size - r, 1)
            dvec_ref[h : h + 1, :] = total


def self_backward(n1, qkv, do, lse, wt, vec, heads):
    examples, length, model = n1.shape
    feats = wt.shape[0]
    whole = lambda *shape: pl.BlockSpec(shape, lambda e: (0,) * len(shape))
    per = lambda *shape: pl.BlockSpec((1, *shape), lambda e: (e, 0, 0))
    return pl.pallas_call(
        self_backward_kernel,
        grid=(examples,),
        in_specs=[
            per(length, model),
            per(feats, length),
            per(heads * HD, length),
            per(8, length),
            whole(*wt.shape),
            whole(*vec.shape),
        ],
        out_specs=[per(length, model), whole(model, feats), whole(8, length)],
        out_shape=[
            jax.ShapeDtypeStruct((examples, length, model), F32),
            jax.ShapeDtypeStruct((model, feats), F32),
            jax.ShapeDtypeStruct((8, length), F32),
        ],
        scratch_shapes=[
            pltpu.VMEM((heads, length, length), F32),
            pltpu.VMEM((heads, length, length), F32),
            pltpu.VMEM((length, feats), BF16),
        ],
        compiler_params=pltpu.CompilerParams(vmem_limit_bytes=48 << 20),
        cost_estimate=cost(16e-6 * PEAK_FLOPS, 12e6),
        name="self_backward",
    )(n1, qkv, do, lse, wt, vec)


def work_list(live):
    examples, blocks = live.shape
    flat = live.reshape(-1)
    index = jnp.arange(flat.shape[0], dtype=jnp.int32)
    block = index % blocks
    visit = (flat > 0) | (block == 0)
    before = jnp.sum(jnp.where(visit[None, :] & (index[None, :] < index[:, None]), 1, 0), axis=1)
    ends = visit & ~jnp.any(
        visit[None, :] & (index[None, :] > index[:, None]) & (index[None, :] // blocks == index[:, None] // blocks), axis=1
    )
    chosen = (before[None, :] == index[:, None]) & visit[None, :]
    take = lambda values: jnp.sum(jnp.where(chosen, values[None, :], 0), axis=1)
    final = jnp.max(jnp.where(visit, index, 0))
    found = jnp.any(chosen, axis=1)
    at = jnp.where(found, take(index), final)
    rows = [at // blocks, at % blocks, take(flat), found & (at % blocks == 0), take(ends.astype(jnp.int32))]
    return jnp.stack([r.astype(jnp.int32) for r in rows])


def memory_project_kernel(work_ref, own_ref, other_ref, w_ref, k_ref, v_ref, wt_ref):
    i = pl.program_id(0)
    block, live = work_ref[1, i], work_ref[2, i]
    half = wt_ref.shape[0] // 2
    own_blocks = 2

    @pl.when(i == 0)
    def _():
        transpose_columns(w_ref, wt_ref)

    def project(rows):
        both = dot(wt_ref[...], rows, (1, 1)).astype(BF16)
        k_ref[0] = both[:half]
        v_ref[0] = both[half:]

    @pl.when((live > 0) & (block < own_blocks))
    def _():
        project(own_ref[0])

    @pl.when((live > 0) & (block >= own_blocks))
    def _():
        project(other_ref[0])


def memory_project(work, own, other, weight):
    examples, rows, model = own.shape
    half = rows // ROW_BLOCK
    feats = weight.shape[1] // 2
    row_spec = lambda first: pl.BlockSpec(
        (1, ROW_BLOCK, model), lambda i, work: (work[0, i], jnp.clip(work[1, i] - first, 0, half - 1), 0)
    )
    out_spec = pl.BlockSpec((1, feats, ROW_BLOCK), lambda i, work: (work[0, i], 0, work[1, i]))
    out = jax.ShapeDtypeStruct((examples, feats, 2 * rows), BF16)
    w_spec = lambda *shape: pl.BlockSpec(shape, lambda i, work: (0, 0))
    return pl.pallas_call(
        memory_project_kernel,
        grid_spec=pltpu.PrefetchScalarGridSpec(
            num_scalar_prefetch=1,
            grid=(work.shape[1],),
            in_specs=[row_spec(0), row_spec(half), w_spec(*weight.shape)],
            out_specs=[out_spec, out_spec, w_spec(2 * feats, model)],
        ),
        out_shape=[out, out, jax.ShapeDtypeStruct((2 * feats, model), BF16)],
        compiler_params=pltpu.CompilerParams(vmem_limit_bytes=48 << 20),
        cost_estimate=cost(12e-6 * PEAK_FLOPS, 12e6),
        name="memory_project",
    )(work, own, other, weight)


def cross_forward_kernel(work_ref, q_ref, k_ref, v_ref, o_ref, lse_ref, peak_ref, total_ref, acc_ref):
    i = pl.program_id(0)
    heads = acc_ref.shape[0] // HD
    live = work_ref[2, i]

    @pl.when(work_ref[3, i] == 1)
    def _():
        peak_ref[...] = jnp.full_like(peak_ref, MASKED)
        total_ref[...] = jnp.zeros_like(total_ref)
        acc_ref[...] = jnp.zeros_like(acc_ref)

    def block(partial):
        for h in range(heads):
            at = slice(HD * h, HD * (h + 1))
            s = dot(k_ref[0, at, :], q_ref[0, at, :], (0, 0))
            if partial:
                s = jnp.where(lax.broadcasted_iota(jnp.int32, s.shape, 0) < live, s, MASKED)
            before = peak_ref[h : h + 1, :]
            peak = jnp.maximum(before, jnp.max(s, axis=0, keepdims=True))
            p = jnp.exp(s - peak)
            shrink = jnp.exp(before - peak)
            peak_ref[h : h + 1, :] = peak
            total_ref[h : h + 1, :] = total_ref[h : h + 1, :] * shrink + jnp.sum(p, axis=0, keepdims=True)
            acc_ref[at, :] = acc_ref[at, :] * shrink + dot(v_ref[0, at, :], p.astype(BF16))

    @pl.when(live == ROW_BLOCK)
    def _():
        block(False)

    @pl.when((live > 0) & (live < ROW_BLOCK))
    def _():
        block(True)

    @pl.when(work_ref[4, i] == 1)
    def _():
        total = total_ref[...]
        some = total > 0
        inverse = jnp.where(some, 1.0 / jnp.where(some, total, 1.0), 0.0)
        lse_ref[0] = jnp.where(some, peak_ref[...] + jnp.log(jnp.where(some, total, 1.0)), MASKED)
        for h in range(heads):
            at = slice(HD * h, HD * (h + 1))
            o_ref[0, at, :] = (acc_ref[at, :] * inverse[h : h + 1, :]).astype(o_ref.dtype)


def cross_forward(work, q, k, v):
    examples, feats, length = q.shape
    q_spec = pl.BlockSpec((1, feats, length), lambda i, work: (work[0, i], 0, 0))
    k_spec = pl.BlockSpec((1, feats, ROW_BLOCK), lambda i, work: (work[0, i], 0, work[1, i]))
    l_spec = pl.BlockSpec((1, 8, length), lambda i, work: (work[0, i], 0, 0))
    return pl.pallas_call(
        cross_forward_kernel,
        grid_spec=pltpu.PrefetchScalarGridSpec(
            num_scalar_prefetch=1,
            grid=(work.shape[1],),
            in_specs=[q_spec, k_spec, k_spec],
            out_specs=[q_spec, l_spec],
            scratch_shapes=[
                pltpu.VMEM((8, length), F32),
                pltpu.VMEM((8, length), F32),
                pltpu.VMEM((feats, length), F32),
            ],
        ),
        out_shape=[
            jax.ShapeDtypeStruct((examples, feats, length), BF16),
            jax.ShapeDtypeStruct((examples, 8, length), F32),
        ],
        compiler_params=pltpu.CompilerParams(vmem_limit_bytes=48 << 20),
        cost_estimate=cost(30e-6 * PEAK_FLOPS, 16e6),
        name="cross_forward",
    )(work, q, k, v)


def cross_backward_kernel(
    work_ref, q_ref, do_ref, lse_ref, inner_ref, k_ref, v_ref, dq_ref, dkv_ref, acc_ref
):
    i = pl.program_id(0)
    feats = acc_ref.shape[0]
    heads = feats // HD
    live = work_ref[2, i]

    @pl.when(work_ref[3, i] == 1)
    def _():
        acc_ref[...] = jnp.zeros_like(acc_ref)

    def block(partial):
        for h in range(heads):
            at = slice(HD * h, HD * (h + 1))
            q, do, k, v = q_ref[0, at, :], do_ref[0, at, :], k_ref[0, at, :], v_ref[0, at, :]
            s = dot(k, q, (0, 0))
            p = jnp.exp(s - lse_ref[0, h : h + 1, :])
            if partial:
                p = jnp.where(lax.broadcasted_iota(jnp.int32, s.shape, 0) < live, p, 0.0)
            dp = dot(v, do, (0, 0))
            ds = (p * (dp - inner_ref[0, h : h + 1, :])).astype(BF16)
            acc_ref[at, :] += dot(k, ds)
            dkv_ref[0, :, at] = dot(ds, q, (1, 1)).astype(BF16)
            dkv_ref[0, :, feats + HD * h : feats + HD * (h + 1)] = dot(p.astype(BF16), do, (1, 1)).astype(BF16)

    @pl.when(live == ROW_BLOCK)
    def _():
        block(False)

    @pl.when((live > 0) & (live < ROW_BLOCK))
    def _():
        block(True)

    @pl.when(work_ref[4, i] == 1)
    def _():
        dq_ref[0] = acc_ref[...].T.astype(BF16)


def cross_backward(work, q, do, lse, inner, k, v):
    examples, feats, length = q.shape
    rows = k.shape[2]
    q_spec = pl.BlockSpec((1, feats, length), lambda i, work: (work[0, i], 0, 0))
    k_spec = pl.BlockSpec((1, feats, ROW_BLOCK), lambda i, work: (work[0, i], 0, work[1, i]))
    l_spec = pl.BlockSpec((1, 8, length), lambda i, work: (work[0, i], 0, 0))
    d_spec = pl.BlockSpec((1, ROW_BLOCK, 2 * feats), lambda i, work: (work[0, i], work[1, i], 0))
    return pl.pallas_call(
        cross_backward_kernel,
        grid_spec=pltpu.PrefetchScalarGridSpec(
            num_scalar_prefetch=1,
            grid=(work.shape[1],),
            in_specs=[q_spec, q_spec, l_spec, l_spec, k_spec, k_spec],
            out_specs=[
                pl.BlockSpec((1, length, feats), lambda i, work: (work[0, i], 0, 0)),
                d_spec,
            ],
            scratch_shapes=[pltpu.VMEM((feats, length), F32)],
        ),
        out_shape=[
            jax.ShapeDtypeStruct((examples, length, feats), BF16),
            jax.ShapeDtypeStruct((examples, rows, 2 * feats), BF16),
        ],
        compiler_params=pltpu.CompilerParams(vmem_limit_bytes=48 << 20),
        cost_estimate=cost(45e-6 * PEAK_FLOPS, 24e6),
        name="cross_backward",
    )(work, q, do, lse, inner, k, v)


def memory_backward_kernel(
    live_ref, own_ref, other_ref, dkv_ref, wt_ref, out_ref, out_other_ref, g_ref, sum_ref
):
    e, j = pl.program_id(0), pl.program_id(1)
    own_blocks = pl.num_programs(1) // 2

    @pl.when((e == 0) & (j == 0))
    def _():
        sum_ref[...] = jnp.zeros_like(sum_ref)

    for mine, rows_ref, to_ref in ((j < own_blocks, own_ref, out_ref), (j >= own_blocks, other_ref, out_other_ref)):

        @pl.when(mine & (live_ref[e, j] > 0))
        def _():
            dkv = dkv_ref[0]
            sum_ref[...] += dot(rows_ref[0], dkv, (0, 0))
            to_ref[0] = dot(dkv, wt_ref[...]).astype(BF16)

        @pl.when(mine & (live_ref[e, j] == 0))
        def _():
            to_ref[0] = jnp.zeros_like(to_ref[0])

    @pl.when((e == pl.num_programs(0) - 1) & (j == pl.num_programs(1) - 1))
    def _():
        g_ref[...] = sum_ref[...].astype(BF16)


def memory_backward(live, own, other, dkv, wt):
    examples, count, model = own.shape
    width = dkv.shape[2]
    half = count // ROW_BLOCK
    row_spec = lambda first: pl.BlockSpec(
        (1, ROW_BLOCK, model), lambda e, j, live: (e, jnp.clip(j - first, 0, half - 1), 0)
    )
    d_spec = pl.BlockSpec((1, ROW_BLOCK, width), lambda e, j, live: (e, j, 0))
    w_spec = pl.BlockSpec(wt.shape, lambda e, j, live: (0, 0))
    return pl.pallas_call(
        memory_backward_kernel,
        grid_spec=pltpu.PrefetchScalarGridSpec(
            num_scalar_prefetch=1,
            grid=(examples, 2 * half),
            in_specs=[row_spec(0), row_spec(half), d_spec, w_spec],
            out_specs=[row_spec(0), row_spec(half), pl.BlockSpec((model, width), lambda e, j, live: (0, 0))],
            scratch_shapes=[pltpu.VMEM((model, width), F32)],
        ),
        out_shape=[
            jax.ShapeDtypeStruct(own.shape, BF16),
            jax.ShapeDtypeStruct(own.shape, BF16),
            jax.ShapeDtypeStruct((model, width), BF16),
        ],
        compiler_params=pltpu.CompilerParams(vmem_limit_bytes=48 << 20),
        cost_estimate=cost(18e-6 * PEAK_FLOPS, 30e6),
        name="memory_backward",
    )(live, own, other, dkv, wt)


def place_index(place_ref, flip):
    return jnp.bitwise_xor(place_ref[0], flip)


def strip(index, size):
    return pl.ds(pl.multiple_of(index * size, size), size)


def self_output_kernel(
    place_ref, x_ref, o0_ref, o1_ref, o2_ref, o3_ref, mine_ref, other_ref, gain_ref,
    n2_ref, q_ref, x1_ref, own_o_ref, wo_ref, wq_ref,
    rows_ref,
):
    core = jnp.bitwise_and(place_ref[0], 1)
    feats = wq_ref.shape[1]
    width = o0_ref.shape[1]
    own = x1_ref.shape[1]

    @pl.when(pl.program_id(0) == 0)
    def _():
        for i, from_ref in ((core, mine_ref), (1 - core, other_ref)):
            wo_ref[:, strip(i, feats)] = from_ref[:, feats:]
        for i, from_ref in enumerate((mine_ref, other_ref)):
            for at in range(0, feats, LANES):
                wq_ref[i, at : at + LANES, :] = from_ref[:, at : at + LANES].T

    x1 = x_ref[0].astype(F32)
    for flip, o_ref in enumerate((o0_ref, o1_ref, o2_ref, o3_ref)):
        heads = strip(place_index(place_ref, flip), width)
        x1 += dot(o_ref[0], wo_ref[heads, :], (0, 0))
        own_o_ref[0, heads, :] = o_ref[0, :, strip(place_ref[0], own)]
    n2 = root_norm(x1, gain_ref[...]).astype(BF16)
    n2_ref[0] = n2
    q_ref[0] = dot(wq_ref[0], n2, (1, 1)).astype(BF16)
    rows_ref[...] = x1
    x1_ref[0] = rows_ref[strip(place_ref[0], own), :]


def self_output_stage(place, x, pieces, mine, other, gain):
    examples, length, model = x.shape
    own, feats, width = length // 4, model // 2, pieces[0].shape[1]
    whole = lambda *shape: pl.BlockSpec(shape, lambda e: (0,) * len(shape))
    per = lambda *shape: pl.BlockSpec((1, *shape), lambda e: (e, 0, 0))
    array = jax.ShapeDtypeStruct
    return pl.pallas_call(
        self_output_kernel,
        grid=(examples,),
        in_specs=[pl.BlockSpec(memory_space=pltpu.SMEM), per(length, model)]
        + [per(width, length)] * 4
        + [whole(*mine.shape), whole(*other.shape), whole(1, model)],
        out_specs=[
            per(length, model),
            per(feats, length),
            per(own, model),
            per(model, own),
            whole(model, model),
            whole(2, feats, model),
        ],
        out_shape=[
            array((examples, length, model), BF16),
            array((examples, feats, length), BF16),
            array((examples, own, model), F32),
            array((examples, model, own), BF16),
            array((model, model), BF16),
            array((2, feats, model), BF16),
        ],
        scratch_shapes=[pltpu.VMEM((length, model), F32)],
        compiler_params=pltpu.CompilerParams(vmem_limit_bytes=48 << 20),
        cost_estimate=cost(6e-6 * PEAK_FLOPS, 10e6),
        name="self_output_stage",
    )(place, x, *pieces, mine, other, gain)


def combine_kernel(place_ref, o_ref, came_ref, lse_ref, other_lse_ref, chip_ref, total_ref):
    row = lax.shift_right_logical(place_ref[0], 1)
    here = strip(row, came_ref.shape[2])
    one, two = lse_ref[0], other_lse_ref[0]
    peak = jnp.maximum(one, two)
    total_ref[0] = peak + jnp.log(jnp.exp(one - peak) + jnp.exp(two - peak))
    own_weight = jnp.exp(lse_ref[0, :, here] - total_ref[0, :, here])
    other_weight = jnp.exp(other_lse_ref[0, :, here] - total_ref[0, :, here])
    for h in range(o_ref.shape[1] // HD):
        at = slice(HD * h, HD * (h + 1))
        one = o_ref[0, at, here].astype(F32) * own_weight[h : h + 1, :]
        chip_ref[0, at, :] = (one + came_ref[0, at, :].astype(F32) * other_weight[h : h + 1, :]).astype(BF16)


def combine(place, o, came, lse, other_lse):
    examples, feats, length = o.shape
    per = lambda *shape: pl.BlockSpec((1, *shape), lambda e: (e, 0, 0))
    return pl.pallas_call(
        combine_kernel,
        grid=(examples,),
        in_specs=[
            pl.BlockSpec(memory_space=pltpu.SMEM),
            per(feats, length),
            per(feats, length // 2),
            per(8, length),
            per(8, length),
        ],
        out_specs=[per(feats, length // 2), per(8, length)],
        out_shape=[
            jax.ShapeDtypeStruct((examples, feats, length // 2), BF16),
            jax.ShapeDtypeStruct((examples, 8, length), F32),
        ],
        compiler_params=pltpu.CompilerParams(vmem_limit_bytes=24 << 20),
        cost_estimate=cost(2e-6 * PEAK_FLOPS, 3e6),
        name="combine",
    )(place, o, came, lse, other_lse)


def norm_back(values, gain, grad):
    scale = lax.rsqrt(jnp.mean(values * values, axis=-1, keepdims=True) + NORM_EPS)
    pulled = grad * gain
    inner = jnp.mean(values * pulled, axis=-1, keepdims=True)
    back = scale * pulled - values * (scale * scale * scale * inner)
    return back, jnp.sum(grad * values * scale, axis=0, keepdims=True)


def feed_forward_kernel(
    place_ref, x1_ref, mine_ref, other_ref, dy_ref, gain_ref, wo_ref, gate_ref, up_ref, down_ref,
    out_ref, dx2_ref, doc_mine_ref, doc_other_ref, inner_mine_ref, inner_other_ref,
    g_ref, g_sent_ref, g_down_ref, g_down_sent_ref, g_out_ref, g_out_sent_ref, g_gain_ref,
    x2_ref, n3_ref, sum_ref, dn3_ref, g_full_ref, *, piece,
):
    i = pl.program_id(0)
    core = jnp.bitwise_and(place_ref[0], 1)
    examples, feats, own = mine_ref.shape

    def deal(low, high, keep_ref, sent_ref):
        keep_ref[...] = jnp.where(core == 0, low, high).astype(BF16)
        sent_ref[...] = jnp.where(core == 0, high, low).astype(BF16)
    sides = ((core, mine_ref, doc_mine_ref, inner_mine_ref), (1 - core, other_ref, doc_other_ref, inner_other_ref))

    @pl.when(i == 0)
    def _():
        for e in range(examples):
            x2 = x1_ref[own * e : own * (e + 1), :]
            for side, o_ref, *_ in sides:
                x2 += dot(o_ref[e], wo_ref[strip(side, feats), :], (0, 0))
            x2_ref[own * e : own * (e + 1), :] = x2
        n3_ref[...] = root_norm(x2_ref[...], gain_ref[...]).astype(BF16)
        sum_ref[...] = jnp.zeros_like(sum_ref)
        dn3_ref[...] = jnp.zeros_like(dn3_ref)

    n3, dy = n3_ref[...], dy_ref[...]
    a, u = dot(n3, gate_ref[...]), dot(n3, up_ref[...])
    dh = dot(dy, down_ref[...], (1, 1))
    root = math.sqrt(2 / math.pi)
    bent = jnp.tanh(root * (a + 0.044715 * (a * a * a)))
    rise = 0.5 * (1.0 + bent)
    gelu = a * rise
    slope = rise + 0.5 * a * (1.0 - bent * bent) * (root * (1.0 + 3 * 0.044715 * (a * a)))
    hidden = (gelu * u).astype(BF16)
    da = (dh * u * slope).astype(BF16)
    du = (dh * gelu).astype(BF16)
    sum_ref[...] += dot(hidden, down_ref[...])
    g_down = dot(hidden, dy, (0, 0))
    pieces = g_down.reshape(g_down.shape[0] // (2 * piece), 2, piece, g_down.shape[1])
    deal(*(pieces[:, side].reshape(g_down_ref.shape) for side in range(2)), g_down_ref, g_down_sent_ref)
    deal(dot(n3, da, (0, 0)), dot(n3, du, (0, 0)), g_ref, g_sent_ref)
    dn3_ref[...] += dot(da, gate_ref[...], (1, 1)) + dot(du, up_ref[...], (1, 1))

    @pl.when(i == pl.num_programs(0) - 1)
    def _():
        x2 = x2_ref[...]
        out_ref[...] = (x2 + sum_ref[...]).astype(BF16)
        back, g_gain = norm_back(x2, gain_ref[...], dn3_ref[...])
        g_gain_ref[...] = g_gain
        dx2 = dy_ref[...].astype(F32) + back
        dx2_ref[...] = dx2
        n3_ref[...] = dx2.astype(BF16)
        for side, o_ref, doc_ref, inner_ref in sides:
            heads = strip(side, feats)
            total = jnp.zeros((feats, wo_ref.shape[1]), F32)
            inner_ref[...] = jnp.zeros_like(inner_ref)
            for e in range(examples):
                dx2r = n3_ref[own * e : own * (e + 1), :]
                total += dot(o_ref[e], dx2r)
                doc = dot(wo_ref[heads, :], dx2r, (1, 1)).astype(BF16)
                doc_ref[e] = doc
                product = doc.astype(F32) * o_ref[e].astype(F32)
                for h in range(feats // HD):
                    inner_ref[e, h : h + 1, :] = jnp.sum(product[HD * h : HD * (h + 1)], axis=0, keepdims=True)
            g_full_ref[heads, :] = total
        deal(g_full_ref[:, :feats], g_full_ref[:, feats:], g_out_ref, g_out_sent_ref)


def feed_forward(place, x1, mine, other, dy, gain, wide_w, down, piece):
    tokens, model = x1.shape
    examples, feats, own = mine.shape
    hidden = down.shape[0]
    part = 256
    whole = lambda *shape: pl.BlockSpec(shape, lambda i: (0,) * len(shape))
    first = model // part
    array = jax.ShapeDtypeStruct
    return pl.pallas_call(
        functools.partial(feed_forward_kernel, piece=piece),
        grid=(hidden // part,),
        in_specs=[
            pl.BlockSpec(memory_space=pltpu.SMEM),
            whole(tokens, model),
            whole(*mine.shape),
            whole(*other.shape),
            whole(tokens, model),
            whole(1, model),
            whole(model, model),
            pl.BlockSpec((model, part), lambda i: (0, first + i)),
            pl.BlockSpec((model, part), lambda i: (0, first + hidden // part + i)),
            pl.BlockSpec((part, model), lambda i: (i, 0)),
        ],
        out_specs=[
            whole(tokens, model),
            whole(tokens, model),
            whole(*mine.shape),
            whole(*mine.shape),
            whole(examples, 8, own),
            whole(examples, 8, own),
            *[pl.BlockSpec((model, part), lambda i: (0, i))] * 2,
            *[pl.BlockSpec((part // 2, model), lambda i: (i, 0))] * 2,
            *[whole(model, feats)] * 2,
            whole(1, model),
        ],
        out_shape=[
            array((tokens, model), BF16),
            array((tokens, model), F32),
            array(mine.shape, BF16),
            array(mine.shape, BF16),
            array((examples, 8, own), F32),
            array((examples, 8, own), F32),
            *[array((model, hidden), BF16)] * 2,
            *[array((hidden // 2, model), BF16)] * 2,
            *[array((model, feats), BF16)] * 2,
            array((1, model), F32),
        ],
        scratch_shapes=[
            pltpu.VMEM((tokens, model), F32),
            pltpu.VMEM((tokens, model), BF16),
            pltpu.VMEM((tokens, model), F32),
            pltpu.VMEM((tokens, model), F32),
            pltpu.VMEM((model, model), F32),
        ],
        compiler_params=pltpu.CompilerParams(vmem_limit_bytes=48 << 20),
        cost_estimate=cost(20e-6 * PEAK_FLOPS, 24e6),
        name="feed_forward",
    )(place, x1, mine, other, dy, gain, wide_w, wide_w, wide_w, down)


def self_output_back_kernel(
    mine_ref, other_ref, wq_ref, x1_ref, gain_ref, dx2_ref, own_o_ref, wo_ref,
    dx1_ref, do_ref, g_out_ref, g_gain_ref,
    sum_ref,
):
    e = pl.program_id(0)

    @pl.when(e == 0)
    def _():
        sum_ref[...] = jnp.zeros_like(sum_ref)
        g_gain_ref[...] = jnp.zeros_like(g_gain_ref)

    dn2 = dot(mine_ref[0], wq_ref[0]) + dot(other_ref[0], wq_ref[1])
    back, g_gain = norm_back(x1_ref[0], gain_ref[...], dn2)
    g_gain_ref[...] += g_gain
    dx1 = dx2_ref[0] + back
    dx1_ref[0] = dx1
    dx1r = dx1.astype(BF16)
    do_ref[0] = dot(wo_ref[...], dx1r, (1, 1)).astype(BF16)
    sum_ref[...] += dot(own_o_ref[0], dx1r)

    @pl.when(e == pl.num_programs(0) - 1)
    def _():
        g_out_ref[...] = sum_ref[...].astype(BF16)


def self_output_back(mine, other, wq, x1, gain, dx2, own_o, wo):
    examples, own, model = x1.shape
    feats = mine.shape[2]
    whole = lambda *shape: pl.BlockSpec(shape, lambda e: (0,) * len(shape))
    per = lambda *shape: pl.BlockSpec((1, *shape), lambda e: (e, 0, 0))
    array = jax.ShapeDtypeStruct
    return pl.pallas_call(
        self_output_back_kernel,
        grid=(examples,),
        in_specs=[
            per(own, feats),
            per(own, feats),
            whole(*wq.shape),
            per(own, model),
            whole(1, model),
            per(own, model),
            per(model, own),
            whole(model, model),
        ],
        out_specs=[per(own, model), per(model, own), whole(model, model), whole(1, model)],
        out_shape=[
            array((examples, own, model), F32),
            array((examples, model, own), BF16),
            array((model, model), BF16),
            array((1, model), F32),
        ],
        scratch_shapes=[pltpu.VMEM((model, model), F32)],
        compiler_params=pltpu.CompilerParams(vmem_limit_bytes=48 << 20),
        cost_estimate=cost(4e-6 * PEAK_FLOPS, 8e6),
        name="self_output_back",
    )(mine, other, wq, x1, gain, dx2, own_o, wo)


def fold_rows(rows, target, columns):
    rest = rows * columns // target
    tile = 16
    if rows % tile or target % tile or rows * target != columns * rest or rows // tile * LANES != rest:
        return (lambda b: b.reshape(*b.shape[:-2], target, rest)), (lambda b: b.reshape(rows, columns))

    def swap(b, down, across):
        b = b.reshape(*b.shape[:-2], down, tile, across, LANES)
        return jnp.swapaxes(b, -4, -2).reshape(*b.shape[:-4], across * tile, down * LANES)

    return (lambda b: swap(b, rows // tile, columns // LANES)), (lambda b: swap(b, target // tile, rest // LANES))


def local(
    dec_input,
    enc_out,
    enc_len,
    cotangent,
    self_query,
    self_key,
    self_value,
    self_output,
    cross_query,
    cross_key,
    cross_value,
    cross_output,
    ffn_gate,
    ffn_up,
    ffn_down,
    self_gain,
    cross_gain,
    ffn_gain,
    bias_table,
):
    place = lax.axis_index("narrow")
    row, core = place // 2, place % 2
    wide = lax.axis_size("wide")
    examples, own, model = dec_input.shape
    length = 4 * own
    heads = model // HD
    own_heads = heads // 4
    memory_rows = enc_out.shape[1]
    share = self_query.shape[0]

    half = lambda w: part_of(w.astype(BF16), core, 2, 1)
    own_qkv = jnp.concatenate(
        [part_of(w.astype(BF16), place, 4, 1) for w in (self_query, self_key, self_value)], 1
    )
    own_qkv = jnp.pad(own_qkv, ((0, 0), (0, -own_qkv.shape[1] % LANES)))
    small = jnp.stack([self_gain, cross_gain, ffn_gain, jnp.pad(bias_table, (0, share - bias_table.shape[0]))], 1)
    small = jnp.pad(small.astype(BF16), ((0, 0), (0, LANES - 4)))
    feats = model // 2
    self_w, small = wide_gather(jnp.concatenate([own_qkv, small], 1), (own_qkv.shape[1], LANES))
    small_rows = small[:, :4].astype(F32).T
    gain_one, gain_two, gain_three = (small_rows[i : i + 1] for i in range(3))
    table = small_rows[3].reshape(wide, share)[:, : bias_table.shape[0]].reshape(BUCKETS, heads)

    both = ("wide", "narrow")
    quarter = lambda w: part_of(w.astype(BF16), place, 4, 0)
    ffn_in = lax.all_gather(
        jnp.concatenate([quarter(cross_output), quarter(ffn_gate), quarter(ffn_up)], 1), both, axis=0, tiled=True
    )
    down_w = lax.all_gather(quarter(ffn_down), both, axis=0, tiled=True)

    enc_other = pair_swap(enc_out)
    starts = (place * memory_rows + np.arange(memory_rows // ROW_BLOCK) * ROW_BLOCK).astype(jnp.int32)
    other_starts = starts + (1 - 2 * core) * memory_rows
    block_starts = jnp.concatenate([starts, other_starts])
    live = jnp.clip(enc_len[:, None] - block_starts[None, :], 0, ROW_BLOCK)

    x_all = narrow_gather(dec_input, 1, row, core)
    hot = jnp.asarray(bucket_table(length))
    distance_bias = jnp.dot(table.T, hot, precision=FULL_ACCURACY)
    vec = jnp.pad(part_of(distance_bias, place, 4, 0), ((0, 8 - own_heads), (0, 0)))
    n1, qkv, self_o, self_lse, self_wt = self_forward(x_all, gain_one, self_w, vec, own_heads)
    across_o = across_swap(self_o)
    pieces = [self_o, pair_swap(self_o), across_o, pair_swap(across_o)]
    memory_w = shared_gather(jnp.concatenate([half(cross_key), half(cross_value)], 1), row, first=(self_o,))
    work = work_list(live)
    keys, values, memory_wt = memory_project(work, enc_out, enc_other, memory_w)
    query_out = after(jnp.concatenate([half(cross_query), half(self_output)], 1), self_o)
    mine_w = shared_gather(query_out, row)
    mine_w = after(mine_w, keys)
    other_w = pair_swap(mine_w)
    me = place.reshape(1).astype(jnp.int32)
    n2, cross_q, x1, own_o, self_out_w, cross_query_wt = self_output_stage(
        me, x_all, pieces, mine_w, other_w, gain_two
    )

    part_o, part_lse = cross_forward(work, cross_q, keys, values)
    came = across_swap(part_of(part_o, 1 - row, 2, 2))
    chip_o, lse = combine(me, part_o, came, part_lse, across_swap(part_lse))
    mine_o, other_o = part_of(chip_o, core, 2, 2), pair_swap(part_of(chip_o, 1 - core, 2, 2))

    tokens = examples * own
    down_rows = ffn_down.shape[0] // 2
    (
        layer_out, dx2, doc_mine, doc_other, inner_mine, inner_other,
        gate_up, gate_up_sent, down, down_sent, grad_co, co_sent, grad_gain_three,
    ) = feed_forward(
        me, x1.reshape(tokens, model), mine_o, other_o, cotangent.reshape(tokens, model), gain_three,
        ffn_in, down_w, down_rows,
    )
    layer_out, dx2 = layer_out.reshape(x1.shape), dx2.reshape(x1.shape)

    rows_of = lambda g: g.reshape(wide, share, -1)
    to_chip = lambda mine, other: jnp.concatenate(in_order(core, mine, pair_swap(other)), 2)
    doc, inner = to_chip(doc_mine, doc_other), to_chip(inner_mine, inner_other)
    doc_came, inner_came = across_swap(doc), across_swap(inner)
    fold, unfold = fold_rows(down_rows, share, model)
    gate_up = plus(gate_up, pair_swap(gate_up_sent))
    early = jnp.concatenate(
        [
            rows_of(plus(grad_co, pair_swap(co_sent))),
            fold(plus(down, pair_swap(down_sent)).reshape(wide, down_rows, model)),
        ],
        2,
    )
    doc_came, inner_came, early, gate_up = lax.optimization_barrier((doc_came, inner_came, early, gate_up))
    early_sum = lax.psum_scatter(
        early.reshape(wide * share, -1), "wide", scatter_dimension=0, tiled=True
    )
    to_all = lambda mine, came: jnp.concatenate(in_order(row, mine, came), 2)
    part_dq, dkv = cross_backward(
        work, cross_q, to_all(doc, doc_came), lse, to_all(inner, inner_came), keys, values
    )

    gate_up_came = across_swap(part_of(gate_up, 1 - row, 2, 1))
    part_dq, dkv, gate_up_came = lax.optimization_barrier((part_dq, dkv, gate_up_came))
    gate_up = wide_scatter_x(rows_of(plus(part_of(gate_up, row, 2, 1), gate_up_came)))

    dq_came = across_swap(part_of(part_dq, 1 - row, 2, 1))
    enc_mine, enc_swapped, grad_memory = memory_backward(live, enc_out, enc_other, dkv, memory_wt)
    enc_came = pair_swap(enc_swapped)
    dq_came, grad_memory, gate_up = lax.optimization_barrier((dq_came, grad_memory, gate_up))
    gate_up_sum = wide_scatter_z(gate_up)
    chip_dq = plus(part_of(part_dq, row, 2, 1), dq_came)
    dq_mine, dq_other = part_of(chip_dq, core, 2, 1), pair_swap(part_of(chip_dq, 1 - core, 2, 1))
    grad_cross_query = jnp.einsum("etd,etf->df", n2, part_dq, preferred_element_type=F32).astype(BF16)
    late = wide_scatter_x(jnp.concatenate([rows_of(grad_cross_query), rows_of(grad_memory)], 2))
    dx1, do, grad_self_output, grad_gain_two = self_output_back(
        dq_mine, dq_other, cross_query_wt, x1, gain_two, dx2, own_o, self_out_w
    )
    enc_grad = plus(enc_mine, enc_came)

    low, high = in_order(row, part_of(do, row, 2, 1), across_swap(part_of(do, 1 - row, 2, 1)))
    column = jnp.stack([low, high], 2)
    low, high = in_order(core, part_of(column, core, 2, 1), pair_swap(part_of(column, 1 - core, 2, 1)))
    do_heads = jnp.stack([low, high], 3).reshape(examples, own_heads * HD, length)
    do_heads, late, enc_grad, gate_up_sum = lax.optimization_barrier((do_heads, late, enc_grad, gate_up_sum))
    part_dn1, grad_self, dvec = self_backward(n1, qkv, do_heads, self_lse, self_wt, vec, own_heads)
    late_sum = wide_scatter_z(late)
    part_dn1, grad_self, late_sum = lax.optimization_barrier((part_dn1, grad_self, late_sum))
    by_core = part_dn1.reshape(examples, 2, 2, own, model)
    column = part_of(by_core, core, 2, 2) + pair_swap(part_of(by_core, 1 - core, 2, 2).astype(BF16)).astype(F32)
    dn1 = part_of(column, row, 2, 1) + across_swap(part_of(column, 1 - row, 2, 1).astype(BF16)).astype(F32)
    grad_in, grad_gain_one = norm_back(
        dec_input.reshape(tokens, model).astype(F32), gain_one, dn1.reshape(tokens, model)
    )
    input_grad = (dx1 + grad_in.reshape(x1.shape)).astype(BF16)

    so = rows_of(plus(part_of(grad_self_output, core, 2, 1), pair_swap(part_of(grad_self_output, 1 - core, 2, 1))))
    so = plus(part_of(so, row, 2, 1), across_swap(part_of(so, 1 - row, 2, 1)))
    self_width = grad_self.shape[1]
    self_halves = grad_self.astype(BF16).reshape(wide, 2, share // 2, self_width)
    last = wide_scatter(jnp.concatenate([self_halves[:, 0], self_halves[:, 1], so], 2))
    low, high = in_order(row, last, across_swap(last))
    last = jnp.stack([low, high])
    low, high = in_order(core, last, pair_swap(last))
    halves = lambda part: jnp.concatenate([part[:, :self_width], part[:, self_width : 2 * self_width]], 0)
    self_sum = [halves(part[y]) for y in range(2) for part in (low, high)]
    q_sum, k_sum, v_sum = (
        jnp.concatenate([part[:, own_heads * HD * i : own_heads * HD * (i + 1)] for part in self_sum], 1)
        for i in range(3)
    )
    so_sum = jnp.concatenate(
        [part[:, :, 2 * self_width :].reshape(share, -1) for part in (low, high)], 1
    )

    early_sum = plus(early_sum, across_swap(early_sum))
    low, high = in_order(core, early_sum, pair_swap(early_sum))
    co_sum = jnp.concatenate([part[:, :feats] for part in (low, high)], 1)
    down_sum = jnp.concatenate([unfold(part[:, feats:]) for part in (low, high)], 0)
    gate_up_sum = jnp.concatenate(in_order(row, gate_up_sum, across_swap(gate_up_sum)), 1)
    gate_sum, up_sum = in_order(core, gate_up_sum, pair_swap(gate_up_sum))
    late_sum = plus(late_sum, across_swap(late_sum))
    low, high = in_order(core, late_sum, pair_swap(late_sum))
    cq_sum, ck_sum, cv_sum = (
        jnp.concatenate([part[:, feats * i : feats * (i + 1)] for part in (low, high)], 1) for i in range(3)
    )

    own_table = jnp.dot(hot, dvec[:own_heads].T, precision=FULL_ACCURACY)
    grad_table = lax.dynamic_update_slice_in_dim(
        jnp.zeros((BUCKETS, heads), F32), own_table, place * own_heads, 1
    )
    small = jnp.concatenate(
        [g.reshape(wide, share) for g in (grad_gain_one, grad_gain_two, grad_gain_three)]
        + [grad_table.reshape(wide, bias_table.shape[0])], 1
    )
    small = small + pair_swap(small)
    small = small + across_swap(small)
    small_sum = wide_scatter(small.reshape(wide, 1, -1)).reshape(-1)
    f = lambda a: a.astype(F32)
    return (
        layer_out,
        input_grad,
        enc_grad,
        *(f(g) for g in (q_sum, k_sum, v_sum, so_sum, cq_sum, ck_sum, cv_sum, co_sum, gate_sum, up_sum, down_sum)),
        small_sum[:share],
        small_sum[share : 2 * share],
        small_sum[2 * share : 3 * share],
        small_sum[3 * share :],
    )


def solution(mesh):
    rows = P("wide", "narrow", None)
    weight, vector = P("wide", None), P("wide")
    return jax.shard_map(
        local,
        mesh=mesh,
        in_specs=(rows, rows, vector, rows, *[weight] * 11, *[vector] * 4),
        out_specs=(rows, rows, rows, *[weight] * 11, *[vector] * 4),
        check_vma=False,
    )
```

time: 703 us -> 509 us (0.72)
  waiting for transfers between devices: 320 us -> 121 us
  starting transfers between devices: 31.6 us -> 97.6 us
  matrix products: 57.8 us -> 2.62 us
  local copies, waits for them, and re-layouts: 63.6 us -> 36.7 us
  other arithmetic: 41.1 us -> 59.7 us
    unnamed x7 -> x3, waiting for transfers between devices: 115 us -> 0.05 us
    ppermute x0 -> x37, starting transfers between devices: none -> 67.1 us  [the longest x12 29.1 us: wide_scatter_z(): total = total + lax.ppermute(sent, 'wide', along(step)).astype(F32)]
    all_gather x2 -> x1, waiting for transfers between devices: 61.3 us -> 0.01 us  [local(): lax.all_gather(jnp.concatenate([quarter(cross_output), quarter(ffn_gate),...]
    ppermute x0 -> x37, waiting for transfers between devices: none -> 57.9 us  [the longest x4 19.7 us: wide_scatter_x(): lax.ppermute(pick(planes, 1 - x, 1), 'wide', BESIDE)]
    dot_general x18 -> x1, matrix products: 57.4 us -> 1.42 us  [local(): jnp.einsum('etd,etf->df', n2, part_dq, preferred_element_type=F32)]
    reduce_scatter x2 -> x1, waiting for transfers between devices: 51.5 us -> 0.01 us  [local(): lax.psum_scatter(early.reshape(wide * share, -1), 'wide', scatter_dimensi...]
    pallas_call x0 -> x7, Pallas kernels: none -> 41.9 us  [the longest x1 23.6 us: feed_forward(): pl.pallas_call(functools.partial(feed_forward_kernel, piece=piece), grid=...]
    ppermute x13 -> x18, waiting for transfers between devices: 89.2 us -> 48.8 us  [across_swap(): return lax.ppermute(value, 'narrow', ACROSS)]
  transfers between devices with their start and end apart: 33 -> 79, of which waited for: 15 -> 35; matrix products, arithmetic and copies ran while one was open for 16% -> 15% of each run, Pallas kernels for 14% -> 29%
where the time goes in v2:
time: 509 us; the launch traced here: 501 us
  Pallas kernels  168 us (33%)
  waiting for transfers between devices  121 us (24%)
  starting transfers between devices  97.6 us (19%)
  other arithmetic  59.7 us (12%)
  local copies, waits for them, and re-layouts  36.7 us (7%)
  between operations  15.5 us (3%)
    ppermute x18, waiting for transfers between devices, across_swap(): return lax.ppermute(value, 'narrow', ACROSS)  48.8 us
    pallas_call x1, Pallas kernels, cross_backward(): pl.pallas_call(cross_backward_kernel, grid_spec=pltpu.PrefetchScalarGridS...  38.9 us
    ppermute x12, starting transfers between devices, wide_scatter_z(): total = total + lax.ppermute(sent, 'wide', along(step)).astype(F32)  29.1 us
    pallas_call x1, Pallas kernels, cross_forward(): pl.pallas_call(cross_forward_kernel, grid_spec=pltpu.PrefetchScalarGridSp...  26.5 us
    pallas_call x1, Pallas kernels, feed_forward(): pl.pallas_call(functools.partial(feed_forward_kernel, piece=piece), grid=...  23.6 us
    convert_element_type x13, other arithmetic, plus(): return (mine.astype(F32) + came.astype(F32)).astype(mine.dtype)  21.7 us
    ppermute x21, starting transfers between devices, pair_swap(): return lax.ppermute(value, 'narrow', PAIR)  20.5 us
    pallas_call x1, Pallas kernels, memory_backward(): pl.pallas_call(memory_backward_kernel, grid_spec=pltpu.PrefetchScalarGrid...  20.3 us
  transfers between devices with their start and end apart: 79, of which 35 were waited for; matrix products, arithmetic and copies ran while one was open for 15% of the time, Pallas kernels for 29%

profile of v2, /device:TPU:9, one launch (start us, length us, event | category | flops | bytes accessed | tf_op | source)
XLA Modules:
  0.0 501.0 jit_solution(3530613170122309267)
XLA Ops:
  26.3 4.8 collective-permute-done.3.refs_2_
  44.5 5.2 %collective-permute-done.7.refs_6_ = bf16[96,768]{1,0:T(8,128)(2,1)S(1)} collective-permute-done((bf16[96,768]{1,0:T(8,128)(2,1)S(1)}, bf16[96,768]{1,0:T(8,128)(2,1)S(1)}, u32[]{:S(2)}, u32[]{:S(2)}) %collective-permute-start.7) | collective-permute-done | bytes 147488 | tf_op jit(solution)/shard_map/ppermute | solution.py:116
  49.7 3.9 collective-permute-done.8.refs_7_
  60.8 10.2 %self_forward.1 = (bf16[3,512,768]{2,1,0:T(8,128)(2,1)}, bf16[3,640,512]{2,1,0:T(8,128)(2,1)S(1)}, bf16[3,192,512]{2,1,0:T(8,128)(2,1)S(1)}, f32[3,8,512]{2,1,0:T(8,128)S(1)}, bf16[640,768]{1,0:T(8,128)(2,1)S(1)}) custom-call(bf16[3,512,768]{2,1,0:T(8,128)(2,1)} %bitcast.219, f32[1,768]{1,0:T(1,128)S(1)} %get-tuple-element.255.gain_ref, ...), custom_call_target="tpu_custom_call" | custom-call | flops 10350000128 | bytes 8000000 | tf_op jit(solution)/shard_map/self_forward/pallas_call | solution.py:218
  92.9 2.8 collective-permute-done.28
  97.0 11.8 %collective-permute-done.19 = bf16[8,48,768]{2,1,0:T(8,128)(2,1)} collective-permute-done((bf16[8,48,768]{2,1,0:T(8,128)(2,1)S(1)}, bf16[8,48,768]{2,1,0:T(8,128)(2,1)}, u32[]{:S(2)}, u32[]{:S(2)}) %collective-permute-start.19) | collective-permute-done | bytes 589856 | tf_op jit(solution)/shard_map/ppermute | solution.py:55
  111.3 12.6 %memory_project.1 = (bf16[3,384,2048]{2,1,0:T(8,128)(2,1)}, bf16[3,384,2048]{2,1,0:T(8,128)(2,1)}, bf16[768,768]{1,0:T(8,128)(2,1)S(1)}) custom-call(s32[5,12]{1,0:T(8,128)S(1)} %stack.111.work_ref, bf16[3,1024,768]{2,1,0:T(8,128)(2,1)} %own_ref.3, bf16[3,1024,768]{2,1,0:T(8,128)(2,1)} %collective-permute-done.20.other_ref, bf16[768,768]{1,0:T(8,128)(2,1)S(1)} %bitcast.205), custom_call_target="tpu_custom_call" | custom-call | flops 13799999488 | bytes 12000000 | tf_op jit(solution)/shard_map/memory_project/pallas_call | solution.py:384
  125.0 4.7 collective-permute-start.29
  130.2 3.5 collective-permute-done.9.o1_ref
  135.4 9.4 %self_output_stage.1 = (bf16[3,512,768]{2,1,0:T(8,128)(2,1)}, bf16[3,384,512]{2,1,0:T(8,128)(2,1)S(1)}, f32[3,128,768]{2,1,0:T(8,128)S(1)}, bf16[3,768,128]{2,1,...) custom-call(s32[1]{0:T(128)} %bitcast.place_ref, bf16[3,512,768]{2,1,0:T(8,128)(2,1)} %bitcast.220, ...), custom_call_target="tpu_custom_call" | custom-call | flops 6899999744 | bytes 10000000 | tf_op jit(solution)/shard_map/self_output_stage/pallas_call | solution.py:639
  145.6 26.5 %cross_forward.1 = (bf16[3,384,512]{2,1,0:T(8,128)(2,1)S(1)}, f32[3,8,512]{2,1,0:T(8,128)S(1)}) custom-call(s32[5,12]{1,0:T(8,128)S(1)} %stack.111.work_ref, bf16[3,384,512]{2,1,0:T(8,128)(2,1)S(1)} %get-tuple-element.113.q_ref, bf16[3,384,2048]{2,1,0:T(8,128)(2,1)} %get-tuple-element.110.k_ref, bf16[3,384,2048]{2,1,0:T(8,128)(2,1)} %get-tuple-element.114.v_ref), custom_call_target="tpu_custom_call" | custom-call | flops 34500001792 | bytes 16000000 | tf_op jit(solution)/shard_map/cross_forward/pallas_call | solution.py:448
  173.8 14.2 %collective-permute-done.31.other_lse_ref = f32[3,8,512]{2,1,0:T(8,128)S(1)} collective-permute-done((f32[3,8,512]{2,1,0:T(8,128)S(1)}, f32[3,8,512]{2,1,0:T(8,128)S(1)}, u32[]{:S(2)}, u32[]{:S(2)}) %collective-permute-start.31) | collective-permute-done | bytes 49184 | tf_op jit(solution)/shard_map/ppermute | solution.py:55
  191.4 23.6 %feed_forward.1 = (bf16[384,768]{1,0:T(8,128)(2,1)}, f32[384,768]{1,0:T(8,128)S(1)}, bf16[3,384,128]{2,1,0:T(8,128)(2,1)S(1)}, bf16[3,384,128]{2,1,0:T(8,128)(2,...) custom-call(s32[1]{0:T(128)} %bitcast.place_ref, ...), custom_call_target="tpu_custom_call" | custom-call | flops 23000000512 | bytes 24000000 | tf_op jit(solution)/shard_map/feed_forward/pallas_call | solution.py:791
  217.5 4.3 collective-permute-done.35
  226.3 3.1 add_convert_fusion.3
  229.3 3.0 reshape_reshape.9
  235.0 3.2 add_convert_fusion.1
  244.7 38.9 %cross_backward.1 = (bf16[3,512,384]{2,1,0:T(8,128)(2,1)S(1)}, bf16[3,2048,768]{2,1,0:T(8,128)(2,1)}) custom-call(s32[5,12]{1,0:T(8,128)S(1)} %stack.111.work_ref, bf16[3,384,512]{2,1,0:T(8,128)(2,1)S(1)} %copy-done.17, bf16[3,384,512]{2,1,0:T(8,128)(2,1)S(1)} %pad_maximum_fusion.6.do_ref, f32[3,8,512]{2,1,0:T(8,128)S(1)} %get-tuple-element.130.lse_ref, ...), custom_call_target="tpu_custom_call" | custom-call | flops 51749998592 | bytes 24000000 | tf_op jit(solution)/shard_map/cross_backward/pallas_call | solution.py:517
  285.8 8.3 %collective-permute-start.42 = (bf16[4,96,1024]{2,1,0:T(8,128)(2,1)S(1)}, bf16[4,96,1024]{2,1,0:T(8,128)(2,1)S(1)}, u32[]{:S(2)}, u32[]{:S(2)}) collective-permute-start(bf16[4,96,1024]{2,1,0:T(8,128)(2,1)S(1)} %dynamic-slice_bitcast_fusion), channel_id=1, source_target_pairs={{0,4},{4,0},{8,12},{12,8},{16,20},{20,16},{24,28},{28,24},{1,5},{5... | collective-permute-start | bytes 2359304 | tf_op jit(solution)/shard_map/ppermute | solution.py:146
  294.3 20.3 %memory_backward.1 = (bf16[3,1024,768]{2,1,0:T(8,128)(2,1)}, bf16[3,1024,768]{2,1,0:T(8,128)(2,1)}, bf16[768,768]{1,0:T(8,128)(2,1)S(1)}) custom-call(s32[3,4]{1,0:T(4,128)S(1)} %copy-done.6, bf16[3,1024,768]{2,1,0:T(8,128)(2,1)} %own_ref.3, bf16[3,1024,768]{2,1,0:T(8,128)(2,1)} %collective-permute-done.20.other_ref, ...), custom_call_target="tpu_custom_call" | custom-call | flops 20700000256 | bytes 30000000 | tf_op jit(solution)/shard_map/memory_backward/pallas_call | solution.py:575
  317.4 16.9 %collective-permute-start.48 = (bf16[96,1024]{1,0:T(8,128)(2,1)S(1)}, bf16[96,1024]{1,0:T(8,128)(2,1)S(1)}, u32[]{:S(2)}, u32[]{:S(2)}) collective-permute-start(bf16[96,1024]{1,0:T(8,128)(2,1)S(1)} %get-tuple-element.200), channel_id=1, source_target_pairs={{0,8},{4,12},{8,16},{12,20},{16,24},{20,28},{24,0},{28,4},{1,9},{5... | collective-permute-start | bytes 589832 | tf_op jit(solution)/shard_map/ppermute | solution.py:159
  336.6 6.7 %self_output_back.1 = (f32[3,128,768]{2,1,0:T(8,128)S(1)}, bf16[3,768,128]{2,1,0:T(8,128)(2,1)}, bf16[768,768]{1,0:T(8,128)(2,1)S(1)}, f32[1,768]{1,0:T(1,128)S(1)}) custom-call(bf16[3,128,384]{2,1,0:T(8,128)(2,1)S(1)} %get-tuple-element.209.mine_ref, bf16[3,128,384]{2,1,0:T(8,128)(2,1)S(1)} %collective-permute-done.43.other_ref, ...), custom_call_target="tpu_custom_call" | custom-call | flops 4600000000 | bytes 8000000 | tf_op jit(solution)/shard_map/self_output_back/pallas_call | solution.py:875
  346.5 5.0 %collective-permute-start.46 = (bf16[4,96,1152]{2,1,0:T(8,128)(2,1)}, bf16[4,96,1152]{2,1,0:T(8,128)(2,1)}, u32[]{:S(2)}, u32[]{:S(2)}) collective-permute-start(bf16[4,96,1152]{2,1,0:T(8,128)(2,1)} %fusion.13), channel_id=1, source_target_pairs={{0,4},{4,0},{8,12},{12,8},{16,20},{20,16},{24,28},{28,24},{1,5},{5... | collective-permute-start | bytes 2654216 | tf_op jit(solution)/shard_map/ppermute | solution.py:146
  361.9 7.7 %collective-permute-done.46 = bf16[4,96,1152]{2,1,0:T(8,128)(2,1)} collective-permute-done((bf16[4,96,1152]{2,1,0:T(8,128)(2,1)}, bf16[4,96,1152]{2,1,0:T(8,128)(2,1)}, u32[]{:S(2)}, u32[]{:S(2)}) %collective-permute-start.46) | collective-permute-done | bytes 884768 | tf_op jit(solution)/shard_map/ppermute | solution.py:146
  382.6 7.2 %add_convert_fusion = bf16[3,1024,768]{2,1,0:T(8,128)(2,1)} fusion(bf16[3,1024,768]{2,1,0:T(8,128)(2,1)} %collective-permute-done.47, bf16[3,1024,768]{2,1,0:T(8,128)(2,1)} %get-tuple-element.151), kind=kLoop, calls=%fused_computation | loop fusion | flops 9437184 | bytes 14155776 | tf_op jit(solution)/shard_map/convert_element_type | solution.py:74
  390.6 3.2 collective-permute-start.51
  395.8 17.3 %self_backward.1 = (f32[3,512,768]{2,1,0:T(8,128)}, f32[768,640]{1,0:T(8,128)S(1)}, f32[8,512]{1,0:T(8,128)S(1)}) custom-call(bf16[3,512,768]{2,1,0:T(8,128)(2,1)} %get-tuple-element.146.n1_ref, bf16[3,640,512]{2,1,0:T(8,128)(2,1)S(1)} %copy-done.19, bf16[3,192,512]{2,1,0:T(8,128)(2,1)S(1)} %copy-done.2, f32[3,8,512]{2,1,0:T(8,128)S(1)} %copy-done.25, ...), custom_call_target="tpu_custom_call" | custom-call | flops 18400000000 | bytes 12000000 | tf_op jit(solution)/shard_map/self_backward/pallas_call | solution.py:303
  421.1 5.1 %collective-permute-start.58 = (bf16[4,48,1664]{2,1,0:T(8,128)(2,1)S(1)}, bf16[4,48,1664]{2,1,0:T(8,128)(2,1)S(1)}, u32[]{:S(2)}, u32[]{:S(2)}) collective-permute-start(bf16[4,48,1664]{2,1,0:T(8,128)(2,1)S(1)} %dynamic-slice_bitcast_fusion.1), channel_id=1, source_target_pairs={{0,4},{4,0},{8,12},{12,8},{16,20},{20,16},{24,28},{28,24},{1,5},{5... | collective-permute-start | bytes 1916936 | tf_op jit(solution)/shard_map/ppermute | solution.py:146
  428.7 11.5 %collective-permute-done.58 = bf16[4,48,1664]{2,1,0:T(8,128)(2,1)S(1)} collective-permute-done((bf16[4,48,1664]{2,1,0:T(8,128)(2,1)S(1)}, bf16[4,48,1664]{2,1,0:T(8,128)(2,1)S(1)}, u32[]{:S(2)}, u32[]{:S(2)}) %collective-permute-start.58) | collective-permute-done | bytes 639008 | tf_op jit(solution)/shard_map/ppermute | solution.py:146
  442.0 3.2 collective-permute-start.60
  446.3 9.3 %collective-permute-done.60 = bf16[48,1664]{1,0:T(8,128)(2,1)S(1)} collective-permute-done((bf16[48,1664]{1,0:T(8,128)(2,1)S(1)}, bf16[48,1664]{1,0:T(8,128)(2,1)S(1)}, u32[]{:S(2)}, u32[]{:S(2)}) %collective-permute-start.60) | collective-permute-done | bytes 159776 | tf_op jit(solution)/shard_map/ppermute | solution.py:159
  468.7 12.1 %collective-permute-done.55 = bf16[3,1,1,128,768]{4,3,0,2,1:T(8,128)(2,1)S(1)} collective-permute-done((bf16[3,1,1,128,768]{4,3,0,2,1:T(8,128)(2,1)S(1)}, bf16[3,1,1,128,768]{4,3,0,2,1:T(8,128)(2,1)S(1)}, u32[]{:S(2)}, u32[]{:S(2)}) %collective-permute-start.55) | collective-permute-done | bytes 589856 | tf_op jit(solution)/shard_map/ppermute | solution.py:55
  (413 shorter events, 166.2 us)
Async XLA Ops:
  7.2 181.6 %all-gather.5.cloned.1.call-start = ((), (), s32[]{:S(2)}) async-start(), calls=%async_computation.2 | async-start | bytes 3244032 | tf_op jit(solution)/shard_map/all_gather | solution.py:964
  9.0 181.1 %all-gather.3.cloned.1.call-start = ((), (), s32[]{:S(2)}) async-start(), calls=%async_computation.1 | async-start | bytes 7704576 | tf_op jit(solution)/shard_map/all_gather | solution.py:961
  11.7 348.7 %reduce-scatter.2.cloned.1.call-start = ((), (), s32[]{:S(2)}) async-start(), calls=%async_computation.3 | async-start | bytes 2433024 | tf_op jit(solution)/shard_map/reduce_scatter | solution.py:1021
  18.6 15.1 %collective-permute-start.4 = (bf16[96,768]{1,0:T(8,128)(2,1)S(1)}, bf16[96,768]{1,0:T(8,128)(2,1)S(1)}, u32[]{:S(2)}, u32[]{:S(2)}) collective-permute-start(bf16[96,768]{1,0:T(8,128)(2,1)S(1)} %fusion.47.refs_0_), channel_id=1, source_target_pairs={{0,24},{4,28},{8,0},{12,4},{16,8},{20,12},{24,16},{28,20},{1,25},{... | collective-permute-start | bytes 442376 | tf_op jit(solution)/shard_map/ppermute | solution.py:114
  21.1 90.2 %collective-permute-start.20 = (bf16[3,1024,768]{2,1,0:T(8,128)(2,1)}, bf16[3,1024,768]{2,1,0:T(8,128)(2,1)}, u32[]{:S(2)}, u32[]{:S(2)}) collective-permute-start(bf16[3,1024,768]{2,1,0:T(8,128)(2,1)} %own_ref.3), channel_id=1, source_target_pairs={{0,1},{1,0},{2,3},{3,2},{4,5},{5,4},{6,7},{7,6},{8,9},{9,8},{10,11... | collective-permute-start | bytes 14155784 | tf_op jit(solution)/shard_map/ppermute | solution.py:51
  37.2 20.2 %collective-permute-start.1 = (bf16[3,2,128,768]{3,2,0,1:T(8,128)(2,1)}, bf16[3,2,128,768]{3,2,0,1:T(8,128)(2,1)}, u32[]{:S(2)}, u32[]{:S(2)}) collective-permute-start(bf16[3,2,128,768]{3,2,0,1:T(8,128)(2,1)} %pad_maximum_fusion.3), channel_id=1, source_target_pairs={{0,1},{1,0},{2,3},{3,2},{4,5},{5,4},{6,7},{7,6},{8,9},{9,8},{10,11... | collective-permute-start | bytes 3538952 | tf_op jit(solution)/shard_map/ppermute | solution.py:51
  44.4 27.5 %collective-permute-start.21 = (bf16[48,768]{1,0:T(8,128)(2,1)S(1)}, bf16[48,768]{1,0:T(8,128)(2,1)S(1)}, u32[]{:S(2)}, u32[]{:S(2)}) collective-permute-start(bf16[48,768]{1,0:T(8,128)(2,1)S(1)} %fusion.52.refs_0_), channel_id=1, source_target_pairs={{0,8},{4,12},{8,16},{12,20},{16,24},{20,28},{24,0},{28,4},{1,9},{5... | collective-permute-start | bytes 221192 | tf_op jit(solution)/shard_map/ppermute | solution.py:114
  49.7 22.3 %collective-permute-start.22 = (bf16[48,768]{1,0:T(8,128)(2,1)S(1)}, bf16[48,768]{1,0:T(8,128)(2,1)S(1)}, u32[]{:S(2)}, u32[]{:S(2)}) collective-permute-start(bf16[48,768]{1,0:T(8,128)(2,1)S(1)} %fusion.52.refs_0_), channel_id=1, source_target_pairs={{0,16},{4,20},{8,24},{12,28},{16,0},{20,4},{24,8},{28,12},{1,17},{... | collective-permute-start | bytes 221192 | tf_op jit(solution)/shard_map/ppermute | solution.py:114
  53.6 18.4 %collective-permute-start.23 = (bf16[48,768]{1,0:T(8,128)(2,1)S(1)}, bf16[48,768]{1,0:T(8,128)(2,1)S(1)}, u32[]{:S(2)}, u32[]{:S(2)}) collective-permute-start(bf16[48,768]{1,0:T(8,128)(2,1)S(1)} %fusion.52.refs_0_), channel_id=1, source_target_pairs={{0,24},{4,28},{8,0},{12,4},{16,8},{20,12},{24,16},{28,20},{1,25},{... | collective-permute-start | bytes 221192 | tf_op jit(solution)/shard_map/ppermute | solution.py:114
  90.6 18.3 %collective-permute-start.19 = (bf16[8,48,768]{2,1,0:T(8,128)(2,1)S(1)}, bf16[8,48,768]{2,1,0:T(8,128)(2,1)}, u32[]{:S(2)}, u32[]{:S(2)}) collective-permute-start(bf16[8,48,768]{2,1,0:T(8,128)(2,1)S(1)} %assemble.4), channel_id=1, source_target_pairs={{0,2},{2,0},{1,3},{3,1},{4,6},{6,4},{5,7},{7,5},{8,10},{10,8},{9,1... | collective-permute-start | bytes 1769480 | tf_op jit(solution)/shard_map/ppermute | solution.py:55
  92.7 37.0 %collective-permute-start.10 = (bf16[3,192,512]{2,1,0:T(8,128)(2,1)S(1)}, bf16[3,192,512]{2,1,0:T(8,128)(2,1)S(1)}, u32[]{:S(2)}, u32[]{:S(2)}) collective-permute-start(bf16[3,192,512]{2,1,0:T(8,128)(2,1)S(1)} %get-tuple-element.100.o0_ref), channel_id=1, source_target_pairs={{0,2},{2,0},{1,3},{3,1},{4,6},{6,4},{5,7},{7,5},{8,10},{10,8},{9,1... | collective-permute-start | bytes 1769480 | tf_op jit(solution)/shard_map/ppermute | solution.py:55
  172.3 15.7 %collective-permute-start.30 = (bf16[3,384,256]{2,1,0:T(8,128)(2,1)S(1)}, bf16[3,384,256]{2,1,0:T(8,128)(2,1)S(1)}, u32[]{:S(2)}, u32[]{:S(2)}) collective-permute-start(bf16[3,384,256]{2,1,0:T(8,128)(2,1)S(1)} %constant_dynamic-slice_fusion.17), channel_id=1, source_target_pairs={{0,2},{2,0},{1,3},{3,1},{4,6},{6,4},{5,7},{7,5},{8,10},{10,8},{9,1... | collective-permute-start | bytes 1769480 | tf_op jit(solution)/shard_map/ppermute | solution.py:55
  172.4 15.6 %collective-permute-start.31 = (f32[3,8,512]{2,1,0:T(8,128)S(1)}, f32[3,8,512]{2,1,0:T(8,128)S(1)}, u32[]{:S(2)}, u32[]{:S(2)}) collective-permute-start(f32[3,8,512]{2,1,0:T(8,128)S(1)} %get-tuple-element.116.lse_ref), channel_id=1, source_target_pairs={{0,2},{2,0},{1,3},{3,1},{4,6},{6,4},{5,7},{7,5},{8,10},{10,8},{9,1... | collective-permute-start | bytes 147464 | tf_op jit(solution)/shard_map/ppermute | solution.py:55
  216.1 17.8 %collective-permute-start.39 = (bf16[768,2048]{1,0:T(8,128)(2,1)}, bf16[768,2048]{1,0:T(8,128)(2,1)}, u32[]{:S(2)}, u32[]{:S(2)}) collective-permute-start(bf16[768,2048]{1,0:T(8,128)(2,1)} %get-tuple-element.128), channel_id=1, source_target_pairs={{0,1},{1,0},{2,3},{3,2},{4,5},{5,4},{6,7},{7,6},{8,9},{9,8},{10,11... | collective-permute-start | bytes 9437192 | tf_op jit(solution)/shard_map/ppermute | solution.py:51
  221.8 16.4 %collective-permute-start.36 = (f32[3,8,256]{2,1,0:T(8,128)S(1)}, f32[3,8,256]{2,1,0:T(8,128)S(1)}, u32[]{:S(2)}, u32[]{:S(2)}) collective-permute-start(f32[3,8,256]{2,1,0:T(8,128)S(1)} %pad_maximum_fusion.14), channel_id=1, source_target_pairs={{0,2},{2,0},{1,3},{3,1},{4,6},{6,4},{5,7},{7,5},{8,10},{10,8},{9,1... | collective-permute-start | bytes 73736 | tf_op jit(solution)/shard_map/ppermute | solution.py:55
  242.8 40.7 %collective-permute-start.40 = (bf16[768,1024]{1,0:T(8,128)(2,1)}, bf16[768,1024]{1,0:T(8,128)(2,1)}, u32[]{:S(2)}, u32[]{:S(2)}) collective-permute-start(bf16[768,1024]{1,0:T(8,128)(2,1)} %constant_dynamic-slice_fusion.14), channel_id=1, source_target_pairs={{0,2},{2,0},{1,3},{3,1},{4,6},{6,4},{5,7},{7,5},{8,10},{10,8},{9,1... | collective-permute-start | bytes 4718600 | tf_op jit(solution)/shard_map/ppermute | solution.py:55
  285.8 30.8 %collective-permute-start.42 = (bf16[4,96,1024]{2,1,0:T(8,128)(2,1)S(1)}, bf16[4,96,1024]{2,1,0:T(8,128)(2,1)S(1)}, u32[]{:S(2)}, u32[]{:S(2)}) collective-permute-start(bf16[4,96,1024]{2,1,0:T(8,128)(2,1)S(1)} %dynamic-slice_bitcast_fusion), channel_id=1, source_target_pairs={{0,4},{4,0},{8,12},{12,8},{16,20},{20,16},{24,28},{28,24},{1,5},{5... | collective-permute-start | bytes 2359304 | tf_op jit(solution)/shard_map/ppermute | solution.py:146
  294.2 22.8 %collective-permute-start.41 = (bf16[3,256,384]{2,1,0:T(8,128)(2,1)S(1)}, bf16[3,256,384]{2,1,0:T(8,128)(2,1)S(1)}, u32[]{:S(2)}, u32[]{:S(2)}) collective-permute-start(bf16[3,256,384]{2,1,0:T(8,128)(2,1)S(1)} %constant_dynamic-slice_fusion.13), channel_id=1, source_target_pairs={{0,2},{2,0},{1,3},{3,1},{4,6},{6,4},{5,7},{7,5},{8,10},{10,8},{9,1... | collective-permute-start | bytes 1769480 | tf_op jit(solution)/shard_map/ppermute | solution.py:55
  314.6 68.0 %collective-permute-start.47 = (bf16[3,1024,768]{2,1,0:T(8,128)(2,1)}, bf16[3,1024,768]{2,1,0:T(8,128)(2,1)}, u32[]{:S(2)}, u32[]{:S(2)}) collective-permute-start(bf16[3,1024,768]{2,1,0:T(8,128)(2,1)} %get-tuple-element.152), channel_id=1, source_target_pairs={{0,1},{1,0},{2,3},{3,2},{4,5},{5,4},{6,7},{7,6},{8,9},{9,8},{10,11... | collective-permute-start | bytes 14155784 | tf_op jit(solution)/shard_map/ppermute | solution.py:51
  317.2 19.4 %collective-permute-start.43 = (bf16[3,128,384]{2,1,0:T(8,128)(2,1)S(1)}, bf16[3,128,384]{2,1,0:T(8,128)(2,1)S(1)}, u32[]{:S(2)}, u32[]{:S(2)}) collective-permute-start(bf16[3,128,384]{2,1,0:T(8,128)(2,1)S(1)} %get-tuple-element.208), channel_id=1, source_target_pairs={{0,1},{1,0},{2,3},{3,2},{4,5},{5,4},{6,7},{7,6},{8,9},{9,8},{10,11... | collective-permute-start | bytes 884744 | tf_op jit(solution)/shard_map/ppermute | solution.py:51
  317.4 29.1 %collective-permute-start.48 = (bf16[96,1024]{1,0:T(8,128)(2,1)S(1)}, bf16[96,1024]{1,0:T(8,128)(2,1)S(1)}, u32[]{:S(2)}, u32[]{:S(2)}) collective-permute-start(bf16[96,1024]{1,0:T(8,128)(2,1)S(1)} %get-tuple-element.200), channel_id=1, source_target_pairs={{0,8},{4,12},{8,16},{12,20},{16,24},{20,28},{24,0},{28,4},{1,9},{5... | collective-permute-start | bytes 589832 | tf_op jit(solution)/shard_map/ppermute | solution.py:159
  334.3 17.2 %collective-permute-start.49 = (bf16[96,1024]{1,0:T(8,128)(2,1)S(1)}, bf16[96,1024]{1,0:T(8,128)(2,1)S(1)}, u32[]{:S(2)}, u32[]{:S(2)}) collective-permute-start(bf16[96,1024]{1,0:T(8,128)(2,1)S(1)} %get-tuple-element.202), channel_id=1, source_target_pairs={{0,16},{4,20},{8,24},{12,28},{16,0},{20,4},{24,8},{28,12},{1,17},{... | collective-permute-start | bytes 589832 | tf_op jit(solution)/shard_map/ppermute | solution.py:159
  334.3 19.8 %collective-permute-start.50 = (bf16[96,1024]{1,0:T(8,128)(2,1)S(1)}, bf16[96,1024]{1,0:T(8,128)(2,1)S(1)}, u32[]{:S(2)}, u32[]{:S(2)}) collective-permute-start(bf16[96,1024]{1,0:T(8,128)(2,1)S(1)} %get-tuple-element.201), channel_id=1, source_target_pairs={{0,24},{4,28},{8,0},{12,4},{16,8},{20,12},{24,16},{28,20},{1,25},{... | collective-permute-start | bytes 589832 | tf_op jit(solution)/shard_map/ppermute | solution.py:159
  346.5 23.0 %collective-permute-start.46 = (bf16[4,96,1152]{2,1,0:T(8,128)(2,1)}, bf16[4,96,1152]{2,1,0:T(8,128)(2,1)}, u32[]{:S(2)}, u32[]{:S(2)}) collective-permute-start(bf16[4,96,1152]{2,1,0:T(8,128)(2,1)} %fusion.13), channel_id=1, source_target_pairs={{0,4},{4,0},{8,12},{12,8},{16,20},{20,16},{24,28},{28,24},{1,5},{5... | collective-permute-start | bytes 2654216 | tf_op jit(solution)/shard_map/ppermute | solution.py:146
  360.4 17.3 %collective-permute-start.57 = (bf16[8,48,384]{2,1,0:T(8,128)(2,1)}, bf16[8,48,384]{2,1,0:T(8,128)(2,1)}, u32[]{:S(2)}, u32[]{:S(2)}) collective-permute-start(bf16[8,48,384]{2,1,0:T(8,128)(2,1)} %constant_dynamic-slice_fusion.6), channel_id=1, source_target_pairs={{0,2},{2,0},{1,3},{3,1},{4,6},{6,4},{5,7},{7,5},{8,10},{10,8},{9,1... | collective-permute-start | bytes 884744 | tf_op jit(solution)/shard_map/ppermute | solution.py:55
  390.6 25.0 %collective-permute-start.51 = (bf16[96,1152]{1,0:T(8,128)(2,1)}, bf16[96,1152]{1,0:T(8,128)(2,1)}, u32[]{:S(2)}, u32[]{:S(2)}) collective-permute-start(bf16[96,1152]{1,0:T(8,128)(2,1)} %get-tuple-element.191), channel_id=1, source_target_pairs={{0,8},{4,12},{8,16},{12,20},{16,24},{20,28},{24,0},{28,4},{1,9},{5... | collective-permute-start | bytes 663560 | tf_op jit(solution)/shard_map/ppermute | solution.py:159
  393.8 21.8 %collective-permute-start.52 = (bf16[96,1152]{1,0:T(8,128)(2,1)}, bf16[96,1152]{1,0:T(8,128)(2,1)}, u32[]{:S(2)}, u32[]{:S(2)}) collective-permute-start(bf16[96,1152]{1,0:T(8,128)(2,1)} %get-tuple-element.193), channel_id=1, source_target_pairs={{0,16},{4,20},{8,24},{12,28},{16,0},{20,4},{24,8},{28,12},{1,17},{... | collective-permute-start | bytes 663560 | tf_op jit(solution)/shard_map/ppermute | solution.py:159
  394.7 20.9 %collective-permute-start.53 = (bf16[96,1152]{1,0:T(8,128)(2,1)}, bf16[96,1152]{1,0:T(8,128)(2,1)}, u32[]{:S(2)}, u32[]{:S(2)}) collective-permute-start(bf16[96,1152]{1,0:T(8,128)(2,1)} %get-tuple-element.192), channel_id=1, source_target_pairs={{0,24},{4,28},{8,0},{12,4},{16,8},{20,12},{24,16},{28,20},{1,25},{... | collective-permute-start | bytes 663560 | tf_op jit(solution)/shard_map/ppermute | solution.py:159
  394.9 18.7 %collective-permute-start.68 = (bf16[96,1024]{1,0:T(8,128)(2,1)S(1)}, bf16[96,1024]{1,0:T(8,128)(2,1)}, u32[]{:S(2)}, u32[]{:S(2)}) collective-permute-start(bf16[96,1024]{1,0:T(8,128)(2,1)S(1)} %copy-done.43), channel_id=1, source_target_pairs={{0,2},{2,0},{1,3},{3,1},{4,6},{6,4},{5,7},{7,5},{8,10},{10,8},{9,1... | collective-permute-start | bytes 589832 | tf_op jit(solution)/shard_map/ppermute | solution.py:55
  418.9 46.5 %collective-permute-start.54 = (bf16[3,2,1,128,768]{4,3,0,2,1:T(8,128)(2,1)S(1)}, bf16[3,2,1,128,768]{4,3,0,2,1:T(8,128)(2,1)S(1)}, u32[]{:S(2)}, u32[]{:S(2)}) collective-permute-start(bf16[3,2,1,128,768]{4,3,0,2,1:T(8,128)(2,1)S(1)} %copy.119), channel_id=1, source_target_pairs={{0,1},{1,0},{2,3},{3,2},{4,5},{5,4},{6,7},{7,6},{8,9},{9,8},{10,11... | collective-permute-start | bytes 3538952 | tf_op jit(solution)/shard_map/ppermute | solution.py:51
  421.1 19.1 %collective-permute-start.58 = (bf16[4,48,1664]{2,1,0:T(8,128)(2,1)S(1)}, bf16[4,48,1664]{2,1,0:T(8,128)(2,1)S(1)}, u32[]{:S(2)}, u32[]{:S(2)}) collective-permute-start(bf16[4,48,1664]{2,1,0:T(8,128)(2,1)S(1)} %dynamic-slice_bitcast_fusion.1), channel_id=1, source_target_pairs={{0,4},{4,0},{8,12},{12,8},{16,20},{20,16},{24,28},{28,24},{1,5},{5... | collective-permute-start | bytes 1916936 | tf_op jit(solution)/shard_map/ppermute | solution.py:146
  465.8 15.0 %collective-permute-start.55 = (bf16[3,1,1,128,768]{4,3,0,2,1:T(8,128)(2,1)S(1)}, bf16[3,1,1,128,768]{4,3,0,2,1:T(8,128)(2,1)S(1)}, u32[]{:S(2)}, u32[]{:S(2)}) collective-permute-start(bf16[3,1,1,128,768]{4,3,0,2,1:T(8,128)(2,1)S(1)} %dynamic-slice_convert_fusion), channel_id=1, source_target_pairs={{0,2},{2,0},{1,3},{3,1},{4,6},{6,4},{5,7},{7,5},{8,10},{10,8},{9,1... | collective-permute-start | bytes 1769480 | tf_op jit(solution)/shard_map/ppermute | solution.py:55
  (98 other events, 1010.6 us)
Sparse Core Ops, SparseCore 0:
  11.5 67.1 all-gather.4
  82.2 76.4 all-gather.2
  243.5 84.7 reduce-scatter.1

commit v3 on v2

--- a/solution.py
+++ b/solution.py
@@ -138,30 +138,49 @@
     return lax.dynamic_index_in_dim(value, index, axis, keepdims=False)
 
 
-def wide_scatter_x(blocks):
+def x_swap(blocks):
     if not by_planes():
-        return blocks
+        return (blocks,)
     x = lax.axis_index("wide") % 2
     planes = blocks.reshape(LINE, 2, *blocks.shape[1:])
-    return plus(pick(planes, x, 1), lax.ppermute(pick(planes, 1 - x, 1), "wide", BESIDE))
-
-
-def wide_scatter_z(planes):
+    return pick(planes, x, 1), lax.ppermute(pick(planes, 1 - x, 1), "wide", BESIDE)
+
+
+def z_swap(planes):
     if not by_planes():
         shape = planes.shape
-        return lax.psum_scatter(
-            planes.reshape(shape[0] * shape[1], *shape[2:]), "wide", scatter_dimension=0, tiled=True
+        return (
+            lax.psum_scatter(
+                planes.reshape(shape[0] * shape[1], *shape[2:]), "wide", scatter_dimension=0, tiled=True
+            ),
         )
     z = lax.axis_index("wide") // 2
-    total = pick(planes, z, 0).astype(F32)
-    for step in range(1, LINE):
-        sent = pick(planes, (z + step) % LINE, 0)
-        total = total + lax.ppermute(sent, "wide", along(step)).astype(F32)
-    return total.astype(planes.dtype)
+    sent = [pick(planes, (z + step) % LINE, 0) for step in range(1, LINE)]
+    return pick(planes, z, 0), *(lax.ppermute(s, "wide", along(i + 1)) for i, s in enumerate(sent))
+
+
+def total(parts):
+    return sum((part.astype(F32) for part in parts[1:]), parts[0].astype(F32)).astype(parts[0].dtype)
+
+
+def wide_scatter_x(blocks):
+    return total(x_swap(blocks))
+
+
+def wide_scatter_z(planes):
+    return total(z_swap(planes))
 
 
 def wide_scatter(blocks):
     return wide_scatter_z(wide_scatter_x(blocks))
+
+
+def place_index(place_ref, flip):
+    return jnp.bitwise_xor(place_ref[0], flip)
+
+
+def strip(index, size):
+    return pl.ds(pl.multiple_of(index * size, size), size)
 
 
 def transpose_columns(weight_ref, out_ref):
@@ -184,7 +203,7 @@
 
 
 def self_forward_kernel(
-    x_ref, gain_ref, w_ref, vec_ref, n1_ref, qkv_ref, out_ref, lse_ref, wt_ref, bias_ref
+    x_ref, gain_ref, w_ref, vec_ref, qkv_ref, out_ref, lse_ref, wt_ref, bias_ref
 ):
     heads = bias_ref.shape[0]
     width = heads * HD
@@ -195,7 +214,6 @@
         position_bias(vec_ref, bias_ref)
 
     normed = root_norm(x_ref[0].astype(F32), gain_ref[...]).astype(BF16)
-    n1_ref[0] = normed
     qkv = dot(wt_ref[...], normed, (1, 1)).astype(BF16)
     qkv_ref[0] = qkv
     lse_ref[...] = jnp.zeros_like(lse_ref)
@@ -225,14 +243,12 @@
             whole(*vec.shape),
         ],
         out_specs=[
-            per(length, model),
             per(feats, length),
             per(heads * HD, length),
             per(8, length),
             whole(feats, model),
         ],
         out_shape=[
-            jax.ShapeDtypeStruct((examples, length, model), BF16),
             jax.ShapeDtypeStruct((examples, feats, length), BF16),
             jax.ShapeDtypeStruct((examples, heads * HD, length), BF16),
             jax.ShapeDtypeStruct((examples, 8, length), F32),
@@ -246,9 +262,9 @@
 
 
 def self_backward_kernel(
-    n1_ref, qkv_ref, do_ref, lse_ref, wt_ref, vec_ref,
-    dn_ref, gw_ref, dvec_ref,
-    bias_ref, dsum_ref, dqkv_ref,
+    place_ref, x_ref, gain_ref, qkv_ref, do0_ref, do1_ref, do2_ref, do3_ref, lse_ref, wt_ref, vec_ref,
+    dn_ref, gw_ref, dvec_ref, g_gain_ref,
+    bias_ref, dsum_ref, dqkv_ref, do_ref, sum_ref,
 ):
     heads, size, _ = bias_ref.shape
     width = heads * HD
@@ -258,14 +274,17 @@
     def _():
         position_bias(vec_ref, bias_ref)
         dsum_ref[...] = jnp.zeros_like(dsum_ref)
-        gw_ref[...] = jnp.zeros_like(gw_ref)
+        sum_ref[...] = jnp.zeros_like(sum_ref)
         dqkv_ref[...] = jnp.zeros_like(dqkv_ref)
-
+        g_gain_ref[...] = jnp.zeros_like(g_gain_ref)
+
+    for flip, piece_ref in enumerate((do0_ref, do1_ref, do2_ref, do3_ref)):
+        do_ref[:, strip(place_index(place_ref, flip), piece_ref.shape[2])] = piece_ref[0]
     for h in range(heads):
         q, k, v = (
             qkv_ref[0, width * part + HD * h : width * part + HD * (h + 1), :] for part in range(3)
         )
-        do = do_ref[0, HD * h : HD * (h + 1), :]
+        do = do_ref[HD * h : HD * (h + 1), :]
         s = dot(k, q, (0, 0)) + bias_ref[h]
         p = jnp.exp(s - lse_ref[0, h : h + 1, :])
         dp = dot(v, do, (0, 0))
@@ -278,11 +297,16 @@
         dqkv_ref[:, at(1)] = dot(ds, q, (1, 1)).astype(BF16)
         dqkv_ref[:, at(2)] = dot(p.astype(BF16), do, (1, 1)).astype(BF16)
     dqkv = dqkv_ref[...]
-    dn_ref[0] = dot(dqkv, wt_ref[...])
-    gw_ref[...] += dot(n1_ref[0], dqkv, (0, 0))
+    dn = dot(dqkv, wt_ref[...])
+    dn_ref[0] = dn.astype(BF16)
+    x = x_ref[0].astype(F32)
+    scaled = x * lax.rsqrt(jnp.mean(x * x, axis=-1, keepdims=True) + NORM_EPS)
+    g_gain_ref[...] += jnp.sum(dn * scaled, axis=0, keepdims=True)
+    sum_ref[...] += dot((scaled * gain_ref[...]).astype(BF16), dqkv, (0, 0))
 
     @pl.when(e == pl.num_programs(0) - 1)
     def _():
+        gw_ref[...] = sum_ref[...].astype(BF16)
         dvec_ref[...] = jnp.zeros_like(dvec_ref)
         for h in range(heads):
             back, count = dsum_ref[h], size
@@ -295,8 +319,8 @@
             dvec_ref[h : h + 1, :] = total
 
 
-def self_backward(n1, qkv, do, lse, wt, vec, heads):
-    examples, length, model = n1.shape
+def self_backward(place, x, gain, qkv, do, lse, wt, vec, heads):
+    examples, length, model = x.shape
     feats = wt.shape[0]
     whole = lambda *shape: pl.BlockSpec(shape, lambda e: (0,) * len(shape))
     per = lambda *shape: pl.BlockSpec((1, *shape), lambda e: (e, 0, 0))
@@ -304,28 +328,33 @@
         self_backward_kernel,
         grid=(examples,),
         in_specs=[
+            pl.BlockSpec(memory_space=pltpu.SMEM),
             per(length, model),
+            whole(1, model),
             per(feats, length),
-            per(heads * HD, length),
+            *[per(heads * HD, length // 4)] * 4,
             per(8, length),
             whole(*wt.shape),
             whole(*vec.shape),
         ],
-        out_specs=[per(length, model), whole(model, feats), whole(8, length)],
+        out_specs=[per(length, model), whole(model, feats), whole(8, length), whole(1, model)],
         out_shape=[
-            jax.ShapeDtypeStruct((examples, length, model), F32),
-            jax.ShapeDtypeStruct((model, feats), F32),
+            jax.ShapeDtypeStruct((examples, length, model), BF16),
+            jax.ShapeDtypeStruct((model, feats), BF16),
             jax.ShapeDtypeStruct((8, length), F32),
+            jax.ShapeDtypeStruct((1, model), F32),
         ],
         scratch_shapes=[
             pltpu.VMEM((heads, length, length), F32),
             pltpu.VMEM((heads, length, length), F32),
             pltpu.VMEM((length, feats), BF16),
+            pltpu.VMEM((heads * HD, length), BF16),
+            pltpu.VMEM((model, feats), F32),
         ],
         compiler_params=pltpu.CompilerParams(vmem_limit_bytes=48 << 20),
         cost_estimate=cost(16e-6 * PEAK_FLOPS, 12e6),
         name="self_backward",
-    )(n1, qkv, do, lse, wt, vec)
+    )(place, x, gain, qkv, *do, lse, wt, vec)
 
 
 def work_list(live):
@@ -469,7 +498,8 @@
 
 
 def cross_backward_kernel(
-    work_ref, q_ref, do_ref, lse_ref, inner_ref, k_ref, v_ref, dq_ref, dkv_ref, acc_ref
+    work_ref, place_ref, q_ref, do0_ref, do1_ref, do2_ref, do3_ref, lse_ref, in0_ref, in1_ref, in2_ref, in3_ref,
+    k_ref, v_ref, dq_ref, dkv_ref, acc_ref, do_ref, inner_ref,
 ):
     i = pl.program_id(0)
     feats = acc_ref.shape[0]
@@ -479,17 +509,23 @@
     @pl.when(work_ref[3, i] == 1)
     def _():
         acc_ref[...] = jnp.zeros_like(acc_ref)
+        for pieces, full_ref in (
+            ((do0_ref, do1_ref, do2_ref, do3_ref), do_ref),
+            ((in0_ref, in1_ref, in2_ref, in3_ref), inner_ref),
+        ):
+            for flip, piece_ref in enumerate(pieces):
+                full_ref[:, strip(place_index(place_ref, flip), piece_ref.shape[2])] = piece_ref[0]
 
     def block(partial):
         for h in range(heads):
             at = slice(HD * h, HD * (h + 1))
-            q, do, k, v = q_ref[0, at, :], do_ref[0, at, :], k_ref[0, at, :], v_ref[0, at, :]
+            q, do, k, v = q_ref[0, at, :], do_ref[at, :], k_ref[0, at, :], v_ref[0, at, :]
             s = dot(k, q, (0, 0))
             p = jnp.exp(s - lse_ref[0, h : h + 1, :])
             if partial:
                 p = jnp.where(lax.broadcasted_iota(jnp.int32, s.shape, 0) < live, p, 0.0)
             dp = dot(v, do, (0, 0))
-            ds = (p * (dp - inner_ref[0, h : h + 1, :])).astype(BF16)
+            ds = (p * (dp - inner_ref[h : h + 1, :])).astype(BF16)
             acc_ref[at, :] += dot(k, ds)
             dkv_ref[0, :, at] = dot(ds, q, (1, 1)).astype(BF16)
             dkv_ref[0, :, feats + HD * h : feats + HD * (h + 1)] = dot(p.astype(BF16), do, (1, 1)).astype(BF16)
@@ -507,24 +543,31 @@
         dq_ref[0] = acc_ref[...].T.astype(BF16)
 
 
-def cross_backward(work, q, do, lse, inner, k, v):
+def cross_backward(work, place, q, do, lse, inner, k, v):
     examples, feats, length = q.shape
     rows = k.shape[2]
-    q_spec = pl.BlockSpec((1, feats, length), lambda i, work: (work[0, i], 0, 0))
-    k_spec = pl.BlockSpec((1, feats, ROW_BLOCK), lambda i, work: (work[0, i], 0, work[1, i]))
-    l_spec = pl.BlockSpec((1, 8, length), lambda i, work: (work[0, i], 0, 0))
-    d_spec = pl.BlockSpec((1, ROW_BLOCK, 2 * feats), lambda i, work: (work[0, i], work[1, i], 0))
+    of_example = lambda *shape: pl.BlockSpec((1, *shape), lambda i, work, place: (work[0, i], 0, 0))
+    k_spec = pl.BlockSpec((1, feats, ROW_BLOCK), lambda i, work, place: (work[0, i], 0, work[1, i]))
+    d_spec = pl.BlockSpec((1, ROW_BLOCK, 2 * feats), lambda i, work, place: (work[0, i], work[1, i], 0))
     return pl.pallas_call(
         cross_backward_kernel,
         grid_spec=pltpu.PrefetchScalarGridSpec(
-            num_scalar_prefetch=1,
+            num_scalar_prefetch=2,
             grid=(work.shape[1],),
-            in_specs=[q_spec, q_spec, l_spec, l_spec, k_spec, k_spec],
-            out_specs=[
-                pl.BlockSpec((1, length, feats), lambda i, work: (work[0, i], 0, 0)),
-                d_spec,
+            in_specs=[
+                of_example(feats, length),
+                *[of_example(feats, length // 4)] * 4,
+                of_example(8, length),
+                *[of_example(8, length // 4)] * 4,
+                k_spec,
+                k_spec,
             ],
-            scratch_shapes=[pltpu.VMEM((feats, length), F32)],
+            out_specs=[of_example(length, feats), d_spec],
+            scratch_shapes=[
+                pltpu.VMEM((feats, length), F32),
+                pltpu.VMEM((feats, length), BF16),
+                pltpu.VMEM((8, length), F32),
+            ],
         ),
         out_shape=[
             jax.ShapeDtypeStruct((examples, length, feats), BF16),
@@ -533,7 +576,7 @@
         compiler_params=pltpu.CompilerParams(vmem_limit_bytes=48 << 20),
         cost_estimate=cost(45e-6 * PEAK_FLOPS, 24e6),
         name="cross_backward",
-    )(work, q, do, lse, inner, k, v)
+    )(work, place, q, *do, lse, *inner, k, v)
 
 
 def memory_backward_kernel(
@@ -590,14 +633,6 @@
         cost_estimate=cost(18e-6 * PEAK_FLOPS, 30e6),
         name="memory_backward",
     )(live, own, other, dkv, wt)
-
-
-def place_index(place_ref, flip):
-    return jnp.bitwise_xor(place_ref[0], flip)
-
-
-def strip(index, size):
-    return pl.ds(pl.multiple_of(index * size, size), size)
 
 
 def self_output_kernel(
@@ -841,11 +876,13 @@
 
 
 def self_output_back_kernel(
-    mine_ref, other_ref, wq_ref, x1_ref, gain_ref, dx2_ref, own_o_ref, wo_ref,
-    dx1_ref, do_ref, g_out_ref, g_gain_ref,
-    sum_ref,
+    place_ref, mine_ref, other_ref, wq_ref, x1_ref, gain_ref, dx2_ref, own_o_ref, wo_ref,
+    dx1_ref, do_mine_ref, do_pair_ref, do_across_ref, g_keep_ref, g_sent_ref, g_gain_ref,
+    sum_ref, do_ref,
 ):
     e = pl.program_id(0)
+    core, row = jnp.bitwise_and(place_ref[0], 1), lax.shift_right_logical(place_ref[0], 1)
+    width, feats = do_mine_ref.shape[1], do_across_ref.shape[1]
 
     @pl.when(e == 0)
     def _():
@@ -858,15 +895,19 @@
     dx1 = dx2_ref[0] + back
     dx1_ref[0] = dx1
     dx1r = dx1.astype(BF16)
-    do_ref[0] = dot(wo_ref[...], dx1r, (1, 1)).astype(BF16)
+    do_ref[...] = dot(wo_ref[...], dx1r, (1, 1)).astype(BF16)
+    do_mine_ref[0] = do_ref[strip(place_ref[0], width), :]
+    do_pair_ref[0] = do_ref[strip(place_index(place_ref, 1), width), :]
+    do_across_ref[0] = do_ref[strip(1 - row, feats), :]
     sum_ref[...] += dot(own_o_ref[0], dx1r)
 
     @pl.when(e == pl.num_programs(0) - 1)
     def _():
-        g_out_ref[...] = sum_ref[...].astype(BF16)
-
-
-def self_output_back(mine, other, wq, x1, gain, dx2, own_o, wo):
+        g_keep_ref[...] = sum_ref[:, strip(core, feats)].astype(BF16)
+        g_sent_ref[...] = sum_ref[:, strip(1 - core, feats)].astype(BF16)
+
+
+def self_output_back(place, mine, other, wq, x1, gain, dx2, own_o, wo):
     examples, own, model = x1.shape
     feats = mine.shape[2]
     whole = lambda *shape: pl.BlockSpec(shape, lambda e: (0,) * len(shape))
@@ -876,6 +917,7 @@
         self_output_back_kernel,
         grid=(examples,),
         in_specs=[
+            pl.BlockSpec(memory_space=pltpu.SMEM),
             per(own, feats),
             per(own, feats),
             whole(*wq.shape),
@@ -885,24 +927,31 @@
             per(model, own),
             whole(model, model),
         ],
-        out_specs=[per(own, model), per(model, own), whole(model, model), whole(1, model)],
+        out_specs=[
+            per(own, model),
+            *[per(model // 4, own)] * 2,
+            per(feats, own),
+            *[whole(model, feats)] * 2,
+            whole(1, model),
+        ],
         out_shape=[
             array((examples, own, model), F32),
-            array((examples, model, own), BF16),
-            array((model, model), BF16),
+            *[array((examples, model // 4, own), BF16)] * 2,
+            array((examples, feats, own), BF16),
+            *[array((model, feats), BF16)] * 2,
             array((1, model), F32),
         ],
-        scratch_shapes=[pltpu.VMEM((model, model), F32)],
+        scratch_shapes=[pltpu.VMEM((model, model), F32), pltpu.VMEM((model, own), BF16)],
         compiler_params=pltpu.CompilerParams(vmem_limit_bytes=48 << 20),
         cost_estimate=cost(4e-6 * PEAK_FLOPS, 8e6),
         name="self_output_back",
-    )(mine, other, wq, x1, gain, dx2, own_o, wo)
+    )(place, mine, other, wq, x1, gain, dx2, own_o, wo)
 
 
 def fold_rows(rows, target, columns):
     rest = rows * columns // target
     tile = 16
-    if rows % tile or target % tile or rows * target != columns * rest or rows // tile * LANES != rest:
+    if rows % tile or rows // tile * LANES != rest or columns // LANES * tile != target:
         return (lambda b: b.reshape(*b.shape[:-2], target, rest)), (lambda b: b.reshape(rows, columns))
 
     def swap(b, down, across):
@@ -973,7 +1022,7 @@
     hot = jnp.asarray(bucket_table(length))
     distance_bias = jnp.dot(table.T, hot, precision=FULL_ACCURACY)
     vec = jnp.pad(part_of(distance_bias, place, 4, 0), ((0, 8 - own_heads), (0, 0)))
-    n1, qkv, self_o, self_lse, self_wt = self_forward(x_all, gain_one, self_w, vec, own_heads)
+    qkv, self_o, self_lse, self_wt = self_forward(x_all, gain_one, self_w, vec, own_heads)
     across_o = across_swap(self_o)
     pieces = [self_o, pair_swap(self_o), across_o, pair_swap(across_o)]
     memory_w = shared_gather(jnp.concatenate([half(cross_key), half(cross_value)], 1), row, first=(self_o,))
@@ -1005,68 +1054,101 @@
     layer_out, dx2 = layer_out.reshape(x1.shape), dx2.reshape(x1.shape)
 
     rows_of = lambda g: g.reshape(wide, share, -1)
-    to_chip = lambda mine, other: jnp.concatenate(in_order(core, mine, pair_swap(other)), 2)
-    doc, inner = to_chip(doc_mine, doc_other), to_chip(inner_mine, inner_other)
-    doc_came, inner_came = across_swap(doc), across_swap(inner)
-    fold, unfold = fold_rows(down_rows, share, model)
-    gate_up = plus(gate_up, pair_swap(gate_up_sent))
-    early = jnp.concatenate(
-        [
-            rows_of(plus(grad_co, pair_swap(co_sent))),
-            fold(plus(down, pair_swap(down_sent)).reshape(wide, down_rows, model)),
-        ],
-        2,
-    )
-    doc_came, inner_came, early, gate_up = lax.optimization_barrier((doc_came, inner_came, early, gate_up))
-    early_sum = lax.psum_scatter(
-        early.reshape(wide * share, -1), "wide", scatter_dimension=0, tiled=True
-    )
-    to_all = lambda mine, came: jnp.concatenate(in_order(row, mine, came), 2)
-    part_dq, dkv = cross_backward(
-        work, cross_q, to_all(doc, doc_came), lse, to_all(inner, inner_came), keys, values
-    )
-
-    gate_up_came = across_swap(part_of(gate_up, 1 - row, 2, 1))
-    part_dq, dkv, gate_up_came = lax.optimization_barrier((part_dq, dkv, gate_up_came))
-    gate_up = wide_scatter_x(rows_of(plus(part_of(gate_up, row, 2, 1), gate_up_came)))
+
+    def from_all(mine, other):
+        pair = pair_swap(other)
+        return [mine, pair, across_swap(mine), across_swap(pair)]
+
+    doc, inner = from_all(doc_mine, doc_other), from_all(inner_mine, inner_other)
+    ffn = gate_up, pair_swap(gate_up_sent)
+    by_y = lambda y: [part_of(g, y, 2, 1).astype(F32) for g in ffn]
+    ffn_sent = sum(by_y(1 - row)).astype(BF16)
+    down = plus(down, pair_swap(down_sent)).reshape(wide, down_rows, model)
+    co = plus(grad_co, pair_swap(co_sent))
+    doc, inner, ffn_sent, down, co = lax.optimization_barrier((doc, inner, ffn_sent, down, co))
+    ffn_came, down = across_swap(ffn_sent), wide_scatter_x(down)
+    part_dq, dkv = cross_backward(work, me, cross_q, doc, lse, inner, keys, values)
+    part_dq, dkv, ffn_came, down = lax.optimization_barrier((part_dq, dkv, ffn_came, down))
+    ffn = wide_scatter_x(rows_of(sum(by_y(row), ffn_came.astype(F32)).astype(BF16)))
 
     dq_came = across_swap(part_of(part_dq, 1 - row, 2, 1))
     enc_mine, enc_swapped, grad_memory = memory_backward(live, enc_out, enc_other, dkv, memory_wt)
     enc_came = pair_swap(enc_swapped)
-    dq_came, grad_memory, gate_up = lax.optimization_barrier((dq_came, grad_memory, gate_up))
-    gate_up_sum = wide_scatter_z(gate_up)
+    dq_came, grad_memory, ffn = lax.optimization_barrier((dq_came, grad_memory, ffn))
+    down_came = across_swap(part_of(down, 1 - row, 2, 1))
+    ffn_sum = wide_scatter_z(ffn)
     chip_dq = plus(part_of(part_dq, row, 2, 1), dq_came)
     dq_mine, dq_other = part_of(chip_dq, core, 2, 1), pair_swap(part_of(chip_dq, 1 - core, 2, 1))
     grad_cross_query = jnp.einsum("etd,etf->df", n2, part_dq, preferred_element_type=F32).astype(BF16)
-    late = wide_scatter_x(jnp.concatenate([rows_of(grad_cross_query), rows_of(grad_memory)], 2))
-    dx1, do, grad_self_output, grad_gain_two = self_output_back(
-        dq_mine, dq_other, cross_query_wt, x1, gain_two, dx2, own_o, self_out_w
-    )
+    late = x_swap(jnp.concatenate([rows_of(g) for g in (grad_cross_query, grad_memory, co)], 2))
+    dx1, do_mine, do_pair, do_across, grad_so, so_sent, grad_gain_two = self_output_back(
+        me, dq_mine, dq_other, cross_query_wt, x1, gain_two, dx2, own_o, self_out_w
+    )
+    do_across, do_pair, down_came = lax.optimization_barrier((do_across, do_pair, down_came))
+
+    do_came = across_swap(do_across)
+    do = [do_mine, pair_swap(do_pair), part_of(do_came, core, 2, 1), pair_swap(part_of(do_came, 1 - core, 2, 1))]
+    so = rows_of(plus(grad_so, pair_swap(so_sent)))
+    down = plus(part_of(down, row, 2, 1), down_came)
+    do, ffn_sum, so, late, down = lax.optimization_barrier((do, ffn_sum, so, late, down))
+    fold, unfold = fold_rows(down.shape[1], share, model)
+    late = z_swap(jnp.concatenate([total(late), fold(down)], 2))
+    so_came = across_swap(part_of(so, 1 - row, 2, 1))
+    part_dn1, grad_self, dvec, grad_gain_one = self_backward(
+        me, x_all, gain_one, qkv, do, self_lse, self_wt, vec, own_heads
+    )
+    part_dn1, grad_self, so_came, late = lax.optimization_barrier((part_dn1, grad_self, so_came, late))
+
+    own_table = jnp.dot(hot, dvec[:own_heads].T, precision=FULL_ACCURACY)
+    grad_table = lax.dynamic_update_slice_in_dim(
+        jnp.zeros((BUCKETS, heads), F32), own_table, place * own_heads, 1
+    )
+    small = [g.reshape(wide, -1) for g in (grad_gain_one, grad_gain_two, grad_gain_three, grad_table)]
+    small = jnp.concatenate(small, 1).astype(BF16)
+    small_count = small.shape[1]
+    small = jnp.pad(small, ((0, 0), (0, share // 2 * LANES - small_count))).reshape(wide, -1, LANES)
+    so = plus(part_of(so, row, 2, 1), so_came)
+    self_width = grad_self.shape[1]
+    self_halves = grad_self.reshape(wide, 2, share // 2, self_width)
+    last = x_swap(jnp.concatenate([self_halves[:, 0], self_halves[:, 1], so, small], 2))
+    by_core = part_dn1.reshape(examples, 2, 2, own, model)
+    column = plus(part_of(by_core, core, 2, 2).astype(F32), pair_swap(part_of(by_core, 1 - core, 2, 2)))
+    dn1_sent = part_of(column, 1 - row, 2, 1).astype(BF16)
     enc_grad = plus(enc_mine, enc_came)
-
-    low, high = in_order(row, part_of(do, row, 2, 1), across_swap(part_of(do, 1 - row, 2, 1)))
-    column = jnp.stack([low, high], 2)
-    low, high = in_order(core, part_of(column, core, 2, 1), pair_swap(part_of(column, 1 - core, 2, 1)))
-    do_heads = jnp.stack([low, high], 3).reshape(examples, own_heads * HD, length)
-    do_heads, late, enc_grad, gate_up_sum = lax.optimization_barrier((do_heads, late, enc_grad, gate_up_sum))
-    part_dn1, grad_self, dvec = self_backward(n1, qkv, do_heads, self_lse, self_wt, vec, own_heads)
-    late_sum = wide_scatter_z(late)
-    part_dn1, grad_self, late_sum = lax.optimization_barrier((part_dn1, grad_self, late_sum))
-    by_core = part_dn1.reshape(examples, 2, 2, own, model)
-    column = part_of(by_core, core, 2, 2) + pair_swap(part_of(by_core, 1 - core, 2, 2).astype(BF16)).astype(F32)
-    dn1 = part_of(column, row, 2, 1) + across_swap(part_of(column, 1 - row, 2, 1).astype(BF16)).astype(F32)
-    grad_in, grad_gain_one = norm_back(
+    sums = jnp.concatenate([ffn_sum, total(late)], 1)
+    last, dn1_sent, enc_grad, sums = lax.optimization_barrier((last, dn1_sent, enc_grad, sums))
+    last, dn1_came, sums_came = z_swap(total(last)), across_swap(dn1_sent), across_swap(sums)
+    last, dn1_came, sums_came = lax.optimization_barrier((last, dn1_came, sums_came))
+    last_sum = total(last)
+    last_came = across_swap(last_sum)
+    dn1 = plus(part_of(column, row, 2, 1), dn1_came)
+    grad_in, _ = norm_back(
         dec_input.reshape(tokens, model).astype(F32), gain_one, dn1.reshape(tokens, model)
     )
     input_grad = (dx1 + grad_in.reshape(x1.shape)).astype(BF16)
 
-    so = rows_of(plus(part_of(grad_self_output, core, 2, 1), pair_swap(part_of(grad_self_output, 1 - core, 2, 1))))
-    so = plus(part_of(so, row, 2, 1), across_swap(part_of(so, 1 - row, 2, 1)))
-    self_width = grad_self.shape[1]
-    self_halves = grad_self.astype(BF16).reshape(wide, 2, share // 2, self_width)
-    last = wide_scatter(jnp.concatenate([self_halves[:, 0], self_halves[:, 1], so], 2))
-    low, high = in_order(row, last, across_swap(last))
-    last = jnp.stack([low, high])
+    bounds = np.cumsum([0, ffn_sum.shape[1], 4 * feats])
+    low, high = in_order(row, sums, sums_came)
+    sums = jnp.concatenate(
+        [
+            low[:, : bounds[1]],
+            high[:, : bounds[1]],
+            plus(sums[:, bounds[1] : bounds[2]], sums_came[:, bounds[1] : bounds[2]]),
+            low[:, bounds[2] :],
+            high[:, bounds[2] :],
+        ],
+        1,
+    )
+    parts = in_order(core, sums, pair_swap(sums))
+    gate_sum, up_sum = (part[:, : 2 * bounds[1]] for part in parts)
+    cq_sum, ck_sum, cv_sum, co_sum = (
+        jnp.concatenate([part[:, 2 * bounds[1] + feats * i : 2 * bounds[1] + feats * (i + 1)] for part in parts], 1)
+        for i in range(4)
+    )
+    down_sum = [jnp.split(part[:, 2 * bounds[1] + 4 * feats :], 2, 1) for part in parts]
+    down_sum = jnp.concatenate([unfold(half) for part in down_sum for half in part], 0)
+
+    last = jnp.stack(in_order(row, last_sum, last_came))
     low, high = in_order(core, last, pair_swap(last))
     halves = lambda part: jnp.concatenate([part[:, :self_width], part[:, self_width : 2 * self_width]], 0)
     self_sum = [halves(part[y]) for y in range(2) for part in (low, high)]
@@ -1075,32 +1157,10 @@
         for i in range(3)
     )
     so_sum = jnp.concatenate(
-        [part[:, :, 2 * self_width :].reshape(share, -1) for part in (low, high)], 1
-    )
-
-    early_sum = plus(early_sum, across_swap(early_sum))
-    low, high = in_order(core, early_sum, pair_swap(early_sum))
-    co_sum = jnp.concatenate([part[:, :feats] for part in (low, high)], 1)
-    down_sum = jnp.concatenate([unfold(part[:, feats:]) for part in (low, high)], 0)
-    gate_up_sum = jnp.concatenate(in_order(row, gate_up_sum, across_swap(gate_up_sum)), 1)
-    gate_sum, up_sum = in_order(core, gate_up_sum, pair_swap(gate_up_sum))
-    late_sum = plus(late_sum, across_swap(late_sum))
-    low, high = in_order(core, late_sum, pair_swap(late_sum))
-    cq_sum, ck_sum, cv_sum = (
-        jnp.concatenate([part[:, feats * i : feats * (i + 1)] for part in (low, high)], 1) for i in range(3)
-    )
-
-    own_table = jnp.dot(hot, dvec[:own_heads].T, precision=FULL_ACCURACY)
-    grad_table = lax.dynamic_update_slice_in_dim(
-        jnp.zeros((BUCKETS, heads), F32), own_table, place * own_heads, 1
-    )
-    small = jnp.concatenate(
-        [g.reshape(wide, share) for g in (grad_gain_one, grad_gain_two, grad_gain_three)]
-        + [grad_table.reshape(wide, bias_table.shape[0])], 1
-    )
-    small = small + pair_swap(small)
-    small = small + across_swap(small)
-    small_sum = wide_scatter(small.reshape(wide, 1, -1)).reshape(-1)
+        [part[:, :, 2 * self_width : 2 * self_width + feats].reshape(share, -1) for part in (low, high)], 1
+    )
+    small_sum = sum(part[y, :, 2 * self_width + feats :].astype(F32) for part in (low, high) for y in range(2))
+    small_sum = small_sum.reshape(-1)[:small_count]
     f = lambda a: a.astype(F32)
     return (
         layer_out,

time: 509 us -> 480 us (0.943)
  starting transfers between devices: 97.6 us -> 67.4 us
  Pallas kernels: 168 us -> 177 us
  local copies, waits for them, and re-layouts: 36.7 us -> 30.3 us
  waiting for transfers between devices: 121 us -> 127 us
    ppermute x16 -> x13, starting transfers between devices: 48.7 us -> 15.9 us  [the longest x9 15.6 us: z_swap(): lax.ppermute(s, 'wide', along(i + 1))]
    ppermute x16 -> x13, waiting for transfers between devices: 32.7 us -> 43 us  [the longest x9 37.1 us: z_swap(): lax.ppermute(s, 'wide', along(i + 1))]
    convert_element_type x13 -> x7, other arithmetic: 21.7 us -> 12.4 us  [plus(): return (mine.astype(F32) + came.astype(F32)).astype(mine.dtype)]
    convert_element_type x4 -> x9, other arithmetic: 2.38 us -> 11.3 us  [the longest x7 6.44 us: total(): sum((part.astype(F32) for part in parts[1:]), parts[0].astype(F32))]
    ppermute x18, waiting for transfers between devices: 48.8 us -> 42.8 us  [across_swap(): return lax.ppermute(value, 'narrow', ACROSS)]
    pallas_call x1, Pallas kernels: 38.9 us -> 44 us  [cross_backward(): pl.pallas_call(cross_backward_kernel, grid_spec=pltpu.PrefetchScalarGridS...]
    ppermute x21 -> x19, starting transfers between devices: 20.5 us -> 23.4 us  [pair_swap(): return lax.ppermute(value, 'narrow', PAIR)]
    unnamed x104 -> x100, local copies, waits for them, and re-layouts: 11.2 us -> 8.74 us
  transfers between devices with their start and end apart: 79 -> 73, of which waited for: 35 -> 32; matrix products, arithmetic and copies ran while one was open for 15% -> 14% of each run, Pallas kernels for 29% -> 32%
where the time goes in v3:
time: 480 us; the launch traced here: 474 us
  Pallas kernels  177 us (37%)
  waiting for transfers between devices  127 us (26%)
  starting transfers between devices  67.4 us (14%)
  other arithmetic  55.1 us (11%)
  local copies, waits for them, and re-layouts  30.3 us (6%)
  between operations  15.6 us (3%)
    pallas_call x1, Pallas kernels, cross_backward(): pl.pallas_call(cross_backward_kernel, grid_spec=pltpu.PrefetchScalarGridS...  44 us
    ppermute x18, waiting for transfers between devices, across_swap(): return lax.ppermute(value, 'narrow', ACROSS)  42.8 us
    ppermute x9, waiting for transfers between devices, z_swap(): lax.ppermute(s, 'wide', along(i + 1))  37.1 us
    pallas_call x1, Pallas kernels, cross_forward(): pl.pallas_call(cross_forward_kernel, grid_spec=pltpu.PrefetchScalarGridSp...  29.6 us
    ppermute x19, starting transfers between devices, pair_swap(): return lax.ppermute(value, 'narrow', PAIR)  23.4 us
    pallas_call x1, Pallas kernels, feed_forward(): pl.pallas_call(functools.partial(feed_forward_kernel, piece=piece), grid=...  23.2 us
    pallas_call x1, Pallas kernels, memory_backward(): pl.pallas_call(memory_backward_kernel, grid_spec=pltpu.PrefetchScalarGrid...  21.4 us
    ppermute x12, waiting for transfers between devices, wide_gather(): pieces = line + [lax.ppermute(piece, 'wide', BESIDE) for piece in line]  19.3 us
  transfers between devices with their start and end apart: 73, of which 32 were waited for; matrix products, arithmetic and copies ran while one was open for 14% of the time, Pallas kernels for 32%

profile of v3, /device:TPU:9, one launch (start us, length us, event | category | flops | bytes accessed | tf_op | source)
XLA Modules:
  0.0 474.2 jit_solution(3797862878661701907)
XLA Ops:
  26.2 4.8 %collective-permute-done.3.refs_2_ = bf16[96,768]{1,0:T(8,128)(2,1)S(1)} collective-permute-done((bf16[96,768]{1,0:T(8,128)(2,1)S(1)}, bf16[96,768]{1,0:T(8,128)(2,1)S(1)}, u32[]{:S(2)}, u32[]{:S(2)}) %collective-permute-start.3) | collective-permute-done | bytes 147488 | tf_op jit(solution)/shard_map/ppermute | solution.py:114
  31.0 2.6 collective-permute-done.4.refs_3_
  44.5 5.2 %collective-permute-done.7.refs_6_ = bf16[96,768]{1,0:T(8,128)(2,1)S(1)} collective-permute-done((bf16[96,768]{1,0:T(8,128)(2,1)S(1)}, bf16[96,768]{1,0:T(8,128)(2,1)S(1)}, u32[]{:S(2)}, u32[]{:S(2)}) %collective-permute-start.7) | collective-permute-done | bytes 147488 | tf_op jit(solution)/shard_map/ppermute | solution.py:116
  49.6 3.9 collective-permute-done.8.refs_7_
  59.9 9.5 %self_forward.1 = (bf16[3,640,512]{2,1,0:T(8,128)(2,1)S(1)}, bf16[3,192,512]{2,1,0:T(8,128)(2,1)S(1)}, f32[3,8,512]{2,1,0:T(8,128)S(1)}, bf16[640,768]{1,0:T(8,128)(2,1)S(1)}) custom-call(bf16[3,512,768]{2,1,0:T(8,128)(2,1)} %bitcast.200, f32[1,768]{1,0:T(1,128)S(1)} %get-tuple-element.326.gain_ref, bf16[768,640]{1,0:T(8,128)(2,1)S(1)} %bitcast.186, ...), custom_call_target="tpu_custom_call" | custom-call | flops 10350000128 | bytes 8000000 | tf_op jit(solution)/shard_map/self_forward/pallas_call | solution.py:236
  87.2 2.7 collective-permute-done.18.refs_7_
  94.9 11.4 %collective-permute-done.19 = bf16[8,48,768]{2,1,0:T(8,128)(2,1)} collective-permute-done((bf16[8,48,768]{2,1,0:T(8,128)(2,1)S(1)}, bf16[8,48,768]{2,1,0:T(8,128)(2,1)}, u32[]{:S(2)}, u32[]{:S(2)}) %collective-permute-start.19) | collective-permute-done | bytes 589856 | tf_op jit(solution)/shard_map/ppermute | solution.py:55
  108.7 14.0 %memory_project.1 = (bf16[3,384,2048]{2,1,0:T(8,128)(2,1)}, bf16[3,384,2048]{2,1,0:T(8,128)(2,1)}, bf16[768,768]{1,0:T(8,128)(2,1)S(1)}) custom-call(s32[5,12]{1,0:T(8,128)S(1)} %stack.93.work_ref, bf16[3,1024,768]{2,1,0:T(8,128)(2,1)} %own_ref.3, bf16[3,1024,768]{2,1,0:T(8,128)(2,1)} %collective-permute-done.20.other_ref, bf16[768,768]{1,0:T(8,128)(2,1)S(1)} %bitcast.182), custom_call_target="tpu_custom_call" | custom-call | flops 13799999488 | bytes 12000000 | tf_op jit(solution)/shard_map/memory_project/pallas_call | solution.py:413
  123.7 6.6 %collective-permute-start.29 = (bf16[768,768]{1,0:T(8,128)(2,1)}, bf16[768,768]{1,0:T(8,128)(2,1)}, u32[]{:S(2)}, u32[]{:S(2)}) collective-permute-start(bf16[768,768]{1,0:T(8,128)(2,1)} %bitcast.15.mine_ref), channel_id=1, source_target_pairs={{0,1},{1,0},{2,3},{3,2},{4,5},{5,4},{6,7},{7,6},{8,9},{9,8},{10,11... | collective-permute-start | bytes 3538952 | tf_op jit(solution)/shard_map/ppermute | solution.py:51
  130.8 3.5 collective-permute-done.9.o1_ref
  136.5 9.4 %self_output_stage.1 = (bf16[3,512,768]{2,1,0:T(8,128)(2,1)}, bf16[3,384,512]{2,1,0:T(8,128)(2,1)S(1)}, f32[3,128,768]{2,1,0:T(8,128)S(1)}, bf16[3,768,128]{2,1,...) custom-call(s32[1]{0:T(128)} %bitcast.place_ref, bf16[3,512,768]{2,1,0:T(8,128)(2,1)} %bitcast.201, ...), custom_call_target="tpu_custom_call" | custom-call | flops 6899999744 | bytes 10000000 | tf_op jit(solution)/shard_map/self_output_stage/pallas_call | solution.py:674
  146.7 29.6 %cross_forward.1 = (bf16[3,384,512]{2,1,0:T(8,128)(2,1)S(1)}, f32[3,8,512]{2,1,0:T(8,128)S(1)}) custom-call(s32[5,12]{1,0:T(8,128)S(1)} %stack.93.work_ref, bf16[3,384,512]{2,1,0:T(8,128)(2,1)S(1)} %get-tuple-element.147.q_ref, bf16[3,384,2048]{2,1,0:T(8,128)(2,1)} %get-tuple-element.144.k_ref, bf16[3,384,2048]{2,1,0:T(8,128)(2,1)} %get-tuple-element.148.v_ref), custom_call_target="tpu_custom_call" | custom-call | flops 34500001792 | bytes 16000000 | tf_op jit(solution)/shard_map/cross_forward/pallas_call | solution.py:477
  177.9 14.8 %collective-permute-done.31.other_lse_ref = f32[3,8,512]{2,1,0:T(8,128)S(1)} collective-permute-done((f32[3,8,512]{2,1,0:T(8,128)S(1)}, f32[3,8,512]{2,1,0:T(8,128)S(1)}, u32[]{:S(2)}, u32[]{:S(2)}) %collective-permute-start.31) | collective-permute-done | bytes 49184 | tf_op jit(solution)/shard_map/ppermute | solution.py:55
  196.2 23.2 %feed_forward.1 = (bf16[384,768]{1,0:T(8,128)(2,1)}, f32[384,768]{1,0:T(8,128)S(1)}, bf16[3,384,128]{2,1,0:T(8,128)(2,1)S(1)}, bf16[3,384,128]{2,1,0:T(8,128)(2,...) custom-call(s32[1]{0:T(128)} %bitcast.place_ref, ...), custom_call_target="tpu_custom_call" | custom-call | flops 23000000512 | bytes 24000000 | tf_op jit(solution)/shard_map/feed_forward/pallas_call | solution.py:826
  221.5 6.8 %collective-permute-done.41 = bf16[768,384]{1,0:T(8,128)(2,1)} collective-permute-done((bf16[768,384]{1,0:T(8,128)(2,1)S(1)}, bf16[768,384]{1,0:T(8,128)(2,1)}, u32[]{:S(2)}, u32[]{:S(2)}) %collective-permute-start.41) | collective-permute-done | bytes 589856 | tf_op jit(solution)/shard_map/ppermute | solution.py:51
  236.0 3.2 collective-permute-done.35.do3_ref
  240.0 44.0 %cross_backward.1 = (bf16[3,512,384]{2,1,0:T(8,128)(2,1)S(1)}, bf16[3,2048,768]{2,1,0:T(8,128)(2,1)}) custom-call(s32[5,12]{1,0:T(8,128)S(1)} %stack.93.work_ref, s32[1]{0:T(128)} %bitcast.place_ref, bf16[3,384,512]{2,1,0:T(8,128)(2,1)S(1)} %copy-done.18, bf16[3,384,128]{2,1,0:T(8,128)(2,1)S(1)} %get-tuple-element.163.do0_ref, ...), custom_call_target="tpu_custom_call" | custom-call | flops 51749998592 | bytes 24000000 | tf_op jit(solution)/shard_map/cross_backward/pallas_call | solution.py:552
  284.3 2.8 add_convert_fusion.1
  288.9 21.4 %memory_backward.1 = (bf16[3,1024,768]{2,1,0:T(8,128)(2,1)}, bf16[3,1024,768]{2,1,0:T(8,128)(2,1)}, bf16[768,768]{1,0:T(8,128)(2,1)S(1)}) custom-call(s32[3,4]{1,0:T(4,128)S(1)} %copy-done.5, bf16[3,1024,768]{2,1,0:T(8,128)(2,1)} %own_ref.3, bf16[3,1024,768]{2,1,0:T(8,128)(2,1)} %collective-permute-done.20.other_ref, ...), custom_call_target="tpu_custom_call" | custom-call | flops 20700000256 | bytes 30000000 | tf_op jit(solution)/shard_map/memory_backward/pallas_call | solution.py:618
  316.5 8.3 %collective-permute-start.51 = (bf16[96,1024]{1,0:T(8,128)(2,1)S(1)}, bf16[96,1024]{1,0:T(8,128)(2,1)S(1)}, u32[]{:S(2)}, u32[]{:S(2)}) collective-permute-start(bf16[96,1024]{1,0:T(8,128)(2,1)S(1)} %get-tuple-element.283), channel_id=1, source_target_pairs={{0,8},{4,12},{8,16},{12,20},{16,24},{20,28},{24,0},{28,4},{1,9},{5... | collective-permute-start | bytes 589832 | tf_op jit(solution)/shard_map/ppermute | solution.py:159
  326.6 6.1 %self_output_back.1 = (f32[3,128,768]{2,1,0:T(8,128)S(1)}, bf16[3,192,128]{2,1,0:T(8,128)(2,1)S(1)}, bf16[3,192,128]{2,1,0:T(8,128)(2,1)S(1)}, bf16[3,384,128]{2...) custom-call(s32[1]{0:T(128)} %bitcast.place_ref, ...), custom_call_target="tpu_custom_call" | custom-call | flops 4600000000 | bytes 8000000 | tf_op jit(solution)/shard_map/self_output_back/pallas_call | solution.py:916
  332.7 4.5 collective-permute-done.51
  347.0 5.5 %collective-permute-done.49 = bf16[3,384,128]{2,1,0:T(8,128)(2,1)} collective-permute-done((bf16[3,384,128]{2,1,0:T(8,128)(2,1)S(1)}, bf16[3,384,128]{2,1,0:T(8,128)(2,1)}, u32[]{:S(2)}, u32[]{:S(2)}) %collective-permute-start.49) | collective-permute-done | bytes 294944 | tf_op jit(solution)/shard_map/ppermute | solution.py:55
  364.8 17.2 %self_backward.1 = (bf16[3,512,768]{2,1,0:T(8,128)(2,1)}, bf16[768,640]{1,0:T(8,128)(2,1)S(1)}, f32[8,512]{1,0:T(8,128)S(1)}, f32[1,768]{1,0:T(1,128)S(1)}) custom-call(s32[1]{0:T(128)} %bitcast.place_ref, bf16[3,512,768]{2,1,0:T(8,128)(2,1)} %bitcast.202, f32[1,768]{1,0:T(1,128)S(1)} %copy-done.7, bf16[3,640,512]{2,1,0:T(8,128)(2,1)S(1)} %copy-done.20, ...), custom_call_target="tpu_custom_call" | custom-call | flops 18400000000 | bytes 12000000 | tf_op jit(solution)/shard_map/self_backward/pallas_call | solution.py:327
  382.8 11.6 %collective-permute-done.58 = bf16[96,2048]{1,0:T(8,128)(2,1)} collective-permute-done((bf16[96,2048]{1,0:T(8,128)(2,1)}, bf16[96,2048]{1,0:T(8,128)(2,1)}, u32[]{:S(2)}, u32[]{:S(2)}) %collective-permute-start.58) | collective-permute-done | bytes 393248 | tf_op jit(solution)/shard_map/ppermute | solution.py:159
  394.4 3.3 collective-permute-done.59
  405.9 5.8 %add_convert_fusion = bf16[3,1024,768]{2,1,0:T(8,128)(2,1)} fusion(bf16[3,1024,768]{2,1,0:T(8,128)(2,1)} %collective-permute-done.62, bf16[3,1024,768]{2,1,0:T(8,128)(2,1)S(1)} %bitcast.195), kind=kLoop, calls=%fused_computation | loop fusion | flops 9437184 | bytes 14155776 | tf_op jit(solution)/shard_map/convert_element_type | solution.py:74
  411.7 5.9 %collective-permute-done.61 = bf16[4,48,1792]{2,1,0:T(8,128)(2,1)S(1)} collective-permute-done((bf16[4,48,1792]{2,1,0:T(8,128)(2,1)S(1)}, bf16[4,48,1792]{2,1,0:T(8,128)(2,1)S(1)}, u32[]{:S(2)}, u32[]{:S(2)}) %collective-permute-start.61) | collective-permute-done | bytes 688160 | tf_op jit(solution)/shard_map/ppermute | solution.py:146
  421.9 3.2 collective-permute-done.63
  425.0 8.4 %collective-permute-done.64 = bf16[48,1792]{1,0:T(8,128)(2,1)} collective-permute-done((bf16[48,1792]{1,0:T(8,128)(2,1)}, bf16[48,1792]{1,0:T(8,128)(2,1)}, u32[]{:S(2)}, u32[]{:S(2)}) %collective-permute-start.64) | collective-permute-done | bytes 172064 | tf_op jit(solution)/shard_map/ppermute | solution.py:159
  433.5 2.9 collective-permute-done.65
  436.3 7.8 %collective-permute-done.67 = bf16[96,3072]{1,0:T(8,128)(2,1)} collective-permute-done((bf16[96,3072]{1,0:T(8,128)(2,1)}, bf16[96,3072]{1,0:T(8,128)(2,1)}, u32[]{:S(2)}, u32[]{:S(2)}) %collective-permute-start.67) | collective-permute-done | bytes 589856 | tf_op jit(solution)/shard_map/ppermute | solution.py:55
  (383 shorter events, 148.7 us)
Async XLA Ops:
  7.2 186.4 %all-gather.5.cloned.1.call-start = ((), (), s32[]{:S(2)}) async-start(), calls=%async_computation.1 | async-start | bytes 3244032 | tf_op jit(solution)/shard_map/all_gather | solution.py:1013
  9.0 185.9 %all-gather.3.cloned.1.call-start = ((), (), s32[]{:S(2)}) async-start(), calls=%async_computation | async-start | bytes 7704576 | tf_op jit(solution)/shard_map/all_gather | solution.py:1010
  18.5 15.1 %collective-permute-start.4 = (bf16[96,768]{1,0:T(8,128)(2,1)S(1)}, bf16[96,768]{1,0:T(8,128)(2,1)S(1)}, u32[]{:S(2)}, u32[]{:S(2)}) collective-permute-start(bf16[96,768]{1,0:T(8,128)(2,1)S(1)} %fusion.44.refs_0_), channel_id=1, source_target_pairs={{0,24},{4,28},{8,0},{12,4},{16,8},{20,12},{24,16},{28,20},{1,25},{... | collective-permute-start | bytes 442376 | tf_op jit(solution)/shard_map/ppermute | solution.py:114
  19.9 14.9 %collective-permute-start = (bf16[3,128,768]{2,1,0:T(8,128)(2,1)S(1)}, bf16[3,128,768]{2,1,0:T(8,128)(2,1)}, u32[]{:S(2)}, u32[]{:S(2)}) collective-permute-start(bf16[3,128,768]{2,1,0:T(8,128)(2,1)S(1)} %copy-done.25), channel_id=1, source_target_pairs={{0,2},{2,0},{1,3},{3,1},{4,6},{6,4},{5,7},{7,5},{8,10},{10,8},{9,1... | collective-permute-start | bytes 1769480 | tf_op jit(solution)/shard_map/ppermute | solution.py:55
  21.1 87.6 %collective-permute-start.20 = (bf16[3,1024,768]{2,1,0:T(8,128)(2,1)}, bf16[3,1024,768]{2,1,0:T(8,128)(2,1)}, u32[]{:S(2)}, u32[]{:S(2)}) collective-permute-start(bf16[3,1024,768]{2,1,0:T(8,128)(2,1)} %own_ref.3), channel_id=1, source_target_pairs={{0,1},{1,0},{2,3},{3,2},{4,5},{5,4},{6,7},{7,6},{8,9},{9,8},{10,11... | collective-permute-start | bytes 14155784 | tf_op jit(solution)/shard_map/ppermute | solution.py:51
  37.2 19.4 %collective-permute-start.1 = (bf16[3,2,128,768]{3,2,0,1:T(8,128)(2,1)}, bf16[3,2,128,768]{3,2,0,1:T(8,128)(2,1)}, u32[]{:S(2)}, u32[]{:S(2)}) collective-permute-start(bf16[3,2,128,768]{3,2,0,1:T(8,128)(2,1)} %pad_maximum_fusion.3), channel_id=1, source_target_pairs={{0,1},{1,0},{2,3},{3,2},{4,5},{5,4},{6,7},{7,6},{8,9},{9,8},{10,11... | collective-permute-start | bytes 3538952 | tf_op jit(solution)/shard_map/ppermute | solution.py:51
  44.4 26.0 %collective-permute-start.21 = (bf16[48,768]{1,0:T(8,128)(2,1)S(1)}, bf16[48,768]{1,0:T(8,128)(2,1)S(1)}, u32[]{:S(2)}, u32[]{:S(2)}) collective-permute-start(bf16[48,768]{1,0:T(8,128)(2,1)S(1)} %fusion.53.refs_0_), channel_id=1, source_target_pairs={{0,8},{4,12},{8,16},{12,20},{16,24},{20,28},{24,0},{28,4},{1,9},{5... | collective-permute-start | bytes 221192 | tf_op jit(solution)/shard_map/ppermute | solution.py:114
  49.6 20.8 %collective-permute-start.22 = (bf16[48,768]{1,0:T(8,128)(2,1)S(1)}, bf16[48,768]{1,0:T(8,128)(2,1)S(1)}, u32[]{:S(2)}, u32[]{:S(2)}) collective-permute-start(bf16[48,768]{1,0:T(8,128)(2,1)S(1)} %fusion.53.refs_0_), channel_id=1, source_target_pairs={{0,16},{4,20},{8,24},{12,28},{16,0},{20,4},{24,8},{28,12},{1,17},{... | collective-permute-start | bytes 221192 | tf_op jit(solution)/shard_map/ppermute | solution.py:114
  53.5 16.9 %collective-permute-start.23 = (bf16[48,768]{1,0:T(8,128)(2,1)S(1)}, bf16[48,768]{1,0:T(8,128)(2,1)S(1)}, u32[]{:S(2)}, u32[]{:S(2)}) collective-permute-start(bf16[48,768]{1,0:T(8,128)(2,1)S(1)} %fusion.53.refs_0_), channel_id=1, source_target_pairs={{0,24},{4,28},{8,0},{12,4},{16,8},{20,12},{24,16},{28,20},{1,25},{... | collective-permute-start | bytes 221192 | tf_op jit(solution)/shard_map/ppermute | solution.py:114
  90.5 15.8 %collective-permute-start.19 = (bf16[8,48,768]{2,1,0:T(8,128)(2,1)S(1)}, bf16[8,48,768]{2,1,0:T(8,128)(2,1)}, u32[]{:S(2)}, u32[]{:S(2)}) collective-permute-start(bf16[8,48,768]{2,1,0:T(8,128)(2,1)S(1)} %assemble.4), channel_id=1, source_target_pairs={{0,2},{2,0},{1,3},{3,1},{4,6},{6,4},{5,7},{7,5},{8,10},{10,8},{9,1... | collective-permute-start | bytes 1769480 | tf_op jit(solution)/shard_map/ppermute | solution.py:55
  93.5 36.9 %collective-permute-start.10 = (bf16[3,192,512]{2,1,0:T(8,128)(2,1)S(1)}, bf16[3,192,512]{2,1,0:T(8,128)(2,1)S(1)}, u32[]{:S(2)}, u32[]{:S(2)}) collective-permute-start(bf16[3,192,512]{2,1,0:T(8,128)(2,1)S(1)} %get-tuple-element.134.o0_ref), channel_id=1, source_target_pairs={{0,2},{2,0},{1,3},{3,1},{4,6},{6,4},{5,7},{7,5},{8,10},{10,8},{9,1... | collective-permute-start | bytes 1769480 | tf_op jit(solution)/shard_map/ppermute | solution.py:55
  176.4 16.3 %collective-permute-start.30 = (bf16[3,384,256]{2,1,0:T(8,128)(2,1)S(1)}, bf16[3,384,256]{2,1,0:T(8,128)(2,1)S(1)}, u32[]{:S(2)}, u32[]{:S(2)}) collective-permute-start(bf16[3,384,256]{2,1,0:T(8,128)(2,1)S(1)} %constant_dynamic-slice_fusion.11), channel_id=1, source_target_pairs={{0,2},{2,0},{1,3},{3,1},{4,6},{6,4},{5,7},{7,5},{8,10},{10,8},{9,1... | collective-permute-start | bytes 1769480 | tf_op jit(solution)/shard_map/ppermute | solution.py:55
  176.5 16.2 %collective-permute-start.31 = (f32[3,8,512]{2,1,0:T(8,128)S(1)}, f32[3,8,512]{2,1,0:T(8,128)S(1)}, u32[]{:S(2)}, u32[]{:S(2)}) collective-permute-start(f32[3,8,512]{2,1,0:T(8,128)S(1)} %get-tuple-element.150.lse_ref), channel_id=1, source_target_pairs={{0,2},{2,0},{1,3},{3,1},{4,6},{6,4},{5,7},{7,5},{8,10},{10,8},{9,1... | collective-permute-start | bytes 147464 | tf_op jit(solution)/shard_map/ppermute | solution.py:55
  221.4 14.6 %collective-permute-start.34 = (bf16[3,384,128]{2,1,0:T(8,128)(2,1)S(1)}, bf16[3,384,128]{2,1,0:T(8,128)(2,1)S(1)}, u32[]{:S(2)}, u32[]{:S(2)}) collective-permute-start(bf16[3,384,128]{2,1,0:T(8,128)(2,1)S(1)} %get-tuple-element.163.do0_ref), channel_id=1, source_target_pairs={{0,2},{2,0},{1,3},{3,1},{4,6},{6,4},{5,7},{7,5},{8,10},{10,8},{9,1... | collective-permute-start | bytes 884744 | tf_op jit(solution)/shard_map/ppermute | solution.py:55
  239.3 44.7 %collective-permute-start.43 = (bf16[4,128,768]{2,1,0:T(8,128)(2,1)S(1)}, bf16[4,128,768]{2,1,0:T(8,128)(2,1)S(1)}, u32[]{:S(2)}, u32[]{:S(2)}) collective-permute-start(bf16[4,128,768]{2,1,0:T(8,128)(2,1)S(1)} %dynamic-slice_bitcast_fusion.3), channel_id=1, source_target_pairs={{0,4},{4,0},{8,12},{12,8},{16,20},{20,16},{24,28},{28,24},{1,5},{5... | collective-permute-start | bytes 2359304 | tf_op jit(solution)/shard_map/ppermute | solution.py:146
  239.4 44.9 %collective-permute-start.42 = (bf16[768,1024]{1,0:T(8,128)(2,1)S(1)}, bf16[768,1024]{1,0:T(8,128)(2,1)S(1)}, u32[]{:S(2)}, u32[]{:S(2)}) collective-permute-start(bf16[768,1024]{1,0:T(8,128)(2,1)S(1)} %add_convert_fusion.3), channel_id=1, source_target_pairs={{0,2},{2,0},{1,3},{3,1},{4,6},{6,4},{5,7},{7,5},{8,10},{10,8},{9,1... | collective-permute-start | bytes 4718600 | tf_op jit(solution)/shard_map/ppermute | solution.py:55
  287.1 24.7 %collective-permute-start.45 = (bf16[4,96,1024]{2,1,0:T(8,128)(2,1)S(1)}, bf16[4,96,1024]{2,1,0:T(8,128)(2,1)S(1)}, u32[]{:S(2)}, u32[]{:S(2)}) collective-permute-start(bf16[4,96,1024]{2,1,0:T(8,128)(2,1)S(1)} %dynamic-slice_bitcast_fusion.2), channel_id=1, source_target_pairs={{0,4},{4,0},{8,12},{12,8},{16,20},{20,16},{24,28},{28,24},{1,5},{5... | collective-permute-start | bytes 2359304 | tf_op jit(solution)/shard_map/ppermute | solution.py:146
  287.3 24.8 %collective-permute-start.44 = (bf16[3,256,384]{2,1,0:T(8,128)(2,1)S(1)}, bf16[3,256,384]{2,1,0:T(8,128)(2,1)S(1)}, u32[]{:S(2)}, u32[]{:S(2)}) collective-permute-start(bf16[3,256,384]{2,1,0:T(8,128)(2,1)S(1)} %constant_dynamic-slice_fusion.8), channel_id=1, source_target_pairs={{0,2},{2,0},{1,3},{3,1},{4,6},{6,4},{5,7},{7,5},{8,10},{10,8},{9,1... | collective-permute-start | bytes 1769480 | tf_op jit(solution)/shard_map/ppermute | solution.py:55
  287.4 56.7 %collective-permute-start.47 = (bf16[4,64,768]{2,1,0:T(8,128)(2,1)S(1)}, bf16[4,64,768]{2,1,0:T(8,128)(2,1)S(1)}, u32[]{:S(2)}, u32[]{:S(2)}) collective-permute-start(bf16[4,64,768]{2,1,0:T(8,128)(2,1)S(1)} %constant_dynamic-slice_fusion.5), channel_id=1, source_target_pairs={{0,2},{2,0},{1,3},{3,1},{4,6},{6,4},{5,7},{7,5},{8,10},{10,8},{9,1... | collective-permute-start | bytes 1179656 | tf_op jit(solution)/shard_map/ppermute | solution.py:55
  316.5 39.6 %collective-permute-start.55 = (bf16[4,96,1536]{2,1,0:T(8,128)(2,1)}, bf16[4,96,1536]{2,1,0:T(8,128)(2,1)}, u32[]{:S(2)}, u32[]{:S(2)}) collective-permute-start(bf16[4,96,1536]{2,1,0:T(8,128)(2,1)} %get-tuple-element.249), channel_id=1, source_target_pairs={{0,4},{4,0},{8,12},{12,8},{16,20},{20,16},{24,28},{28,24},{1,5},{5... | collective-permute-start | bytes 3538952 | tf_op jit(solution)/shard_map/ppermute | solution.py:146
  316.5 20.7 %collective-permute-start.51 = (bf16[96,1024]{1,0:T(8,128)(2,1)S(1)}, bf16[96,1024]{1,0:T(8,128)(2,1)S(1)}, u32[]{:S(2)}, u32[]{:S(2)}) collective-permute-start(bf16[96,1024]{1,0:T(8,128)(2,1)S(1)} %get-tuple-element.283), channel_id=1, source_target_pairs={{0,8},{4,12},{8,16},{12,20},{16,24},{20,28},{24,0},{28,4},{1,9},{5... | collective-permute-start | bytes 589832 | tf_op jit(solution)/shard_map/ppermute | solution.py:159
  324.8 16.6 %collective-permute-start.52 = (bf16[96,1024]{1,0:T(8,128)(2,1)S(1)}, bf16[96,1024]{1,0:T(8,128)(2,1)S(1)}, u32[]{:S(2)}, u32[]{:S(2)}) collective-permute-start(bf16[96,1024]{1,0:T(8,128)(2,1)S(1)} %get-tuple-element.285), channel_id=1, source_target_pairs={{0,16},{4,20},{8,24},{12,28},{16,0},{20,4},{24,8},{28,12},{1,17},{... | collective-permute-start | bytes 589832 | tf_op jit(solution)/shard_map/ppermute | solution.py:159
  325.2 18.1 %collective-permute-start.53 = (bf16[96,1024]{1,0:T(8,128)(2,1)S(1)}, bf16[96,1024]{1,0:T(8,128)(2,1)S(1)}, u32[]{:S(2)}, u32[]{:S(2)}) collective-permute-start(bf16[96,1024]{1,0:T(8,128)(2,1)S(1)} %get-tuple-element.284), channel_id=1, source_target_pairs={{0,24},{4,28},{8,0},{12,4},{16,8},{20,12},{24,16},{28,20},{1,25},{... | collective-permute-start | bytes 589832 | tf_op jit(solution)/shard_map/ppermute | solution.py:159
  337.3 68.7 %collective-permute-start.62 = (bf16[3,1024,768]{2,1,0:T(8,128)(2,1)}, bf16[3,1024,768]{2,1,0:T(8,128)(2,1)}, u32[]{:S(2)}, u32[]{:S(2)}) collective-permute-start(bf16[3,1024,768]{2,1,0:T(8,128)(2,1)} %get-tuple-element.221), channel_id=1, source_target_pairs={{0,1},{1,0},{2,3},{3,2},{4,5},{5,4},{6,7},{7,6},{8,9},{9,8},{10,11... | collective-permute-start | bytes 14155784 | tf_op jit(solution)/shard_map/ppermute | solution.py:51
  360.2 22.7 %collective-permute-start.57 = (bf16[96,2048]{1,0:T(8,128)(2,1)}, bf16[96,2048]{1,0:T(8,128)(2,1)}, u32[]{:S(2)}, u32[]{:S(2)}) collective-permute-start(bf16[96,2048]{1,0:T(8,128)(2,1)} %get-tuple-element.257), channel_id=1, source_target_pairs={{0,8},{4,12},{8,16},{12,20},{16,24},{20,28},{24,0},{28,4},{1,9},{5... | collective-permute-start | bytes 1179656 | tf_op jit(solution)/shard_map/ppermute | solution.py:159
  360.2 34.2 %collective-permute-start.58 = (bf16[96,2048]{1,0:T(8,128)(2,1)}, bf16[96,2048]{1,0:T(8,128)(2,1)}, u32[]{:S(2)}, u32[]{:S(2)}) collective-permute-start(bf16[96,2048]{1,0:T(8,128)(2,1)} %get-tuple-element.258), channel_id=1, source_target_pairs={{0,16},{4,20},{8,24},{12,28},{16,0},{20,4},{24,8},{28,12},{1,17},{... | collective-permute-start | bytes 1179656 | tf_op jit(solution)/shard_map/ppermute | solution.py:159
  362.6 35.2 %collective-permute-start.59 = (bf16[96,2048]{1,0:T(8,128)(2,1)}, bf16[96,2048]{1,0:T(8,128)(2,1)}, u32[]{:S(2)}, u32[]{:S(2)}) collective-permute-start(bf16[96,2048]{1,0:T(8,128)(2,1)} %get-tuple-element.255), channel_id=1, source_target_pairs={{0,24},{4,28},{8,0},{12,4},{16,8},{20,12},{24,16},{28,20},{1,25},{... | collective-permute-start | bytes 1179656 | tf_op jit(solution)/shard_map/ppermute | solution.py:159
  364.8 18.1 %collective-permute-start.56 = (bf16[8,48,384]{2,1,0:T(8,128)(2,1)}, bf16[8,48,384]{2,1,0:T(8,128)(2,1)S(1)}, u32[]{:S(2)}, u32[]{:S(2)}) collective-permute-start(bf16[8,48,384]{2,1,0:T(8,128)(2,1)} %constant_dynamic-slice_fusion.2), channel_id=1, source_target_pairs={{0,2},{2,0},{1,3},{3,1},{4,6},{6,4},{5,7},{7,5},{8,10},{10,8},{9,1... | collective-permute-start | bytes 884744 | tf_op jit(solution)/shard_map/ppermute | solution.py:55
  401.1 16.6 %collective-permute-start.61 = (bf16[4,48,1792]{2,1,0:T(8,128)(2,1)S(1)}, bf16[4,48,1792]{2,1,0:T(8,128)(2,1)S(1)}, u32[]{:S(2)}, u32[]{:S(2)}) collective-permute-start(bf16[4,48,1792]{2,1,0:T(8,128)(2,1)S(1)} %get-tuple-element.259), channel_id=1, source_target_pairs={{0,4},{4,0},{8,12},{12,8},{16,20},{20,16},{24,28},{28,24},{1,5},{5... | collective-permute-start | bytes 2064392 | tf_op jit(solution)/shard_map/ppermute | solution.py:146
  417.7 18.7 %collective-permute-start.66 = (bf16[3,1,1,128,768]{4,3,0,2,1:T(8,128)(2,1)}, bf16[3,1,1,128,768]{4,3,0,2,1:T(8,128)(2,1)}, u32[]{:S(2)}, u32[]{:S(2)}) collective-permute-start(bf16[3,1,1,128,768]{4,3,0,2,1:T(8,128)(2,1)} %dynamic-slice_convert_fusion), channel_id=1, source_target_pairs={{0,2},{2,0},{1,3},{3,1},{4,6},{6,4},{5,7},{7,5},{8,10},{10,8},{9,1... | collective-permute-start | bytes 1769480 | tf_op jit(solution)/shard_map/ppermute | solution.py:55
  417.7 26.5 %collective-permute-start.67 = (bf16[96,3072]{1,0:T(8,128)(2,1)}, bf16[96,3072]{1,0:T(8,128)(2,1)}, u32[]{:S(2)}, u32[]{:S(2)}) collective-permute-start(bf16[96,3072]{1,0:T(8,128)(2,1)} %pad_maximum_fusion.6), channel_id=1, source_target_pairs={{0,2},{2,0},{1,3},{3,1},{4,6},{6,4},{5,7},{7,5},{8,10},{10,8},{9,1... | collective-permute-start | bytes 1769480 | tf_op jit(solution)/shard_map/ppermute | solution.py:55
  420.2 16.2 %collective-permute-start.65 = (bf16[48,1792]{1,0:T(8,128)(2,1)}, bf16[48,1792]{1,0:T(8,128)(2,1)}, u32[]{:S(2)}, u32[]{:S(2)}) collective-permute-start(bf16[48,1792]{1,0:T(8,128)(2,1)} %get-tuple-element.288), channel_id=1, source_target_pairs={{0,24},{4,28},{8,0},{12,4},{16,8},{20,12},{24,16},{28,20},{1,25},{... | collective-permute-start | bytes 516104 | tf_op jit(solution)/shard_map/ppermute | solution.py:159
  (86 other events, 736.3 us)
Sparse Core Ops, SparseCore 0:
  11.5 67.1 all-gather.4
  82.2 75.9 all-gather.2

commit v4 on v3

--- a/solution.py
+++ b/solution.py
@@ -217,14 +217,17 @@
     qkv = dot(wt_ref[...], normed, (1, 1)).astype(BF16)
     qkv_ref[0] = qkv
     lse_ref[...] = jnp.zeros_like(lse_ref)
+    piece = lambda part, h: qkv[width * part + HD * h : width * part + HD * (h + 1)]
+    following = dot(piece(1, 0), piece(0, 0), (0, 0))
     for h in range(heads):
-        q, k, v = (qkv[width * part + HD * h : width * part + HD * (h + 1)] for part in range(3))
-        s = dot(k, q, (0, 0)) + bias_ref[h]
+        s = following + bias_ref[h]
+        if h + 1 < heads:
+            following = dot(piece(1, h + 1), piece(0, h + 1), (0, 0))
         peak = jnp.max(s, axis=0, keepdims=True)
         raised = jnp.exp(s - peak)
         total = jnp.sum(raised, axis=0, keepdims=True)
         weight = (raised * (1.0 / total)).astype(BF16)
-        out_ref[0, HD * h : HD * (h + 1), :] = dot(v, weight).astype(BF16)
+        out_ref[0, HD * h : HD * (h + 1), :] = dot(piece(2, h), weight).astype(BF16)
         lse_ref[0, h : h + 1, :] = peak + jnp.log(total)
 
 
@@ -280,22 +283,23 @@
 
     for flip, piece_ref in enumerate((do0_ref, do1_ref, do2_ref, do3_ref)):
         do_ref[:, strip(place_index(place_ref, flip), piece_ref.shape[2])] = piece_ref[0]
+    piece = lambda part, h: qkv_ref[0, width * part + HD * h : width * part + HD * (h + 1), :]
+    out = lambda h: do_ref[HD * h : HD * (h + 1), :]
+    products = lambda h: (dot(piece(1, h), piece(0, h), (0, 0)), dot(piece(2, h), out(h), (0, 0)))
+    following = products(0)
     for h in range(heads):
-        q, k, v = (
-            qkv_ref[0, width * part + HD * h : width * part + HD * (h + 1), :] for part in range(3)
-        )
-        do = do_ref[HD * h : HD * (h + 1), :]
-        s = dot(k, q, (0, 0)) + bias_ref[h]
-        p = jnp.exp(s - lse_ref[0, h : h + 1, :])
-        dp = dot(v, do, (0, 0))
+        s, dp = following
+        if h + 1 < heads:
+            following = products(h + 1)
+        p = jnp.exp(s + bias_ref[h] - lse_ref[0, h : h + 1, :])
         inner = jnp.sum(p * dp, axis=0, keepdims=True)
         ds = p * (dp - inner)
         dsum_ref[h] += ds
         ds = ds.astype(BF16)
         at = lambda part: slice(width * part + HD * h, width * part + HD * (h + 1))
-        dqkv_ref[:, at(0)] = dot(k, ds).T.astype(BF16)
-        dqkv_ref[:, at(1)] = dot(ds, q, (1, 1)).astype(BF16)
-        dqkv_ref[:, at(2)] = dot(p.astype(BF16), do, (1, 1)).astype(BF16)
+        dqkv_ref[:, at(0)] = dot(piece(1, h), ds).T.astype(BF16)
+        dqkv_ref[:, at(1)] = dot(ds, piece(0, h), (1, 1)).astype(BF16)
+        dqkv_ref[:, at(2)] = dot(p.astype(BF16), out(h), (1, 1)).astype(BF16)
     dqkv = dqkv_ref[...]
     dn = dot(dqkv, wt_ref[...])
     dn_ref[0] = dn.astype(BF16)
@@ -436,10 +440,17 @@
         total_ref[...] = jnp.zeros_like(total_ref)
         acc_ref[...] = jnp.zeros_like(acc_ref)
 
+    def scores(h):
+        at = slice(HD * h, HD * (h + 1))
+        return dot(k_ref[0, at, :], q_ref[0, at, :], (0, 0))
+
     def block(partial):
+        following = scores(0)
         for h in range(heads):
             at = slice(HD * h, HD * (h + 1))
-            s = dot(k_ref[0, at, :], q_ref[0, at, :], (0, 0))
+            s = following
+            if h + 1 < heads:
+                following = scores(h + 1)
             if partial:
                 s = jnp.where(lax.broadcasted_iota(jnp.int32, s.shape, 0) < live, s, MASKED)
             before = peak_ref[h : h + 1, :]
@@ -516,19 +527,24 @@
             for flip, piece_ref in enumerate(pieces):
                 full_ref[:, strip(place_index(place_ref, flip), piece_ref.shape[2])] = piece_ref[0]
 
+    def products(h):
+        at = slice(HD * h, HD * (h + 1))
+        return dot(k_ref[0, at, :], q_ref[0, at, :], (0, 0)), dot(v_ref[0, at, :], do_ref[at, :], (0, 0))
+
     def block(partial):
+        following = products(0)
         for h in range(heads):
             at = slice(HD * h, HD * (h + 1))
-            q, do, k, v = q_ref[0, at, :], do_ref[at, :], k_ref[0, at, :], v_ref[0, at, :]
-            s = dot(k, q, (0, 0))
+            s, dp = following
+            if h + 1 < heads:
+                following = products(h + 1)
             p = jnp.exp(s - lse_ref[0, h : h + 1, :])
             if partial:
                 p = jnp.where(lax.broadcasted_iota(jnp.int32, s.shape, 0) < live, p, 0.0)
-            dp = dot(v, do, (0, 0))
             ds = (p * (dp - inner_ref[h : h + 1, :])).astype(BF16)
-            acc_ref[at, :] += dot(k, ds)
-            dkv_ref[0, :, at] = dot(ds, q, (1, 1)).astype(BF16)
-            dkv_ref[0, :, feats + HD * h : feats + HD * (h + 1)] = dot(p.astype(BF16), do, (1, 1)).astype(BF16)
+            acc_ref[at, :] += dot(k_ref[0, at, :], ds)
+            dkv_ref[0, :, at] = dot(ds, q_ref[0, at, :], (1, 1)).astype(BF16)
+            dkv_ref[0, :, feats + HD * h : feats + HD * (h + 1)] = dot(p.astype(BF16), do_ref[at, :], (1, 1)).astype(BF16)
 
     @pl.when(live == ROW_BLOCK)
     def _():
@@ -1029,7 +1045,7 @@
     work = work_list(live)
     keys, values, memory_wt = memory_project(work, enc_out, enc_other, memory_w)
     query_out = after(jnp.concatenate([half(cross_query), half(self_output)], 1), self_o)
-    mine_w = shared_gather(query_out, row)
+    (mine_w,) = wide_gather(query_out, (query_out.shape[1],))
     mine_w = after(mine_w, keys)
     other_w = pair_swap(mine_w)
     me = place.reshape(1).astype(jnp.int32)
@@ -1076,7 +1092,6 @@
     enc_came = pair_swap(enc_swapped)
     dq_came, grad_memory, ffn = lax.optimization_barrier((dq_came, grad_memory, ffn))
     down_came = across_swap(part_of(down, 1 - row, 2, 1))
-    ffn_sum = wide_scatter_z(ffn)
     chip_dq = plus(part_of(part_dq, row, 2, 1), dq_came)
     dq_mine, dq_other = part_of(chip_dq, core, 2, 1), pair_swap(part_of(chip_dq, 1 - core, 2, 1))
     grad_cross_query = jnp.einsum("etd,etf->df", n2, part_dq, preferred_element_type=F32).astype(BF16)
@@ -1084,20 +1099,22 @@
     dx1, do_mine, do_pair, do_across, grad_so, so_sent, grad_gain_two = self_output_back(
         me, dq_mine, dq_other, cross_query_wt, x1, gain_two, dx2, own_o, self_out_w
     )
-    do_across, do_pair, down_came = lax.optimization_barrier((do_across, do_pair, down_came))
+
+    ffn = z_swap(after(ffn, do_across))
 
     do_came = across_swap(do_across)
     do = [do_mine, pair_swap(do_pair), part_of(do_came, core, 2, 1), pair_swap(part_of(do_came, 1 - core, 2, 1))]
     so = rows_of(plus(grad_so, pair_swap(so_sent)))
     down = plus(part_of(down, row, 2, 1), down_came)
-    do, ffn_sum, so, late, down = lax.optimization_barrier((do, ffn_sum, so, late, down))
+    do, so, late, down = lax.optimization_barrier((do, so, late, down))
     fold, unfold = fold_rows(down.shape[1], share, model)
     late = z_swap(jnp.concatenate([total(late), fold(down)], 2))
     so_came = across_swap(part_of(so, 1 - row, 2, 1))
     part_dn1, grad_self, dvec, grad_gain_one = self_backward(
         me, x_all, gain_one, qkv, do, self_lse, self_wt, vec, own_heads
     )
-    part_dn1, grad_self, so_came, late = lax.optimization_barrier((part_dn1, grad_self, so_came, late))
+    part_dn1, grad_self, so_came, ffn, *early = lax.optimization_barrier((part_dn1, grad_self, so_came, ffn, *late[:-1]))
+    late, ffn_sum = (*early, *late[-1:]), total(ffn)
 
     own_table = jnp.dot(hot, dvec[:own_heads].T, precision=FULL_ACCURACY)
     grad_table = lax.dynamic_update_slice_in_dim(
@@ -1116,8 +1133,9 @@
     dn1_sent = part_of(column, 1 - row, 2, 1).astype(BF16)
     enc_grad = plus(enc_mine, enc_came)
     sums = jnp.concatenate([ffn_sum, total(late)], 1)
+    dn1_came, sums_came = across_swap(dn1_sent), across_swap(sums)
     last, dn1_sent, enc_grad, sums = lax.optimization_barrier((last, dn1_sent, enc_grad, sums))
-    last, dn1_came, sums_came = z_swap(total(last)), across_swap(dn1_sent), across_swap(sums)
+    last = z_swap(total(last))
     last, dn1_came, sums_came = lax.optimization_barrier((last, dn1_came, sums_came))
     last_sum = total(last)
     last_came = across_swap(last_sum)

time: 480 us -> 450 us (0.938)
  starting transfers between devices: 67.4 us -> 56 us
  waiting for transfers between devices: 127 us -> 116 us
  Pallas kernels: 177 us -> 168 us
    ppermute x9, waiting for transfers between devices: 37.1 us -> 17.2 us  [z_swap(): lax.ppermute(s, 'wide', along(i + 1))]
    ppermute x19, starting transfers between devices: 23.4 us -> 13.3 us  [pair_swap(): return lax.ppermute(value, 'narrow', PAIR)]
    ppermute x9, starting transfers between devices: 15.6 us -> 6.24 us  [z_swap(): lax.ppermute(s, 'wide', along(i + 1))]
    ppermute x4, starting transfers between devices: 0.25 us -> 8.81 us  [x_swap(): lax.ppermute(pick(planes, 1 - x, 1), 'wide', BESIDE)]
    ppermute x9, waiting for transfers between devices: 8.58 us -> 16 us  [wide_gather(): lax.ppermute(block, 'wide', along(step))]
    ppermute x18 -> x17, waiting for transfers between devices: 42.8 us -> 36.4 us  [across_swap(): return lax.ppermute(value, 'narrow', ACROSS)]
    ppermute x12, waiting for transfers between devices: 19.3 us -> 25.5 us  [wide_gather(): pieces = line + [lax.ppermute(piece, 'wide', BESIDE) for piece in line]]
    pallas_call x1, Pallas kernels: 29.6 us -> 24.7 us  [cross_forward(): pl.pallas_call(cross_forward_kernel, grid_spec=pltpu.PrefetchScalarGridSp...]
  transfers between devices with their start and end apart: 73 -> 72, of which waited for: 32 -> 29; matrix products, arithmetic and copies ran while one was open for 14% -> 16% of each run, Pallas kernels for 32% -> 33%
where the time goes in v4:
time: 450 us; the launch traced here: 443 us
  Pallas kernels  168 us (37%)
  waiting for transfers between devices  116 us (26%)
  starting transfers between devices  56 us (12%)
  other arithmetic  53.5 us (12%)
  local copies, waits for them, and re-layouts  31.4 us (7%)
  between operations  15.5 us (3%)
    pallas_call x1, Pallas kernels, cross_backward(): pl.pallas_call(cross_backward_kernel, grid_spec=pltpu.PrefetchScalarGridS...  41.3 us
    ppermute x17, waiting for transfers between devices, across_swap(): return lax.ppermute(value, 'narrow', ACROSS)  36.4 us
    ppermute x12, waiting for transfers between devices, wide_gather(): pieces = line + [lax.ppermute(piece, 'wide', BESIDE) for piece in line]  25.5 us
    pallas_call x1, Pallas kernels, cross_forward(): pl.pallas_call(cross_forward_kernel, grid_spec=pltpu.PrefetchScalarGridSp...  24.7 us
    pallas_call x1, Pallas kernels, feed_forward(): pl.pallas_call(functools.partial(feed_forward_kernel, piece=piece), grid=...  22.8 us
    pallas_call x1, Pallas kernels, memory_backward(): pl.pallas_call(memory_backward_kernel, grid_spec=pltpu.PrefetchScalarGrid...  21.4 us
    pallas_call x1, Pallas kernels, self_backward(): pl.pallas_call(self_backward_kernel, grid=(examples,), in_specs=[pl.Block...  17.4 us
    ppermute x9, waiting for transfers between devices, z_swap(): lax.ppermute(s, 'wide', along(i + 1))  17.2 us
  transfers between devices with their start and end apart: 72, of which 29 were waited for; matrix products, arithmetic and copies ran while one was open for 16% of the time, Pallas kernels for 33%

profile of v4, /device:TPU:9, one launch (start us, length us, event | category | flops | bytes accessed | tf_op | source)
XLA Modules:
  0.0 442.9 jit_solution(4911885583937803735)
XLA Ops:
  26.4 4.6 %collective-permute-done.3.refs_2_ = bf16[96,768]{1,0:T(8,128)(2,1)S(1)} collective-permute-done((bf16[96,768]{1,0:T(8,128)(2,1)S(1)}, bf16[96,768]{1,0:T(8,128)(2,1)S(1)}, u32[]{:S(2)}, u32[]{:S(2)}) %collective-permute-start.3) | collective-permute-done | bytes 147488 | tf_op jit(solution)/shard_map/ppermute | solution.py:114
  31.0 2.6 collective-permute-done.4.refs_3_
  40.4 2.6 collective-permute-done.6.refs_5_
  43.1 3.8 collective-permute-done.7.refs_6_
  47.1 5.1 %collective-permute-done.8.refs_7_ = bf16[96,768]{1,0:T(8,128)(2,1)S(1)} collective-permute-done((bf16[96,768]{1,0:T(8,128)(2,1)S(1)}, bf16[96,768]{1,0:T(8,128)(2,1)S(1)}, u32[]{:S(2)}, u32[]{:S(2)}) %collective-permute-start.8) | collective-permute-done | bytes 147488 | tf_op jit(solution)/shard_map/ppermute | solution.py:116
  59.4 9.5 %self_forward.1 = (bf16[3,640,512]{2,1,0:T(8,128)(2,1)S(1)}, bf16[3,192,512]{2,1,0:T(8,128)(2,1)S(1)}, f32[3,8,512]{2,1,0:T(8,128)S(1)}, bf16[640,768]{1,0:T(8,128)(2,1)S(1)}) custom-call(bf16[3,512,768]{2,1,0:T(8,128)(2,1)} %bitcast.195, f32[1,768]{1,0:T(1,128)S(1)} %get-tuple-element.323.gain_ref, bf16[768,640]{1,0:T(8,128)(2,1)S(1)} %bitcast.181, ...), custom_call_target="tpu_custom_call" | custom-call | flops 10350000128 | bytes 8000000 | tf_op jit(solution)/shard_map/self_forward/pallas_call | solution.py:239
  81.1 5.3 %collective-permute-done.13.refs_2_ = bf16[96,768]{1,0:T(8,128)(2,1)S(1)} collective-permute-done((bf16[96,768]{1,0:T(8,128)(2,1)S(1)}, bf16[96,768]{1,0:T(8,128)(2,1)S(1)}, u32[]{:S(2)}, u32[]{:S(2)}) %collective-permute-start.13) | collective-permute-done | bytes 147488 | tf_op jit(solution)/shard_map/ppermute | solution.py:114
  86.4 3.5 collective-permute-done.14.refs_3_
  93.0 3.9 collective-permute-done.15.refs_4_
  103.3 3.2 collective-permute-done.18.refs_7_
  108.9 13.5 %memory_project.1 = (bf16[3,384,2048]{2,1,0:T(8,128)(2,1)}, bf16[3,384,2048]{2,1,0:T(8,128)(2,1)}, bf16[768,768]{1,0:T(8,128)(2,1)S(1)}) custom-call(s32[5,12]{1,0:T(8,128)S(1)} %stack.81.work_ref, bf16[3,1024,768]{2,1,0:T(8,128)(2,1)} %own_ref.3, bf16[3,1024,768]{2,1,0:T(8,128)(2,1)} %collective-permute-done.19.other_ref, bf16[768,768]{1,0:T(8,128)(2,1)S(1)} %bitcast.177), custom_call_target="tpu_custom_call" | custom-call | flops 13799999488 | bytes 12000000 | tf_op jit(solution)/shard_map/memory_project/pallas_call | solution.py:417
  123.9 3.6 collective-permute-done.9.o1_ref
  128.2 9.5 %self_output_stage.1 = (bf16[3,512,768]{2,1,0:T(8,128)(2,1)}, bf16[3,384,512]{2,1,0:T(8,128)(2,1)S(1)}, f32[3,128,768]{2,1,0:T(8,128)S(1)}, bf16[3,768,128]{2,1,...) custom-call(s32[1]{0:T(128)} %bitcast.place_ref, bf16[3,512,768]{2,1,0:T(8,128)(2,1)} %bitcast.196, ...), custom_call_target="tpu_custom_call" | custom-call | flops 6899999744 | bytes 10000000 | tf_op jit(solution)/shard_map/self_output_stage/pallas_call | solution.py:690
  138.5 24.7 %cross_forward.1 = (bf16[3,384,512]{2,1,0:T(8,128)(2,1)S(1)}, f32[3,8,512]{2,1,0:T(8,128)S(1)}) custom-call(s32[5,12]{1,0:T(8,128)S(1)} %stack.81.work_ref, bf16[3,384,512]{2,1,0:T(8,128)(2,1)S(1)} %get-tuple-element.146.q_ref, bf16[3,384,2048]{2,1,0:T(8,128)(2,1)} %get-tuple-element.143.k_ref, bf16[3,384,2048]{2,1,0:T(8,128)(2,1)} %get-tuple-element.147.v_ref), custom_call_target="tpu_custom_call" | custom-call | flops 34500001792 | bytes 16000000 | tf_op jit(solution)/shard_map/cross_forward/pallas_call | solution.py:488
  164.8 14.3 %collective-permute-done.30.other_lse_ref = f32[3,8,512]{2,1,0:T(8,128)S(1)} collective-permute-done((f32[3,8,512]{2,1,0:T(8,128)S(1)}, f32[3,8,512]{2,1,0:T(8,128)S(1)}, u32[]{:S(2)}, u32[]{:S(2)}) %collective-permute-start.30) | collective-permute-done | bytes 49184 | tf_op jit(solution)/shard_map/ppermute | solution.py:55
  182.6 22.8 %feed_forward.1 = (bf16[384,768]{1,0:T(8,128)(2,1)}, f32[384,768]{1,0:T(8,128)S(1)}, bf16[3,384,128]{2,1,0:T(8,128)(2,1)S(1)}, bf16[3,384,128]{2,1,0:T(8,128)(2,...) custom-call(s32[1]{0:T(128)} %bitcast.place_ref, ...), custom_call_target="tpu_custom_call" | custom-call | flops 23000000512 | bytes 24000000 | tf_op jit(solution)/shard_map/feed_forward/pallas_call | solution.py:842
  207.6 6.8 %collective-permute-done.40 = bf16[768,384]{1,0:T(8,128)(2,1)} collective-permute-done((bf16[768,384]{1,0:T(8,128)(2,1)S(1)}, bf16[768,384]{1,0:T(8,128)(2,1)}, u32[]{:S(2)}, u32[]{:S(2)}) %collective-permute-start.40) | collective-permute-done | bytes 589856 | tf_op jit(solution)/shard_map/ppermute | solution.py:51
  222.1 3.2 collective-permute-done.34.do3_ref
  225.4 4.8 %collective-permute-start.42 = (bf16[4,128,768]{2,1,0:T(8,128)(2,1)S(1)}, bf16[4,128,768]{2,1,0:T(8,128)(2,1)S(1)}, u32[]{:S(2)}, u32[]{:S(2)}) collective-permute-start(bf16[4,128,768]{2,1,0:T(8,128)(2,1)S(1)} %dynamic-slice_bitcast_fusion.3), channel_id=1, source_target_pairs={{0,4},{4,0},{8,12},{12,8},{16,20},{20,16},{24,28},{28,24},{1,5},{5... | collective-permute-start | bytes 2359304 | tf_op jit(solution)/shard_map/ppermute | solution.py:146
  230.8 41.3 %cross_backward.1 = (bf16[3,512,384]{2,1,0:T(8,128)(2,1)S(1)}, bf16[3,2048,768]{2,1,0:T(8,128)(2,1)}) custom-call(s32[5,12]{1,0:T(8,128)S(1)} %stack.81.work_ref, s32[1]{0:T(128)} %bitcast.place_ref, bf16[3,384,512]{2,1,0:T(8,128)(2,1)S(1)} %copy-done.17, bf16[3,384,128]{2,1,0:T(8,128)(2,1)S(1)} %get-tuple-element.162.do0_ref, ...), custom_call_target="tpu_custom_call" | custom-call | flops 51749998592 | bytes 24000000 | tf_op jit(solution)/shard_map/cross_backward/pallas_call | solution.py:568
  275.0 3.9 collective-permute-start.44
  280.5 21.4 %memory_backward.1 = (bf16[3,1024,768]{2,1,0:T(8,128)(2,1)}, bf16[3,1024,768]{2,1,0:T(8,128)(2,1)}, bf16[768,768]{1,0:T(8,128)(2,1)S(1)}) custom-call(s32[3,4]{1,0:T(4,128)S(1)} %copy-done.6, bf16[3,1024,768]{2,1,0:T(8,128)(2,1)} %own_ref.3, bf16[3,1024,768]{2,1,0:T(8,128)(2,1)} %collective-permute-done.19.other_ref, ...), custom_call_target="tpu_custom_call" | custom-call | flops 20700000256 | bytes 30000000 | tf_op jit(solution)/shard_map/memory_backward/pallas_call | solution.py:634
  309.2 3.1 collective-permute-done.45.other_ref
  312.3 6.0 %self_output_back.1 = (f32[3,128,768]{2,1,0:T(8,128)S(1)}, bf16[3,192,128]{2,1,0:T(8,128)(2,1)S(1)}, bf16[3,192,128]{2,1,0:T(8,128)(2,1)S(1)}, bf16[3,384,128]{2...) custom-call(s32[1]{0:T(128)} %bitcast.place_ref, ...), custom_call_target="tpu_custom_call" | custom-call | flops 4600000000 | bytes 8000000 | tf_op jit(solution)/shard_map/self_output_back/pallas_call | solution.py:932
  321.9 5.5 %collective-permute-done.47 = bf16[3,384,128]{2,1,0:T(8,128)(2,1)} collective-permute-done((bf16[3,384,128]{2,1,0:T(8,128)(2,1)S(1)}, bf16[3,384,128]{2,1,0:T(8,128)(2,1)}, u32[]{:S(2)}, u32[]{:S(2)}) %collective-permute-start.47) | collective-permute-done | bytes 294944 | tf_op jit(solution)/shard_map/ppermute | solution.py:55
  331.5 5.1 %collective-permute-done.50 = bf16[4,96,1536]{2,1,0:T(8,128)(2,1)} collective-permute-done((bf16[4,96,1536]{2,1,0:T(8,128)(2,1)}, bf16[4,96,1536]{2,1,0:T(8,128)(2,1)}, u32[]{:S(2)}, u32[]{:S(2)}) %collective-permute-start.50) | collective-permute-done | bytes 1179680 | tf_op jit(solution)/shard_map/ppermute | solution.py:146
  341.6 17.4 %self_backward.1 = (bf16[3,512,768]{2,1,0:T(8,128)(2,1)}, bf16[768,640]{1,0:T(8,128)(2,1)S(1)}, f32[8,512]{1,0:T(8,128)S(1)}, f32[1,768]{1,0:T(1,128)S(1)}) custom-call(s32[1]{0:T(128)} %bitcast.place_ref, bf16[3,512,768]{2,1,0:T(8,128)(2,1)} %bitcast.197, f32[1,768]{1,0:T(1,128)S(1)} %copy-done.8, bf16[3,640,512]{2,1,0:T(8,128)(2,1)S(1)} %copy-done.19, ...), custom_call_target="tpu_custom_call" | custom-call | flops 18400000000 | bytes 12000000 | tf_op jit(solution)/shard_map/self_backward/pallas_call | solution.py:331
  362.0 11.3 %collective-permute-done.55 = bf16[96,1024]{1,0:T(8,128)(2,1)} collective-permute-done((bf16[96,1024]{1,0:T(8,128)(2,1)}, bf16[96,1024]{1,0:T(8,128)(2,1)}, u32[]{:S(2)}, u32[]{:S(2)}) %collective-permute-start.55) | collective-permute-done | bytes 196640 | tf_op jit(solution)/shard_map/ppermute | solution.py:159
  379.2 4.6 %collective-permute-done.61 = bf16[96,2048]{1,0:T(8,128)(2,1)S(1)} collective-permute-done((bf16[96,2048]{1,0:T(8,128)(2,1)}, bf16[96,2048]{1,0:T(8,128)(2,1)S(1)}, u32[]{:S(2)}, u32[]{:S(2)}) %collective-permute-start.61) | collective-permute-done | bytes 393248 | tf_op jit(solution)/shard_map/ppermute | solution.py:159
  388.6 5.8 %add_convert_fusion = bf16[3,1024,768]{2,1,0:T(8,128)(2,1)} fusion(bf16[3,1024,768]{2,1,0:T(8,128)(2,1)} %collective-permute-done.60, bf16[3,1024,768]{2,1,0:T(8,128)(2,1)S(1)} %bitcast.190), kind=kLoop, calls=%fused_computation | loop fusion | flops 9437184 | bytes 14155776 | tf_op jit(solution)/shard_map/convert_element_type | solution.py:74
  395.5 3.0 collective-permute-start.63
  399.8 12.6 %collective-permute-done.65 = bf16[3,1,1,128,768]{4,3,0,2,1:T(8,128)(2,1)} collective-permute-done((bf16[3,1,1,128,768]{4,3,0,2,1:T(8,128)(2,1)}, bf16[3,1,1,128,768]{4,3,0,2,1:T(8,128)(2,1)}, u32[]{:S(2)}, u32[]{:S(2)}) %collective-permute-start.65) | collective-permute-done | bytes 589856 | tf_op jit(solution)/shard_map/ppermute | solution.py:55
  (375 shorter events, 139.1 us)
Async XLA Ops:
  7.2 172.9 %all-gather.5.cloned.1.call-start = ((), (), s32[]{:S(2)}) async-start(), calls=%async_computation.1 | async-start | bytes 3244032 | tf_op jit(solution)/shard_map/all_gather | solution.py:1029
  9.0 172.3 %all-gather.3.cloned.1.call-start = ((), (), s32[]{:S(2)}) async-start(), calls=%async_computation | async-start | bytes 7704576 | tf_op jit(solution)/shard_map/all_gather | solution.py:1026
  18.5 15.1 %collective-permute-start.4 = (bf16[96,768]{1,0:T(8,128)(2,1)S(1)}, bf16[96,768]{1,0:T(8,128)(2,1)S(1)}, u32[]{:S(2)}, u32[]{:S(2)}) collective-permute-start(bf16[96,768]{1,0:T(8,128)(2,1)S(1)} %fusion.41.refs_0_), channel_id=1, source_target_pairs={{0,24},{4,28},{8,0},{12,4},{16,8},{20,12},{24,16},{28,20},{1,25},{... | collective-permute-start | bytes 442376 | tf_op jit(solution)/shard_map/ppermute | solution.py:114
  19.9 14.9 %collective-permute-start = (bf16[3,128,768]{2,1,0:T(8,128)(2,1)S(1)}, bf16[3,128,768]{2,1,0:T(8,128)(2,1)S(1)}, u32[]{:S(2)}, u32[]{:S(2)}) collective-permute-start(bf16[3,128,768]{2,1,0:T(8,128)(2,1)S(1)} %copy-done.26), channel_id=1, source_target_pairs={{0,2},{2,0},{1,3},{3,1},{4,6},{6,4},{5,7},{7,5},{8,10},{10,8},{9,1... | collective-permute-start | bytes 1769480 | tf_op jit(solution)/shard_map/ppermute | solution.py:55
  21.1 87.8 %collective-permute-start.19 = (bf16[3,1024,768]{2,1,0:T(8,128)(2,1)}, bf16[3,1024,768]{2,1,0:T(8,128)(2,1)}, u32[]{:S(2)}, u32[]{:S(2)}) collective-permute-start(bf16[3,1024,768]{2,1,0:T(8,128)(2,1)} %own_ref.3), channel_id=1, source_target_pairs={{0,1},{1,0},{2,3},{3,2},{4,5},{5,4},{6,7},{7,6},{8,9},{9,8},{10,11... | collective-permute-start | bytes 14155784 | tf_op jit(solution)/shard_map/ppermute | solution.py:51
  36.1 19.9 %collective-permute-start.1 = (bf16[3,2,128,768]{3,2,0,1:T(8,128)(2,1)}, bf16[3,2,128,768]{3,2,0,1:T(8,128)(2,1)}, u32[]{:S(2)}, u32[]{:S(2)}) collective-permute-start(bf16[3,2,128,768]{3,2,0,1:T(8,128)(2,1)} %pad_maximum_fusion.3), channel_id=1, source_target_pairs={{0,1},{1,0},{2,3},{3,2},{4,5},{5,4},{6,7},{7,6},{8,9},{9,8},{10,11... | collective-permute-start | bytes 3538952 | tf_op jit(solution)/shard_map/ppermute | solution.py:51
  43.1 27.1 %collective-permute-start.20 = (bf16[48,768]{1,0:T(8,128)(2,1)S(1)}, bf16[48,768]{1,0:T(8,128)(2,1)S(1)}, u32[]{:S(2)}, u32[]{:S(2)}) collective-permute-start(bf16[48,768]{1,0:T(8,128)(2,1)S(1)} %fusion.50.refs_0_), channel_id=1, source_target_pairs={{0,8},{4,12},{8,16},{12,20},{16,24},{20,28},{24,0},{28,4},{1,9},{5... | collective-permute-start | bytes 221192 | tf_op jit(solution)/shard_map/ppermute | solution.py:114
  47.0 23.2 %collective-permute-start.21 = (bf16[48,768]{1,0:T(8,128)(2,1)S(1)}, bf16[48,768]{1,0:T(8,128)(2,1)S(1)}, u32[]{:S(2)}, u32[]{:S(2)}) collective-permute-start(bf16[48,768]{1,0:T(8,128)(2,1)S(1)} %fusion.50.refs_0_), channel_id=1, source_target_pairs={{0,16},{4,20},{8,24},{12,28},{16,0},{20,4},{24,8},{28,12},{1,17},{... | collective-permute-start | bytes 221192 | tf_op jit(solution)/shard_map/ppermute | solution.py:114
  52.2 18.0 %collective-permute-start.22 = (bf16[48,768]{1,0:T(8,128)(2,1)S(1)}, bf16[48,768]{1,0:T(8,128)(2,1)S(1)}, u32[]{:S(2)}, u32[]{:S(2)}) collective-permute-start(bf16[48,768]{1,0:T(8,128)(2,1)S(1)} %fusion.50.refs_0_), channel_id=1, source_target_pairs={{0,24},{4,28},{8,0},{12,4},{16,8},{20,12},{24,16},{28,20},{1,25},{... | collective-permute-start | bytes 221192 | tf_op jit(solution)/shard_map/ppermute | solution.py:114
  79.1 27.9 %collective-permute-start.27 = (bf16[8,48,768]{2,1,0:T(8,128)(2,1)S(1)}, bf16[8,48,768]{2,1,0:T(8,128)(2,1)}, u32[]{:S(2)}, u32[]{:S(2)}) collective-permute-start(bf16[8,48,768]{2,1,0:T(8,128)(2,1)S(1)} %assemble.5), channel_id=1, source_target_pairs={{0,2},{2,0},{1,3},{3,1},{4,6},{6,4},{5,7},{7,5},{8,10},{10,8},{9,1... | collective-permute-start | bytes 1769480 | tf_op jit(solution)/shard_map/ppermute | solution.py:55
  100.1 23.8 %collective-permute-start.10 = (bf16[3,192,512]{2,1,0:T(8,128)(2,1)S(1)}, bf16[3,192,512]{2,1,0:T(8,128)(2,1)}, u32[]{:S(2)}, u32[]{:S(2)}) collective-permute-start(bf16[3,192,512]{2,1,0:T(8,128)(2,1)S(1)} %get-tuple-element.133.o0_ref), channel_id=1, source_target_pairs={{0,2},{2,0},{1,3},{3,1},{4,6},{6,4},{5,7},{7,5},{8,10},{10,8},{9,1... | collective-permute-start | bytes 1769480 | tf_op jit(solution)/shard_map/ppermute | solution.py:55
  163.3 15.9 %collective-permute-start.29 = (bf16[3,384,256]{2,1,0:T(8,128)(2,1)S(1)}, bf16[3,384,256]{2,1,0:T(8,128)(2,1)S(1)}, u32[]{:S(2)}, u32[]{:S(2)}) collective-permute-start(bf16[3,384,256]{2,1,0:T(8,128)(2,1)S(1)} %constant_dynamic-slice_fusion.11), channel_id=1, source_target_pairs={{0,2},{2,0},{1,3},{3,1},{4,6},{6,4},{5,7},{7,5},{8,10},{10,8},{9,1... | collective-permute-start | bytes 1769480 | tf_op jit(solution)/shard_map/ppermute | solution.py:55
  163.4 15.8 %collective-permute-start.30 = (f32[3,8,512]{2,1,0:T(8,128)S(1)}, f32[3,8,512]{2,1,0:T(8,128)S(1)}, u32[]{:S(2)}, u32[]{:S(2)}) collective-permute-start(f32[3,8,512]{2,1,0:T(8,128)S(1)} %get-tuple-element.149.lse_ref), channel_id=1, source_target_pairs={{0,2},{2,0},{1,3},{3,1},{4,6},{6,4},{5,7},{7,5},{8,10},{10,8},{9,1... | collective-permute-start | bytes 147464 | tf_op jit(solution)/shard_map/ppermute | solution.py:55
  207.5 14.6 %collective-permute-start.33 = (bf16[3,384,128]{2,1,0:T(8,128)(2,1)S(1)}, bf16[3,384,128]{2,1,0:T(8,128)(2,1)S(1)}, u32[]{:S(2)}, u32[]{:S(2)}) collective-permute-start(bf16[3,384,128]{2,1,0:T(8,128)(2,1)S(1)} %get-tuple-element.162.do0_ref), channel_id=1, source_target_pairs={{0,2},{2,0},{1,3},{3,1},{4,6},{6,4},{5,7},{7,5},{8,10},{10,8},{9,1... | collective-permute-start | bytes 884744 | tf_op jit(solution)/shard_map/ppermute | solution.py:55
  225.4 46.7 %collective-permute-start.42 = (bf16[4,128,768]{2,1,0:T(8,128)(2,1)S(1)}, bf16[4,128,768]{2,1,0:T(8,128)(2,1)S(1)}, u32[]{:S(2)}, u32[]{:S(2)}) collective-permute-start(bf16[4,128,768]{2,1,0:T(8,128)(2,1)S(1)} %dynamic-slice_bitcast_fusion.3), channel_id=1, source_target_pairs={{0,4},{4,0},{8,12},{12,8},{16,20},{20,16},{24,28},{28,24},{1,5},{5... | collective-permute-start | bytes 2359304 | tf_op jit(solution)/shard_map/ppermute | solution.py:146
  230.2 42.1 %collective-permute-start.41 = (bf16[768,1024]{1,0:T(8,128)(2,1)S(1)}, bf16[768,1024]{1,0:T(8,128)(2,1)S(1)}, u32[]{:S(2)}, u32[]{:S(2)}) collective-permute-start(bf16[768,1024]{1,0:T(8,128)(2,1)S(1)} %add_convert_fusion.3), channel_id=1, source_target_pairs={{0,2},{2,0},{1,3},{3,1},{4,6},{6,4},{5,7},{7,5},{8,10},{10,8},{9,1... | collective-permute-start | bytes 4718600 | tf_op jit(solution)/shard_map/ppermute | solution.py:55
  272.4 46.4 %collective-permute-start.51 = (bf16[4,64,768]{2,1,0:T(8,128)(2,1)S(1)}, bf16[4,64,768]{2,1,0:T(8,128)(2,1)S(1)}, u32[]{:S(2)}, u32[]{:S(2)}) collective-permute-start(bf16[4,64,768]{2,1,0:T(8,128)(2,1)S(1)} %constant_dynamic-slice_fusion.3), channel_id=1, source_target_pairs={{0,2},{2,0},{1,3},{3,1},{4,6},{6,4},{5,7},{7,5},{8,10},{10,8},{9,1... | collective-permute-start | bytes 1179656 | tf_op jit(solution)/shard_map/ppermute | solution.py:55
  275.0 30.7 %collective-permute-start.44 = (bf16[4,96,1024]{2,1,0:T(8,128)(2,1)S(1)}, bf16[4,96,1024]{2,1,0:T(8,128)(2,1)S(1)}, u32[]{:S(2)}, u32[]{:S(2)}) collective-permute-start(bf16[4,96,1024]{2,1,0:T(8,128)(2,1)S(1)} %dynamic-slice_bitcast_fusion.2), channel_id=1, source_target_pairs={{0,4},{4,0},{8,12},{12,8},{16,20},{20,16},{24,28},{28,24},{1,5},{5... | collective-permute-start | bytes 2359304 | tf_op jit(solution)/shard_map/ppermute | solution.py:146
  279.0 27.9 %collective-permute-start.43 = (bf16[3,256,384]{2,1,0:T(8,128)(2,1)S(1)}, bf16[3,256,384]{2,1,0:T(8,128)(2,1)S(1)}, u32[]{:S(2)}, u32[]{:S(2)}) collective-permute-start(bf16[3,256,384]{2,1,0:T(8,128)(2,1)S(1)} %constant_dynamic-slice_fusion.8), channel_id=1, source_target_pairs={{0,2},{2,0},{1,3},{3,1},{4,6},{6,4},{5,7},{7,5},{8,10},{10,8},{9,1... | collective-permute-start | bytes 1769480 | tf_op jit(solution)/shard_map/ppermute | solution.py:55
  301.9 86.7 %collective-permute-start.60 = (bf16[3,1024,768]{2,1,0:T(8,128)(2,1)}, bf16[3,1024,768]{2,1,0:T(8,128)(2,1)}, u32[]{:S(2)}, u32[]{:S(2)}) collective-permute-start(bf16[3,1024,768]{2,1,0:T(8,128)(2,1)} %get-tuple-element.218), channel_id=1, source_target_pairs={{0,1},{1,0},{2,3},{3,2},{4,5},{5,4},{6,7},{7,6},{8,9},{9,8},{10,11... | collective-permute-start | bytes 14155784 | tf_op jit(solution)/shard_map/ppermute | solution.py:51
  309.2 27.4 %collective-permute-start.50 = (bf16[4,96,1536]{2,1,0:T(8,128)(2,1)}, bf16[4,96,1536]{2,1,0:T(8,128)(2,1)}, u32[]{:S(2)}, u32[]{:S(2)}) collective-permute-start(bf16[4,96,1536]{2,1,0:T(8,128)(2,1)} %get-tuple-element.247), channel_id=1, source_target_pairs={{0,4},{4,0},{8,12},{12,8},{16,20},{20,16},{24,28},{28,24},{1,5},{5... | collective-permute-start | bytes 3538952 | tf_op jit(solution)/shard_map/ppermute | solution.py:146
  327.3 32.4 %collective-permute-start.53 = (bf16[96,1024]{1,0:T(8,128)(2,1)}, bf16[96,1024]{1,0:T(8,128)(2,1)}, u32[]{:S(2)}, u32[]{:S(2)}) collective-permute-start(bf16[96,1024]{1,0:T(8,128)(2,1)} %get-tuple-element.281), channel_id=1, source_target_pairs={{0,8},{4,12},{8,16},{12,20},{16,24},{20,28},{24,0},{28,4},{1,9},{5... | collective-permute-start | bytes 589832 | tf_op jit(solution)/shard_map/ppermute | solution.py:159
  331.5 28.9 %collective-permute-start.54 = (bf16[96,1024]{1,0:T(8,128)(2,1)}, bf16[96,1024]{1,0:T(8,128)(2,1)}, u32[]{:S(2)}, u32[]{:S(2)}) collective-permute-start(bf16[96,1024]{1,0:T(8,128)(2,1)} %get-tuple-element.280), channel_id=1, source_target_pairs={{0,16},{4,20},{8,24},{12,28},{16,0},{20,4},{24,8},{28,12},{1,17},{... | collective-permute-start | bytes 589832 | tf_op jit(solution)/shard_map/ppermute | solution.py:159
  340.5 33.9 %collective-permute-start.56 = (bf16[96,2048]{1,0:T(8,128)(2,1)}, bf16[96,2048]{1,0:T(8,128)(2,1)}, u32[]{:S(2)}, u32[]{:S(2)}) collective-permute-start(bf16[96,2048]{1,0:T(8,128)(2,1)} %get-tuple-element.255), channel_id=1, source_target_pairs={{0,8},{4,12},{8,16},{12,20},{16,24},{20,28},{24,0},{28,4},{1,9},{5... | collective-permute-start | bytes 1179656 | tf_op jit(solution)/shard_map/ppermute | solution.py:159
  340.5 33.9 %collective-permute-start.57 = (bf16[96,2048]{1,0:T(8,128)(2,1)}, bf16[96,2048]{1,0:T(8,128)(2,1)}, u32[]{:S(2)}, u32[]{:S(2)}) collective-permute-start(bf16[96,2048]{1,0:T(8,128)(2,1)} %get-tuple-element.256), channel_id=1, source_target_pairs={{0,16},{4,20},{8,24},{12,28},{16,0},{20,4},{24,8},{28,12},{1,17},{... | collective-permute-start | bytes 1179656 | tf_op jit(solution)/shard_map/ppermute | solution.py:159
  359.7 14.7 %collective-permute-start.52 = (bf16[8,48,384]{2,1,0:T(8,128)(2,1)}, bf16[8,48,384]{2,1,0:T(8,128)(2,1)S(1)}, u32[]{:S(2)}, u32[]{:S(2)}) collective-permute-start(bf16[8,48,384]{2,1,0:T(8,128)(2,1)} %constant_dynamic-slice_fusion.2), channel_id=1, source_target_pairs={{0,2},{2,0},{1,3},{3,1},{4,6},{6,4},{5,7},{7,5},{8,10},{10,8},{9,1... | collective-permute-start | bytes 884744 | tf_op jit(solution)/shard_map/ppermute | solution.py:55
  377.7 16.7 %collective-permute-start.59 = (bf16[4,48,1792]{2,1,0:T(8,128)(2,1)S(1)}, bf16[4,48,1792]{2,1,0:T(8,128)(2,1)S(1)}, u32[]{:S(2)}, u32[]{:S(2)}) collective-permute-start(bf16[4,48,1792]{2,1,0:T(8,128)(2,1)S(1)} %get-tuple-element.257), channel_id=1, source_target_pairs={{0,4},{4,0},{8,12},{12,8},{16,20},{20,16},{24,28},{28,24},{1,5},{5... | collective-permute-start | bytes 2064392 | tf_op jit(solution)/shard_map/ppermute | solution.py:146
  386.0 13.8 %collective-permute-start.66 = (bf16[96,3072]{1,0:T(8,128)(2,1)}, bf16[96,3072]{1,0:T(8,128)(2,1)}, u32[]{:S(2)}, u32[]{:S(2)}) collective-permute-start(bf16[96,3072]{1,0:T(8,128)(2,1)} %pad_maximum_fusion.5), channel_id=1, source_target_pairs={{0,2},{2,0},{1,3},{3,1},{4,6},{6,4},{5,7},{7,5},{8,10},{10,8},{9,1... | collective-permute-start | bytes 1769480 | tf_op jit(solution)/shard_map/ppermute | solution.py:55
  387.1 25.3 %collective-permute-start.65 = (bf16[3,1,1,128,768]{4,3,0,2,1:T(8,128)(2,1)}, bf16[3,1,1,128,768]{4,3,0,2,1:T(8,128)(2,1)}, u32[]{:S(2)}, u32[]{:S(2)}) collective-permute-start(bf16[3,1,1,128,768]{4,3,0,2,1:T(8,128)(2,1)} %dynamic-slice_convert_fusion), channel_id=1, source_target_pairs={{0,2},{2,0},{1,3},{3,1},{4,6},{6,4},{5,7},{7,5},{8,10},{10,8},{9,1... | collective-permute-start | bytes 1769480 | tf_op jit(solution)/shard_map/ppermute | solution.py:55
  395.4 17.0 %collective-permute-start.62 = (bf16[48,1792]{1,0:T(8,128)(2,1)}, bf16[48,1792]{1,0:T(8,128)(2,1)}, u32[]{:S(2)}, u32[]{:S(2)}) collective-permute-start(bf16[48,1792]{1,0:T(8,128)(2,1)} %get-tuple-element.287), channel_id=1, source_target_pairs={{0,8},{4,12},{8,16},{12,20},{16,24},{20,28},{24,0},{28,4},{1,9},{5... | collective-permute-start | bytes 516104 | tf_op jit(solution)/shard_map/ppermute | solution.py:159
  395.5 16.9 %collective-permute-start.63 = (bf16[48,1792]{1,0:T(8,128)(2,1)}, bf16[48,1792]{1,0:T(8,128)(2,1)}, u32[]{:S(2)}, u32[]{:S(2)}) collective-permute-start(bf16[48,1792]{1,0:T(8,128)(2,1)} %get-tuple-element.286), channel_id=1, source_target_pairs={{0,16},{4,20},{8,24},{12,28},{16,0},{20,4},{24,8},{28,12},{1,17},{... | collective-permute-start | bytes 516104 | tf_op jit(solution)/shard_map/ppermute | solution.py:159
  398.6 15.2 %collective-permute-start.64 = (bf16[48,1792]{1,0:T(8,128)(2,1)}, bf16[48,1792]{1,0:T(8,128)(2,1)}, u32[]{:S(2)}, u32[]{:S(2)}) collective-permute-start(bf16[48,1792]{1,0:T(8,128)(2,1)} %get-tuple-element.285), channel_id=1, source_target_pairs={{0,24},{4,28},{8,0},{12,4},{16,8},{20,12},{24,16},{28,20},{1,25},{... | collective-permute-start | bytes 516104 | tf_op jit(solution)/shard_map/ppermute | solution.py:159
  (84 other events, 772.5 us)
Sparse Core Ops, SparseCore 0:
  11.5 67.0 all-gather.4
  82.1 75.2 all-gather.2

commit v5 on v4

--- a/solution.py
+++ b/solution.py
@@ -1136,7 +1136,7 @@
     dn1_came, sums_came = across_swap(dn1_sent), across_swap(sums)
     last, dn1_sent, enc_grad, sums = lax.optimization_barrier((last, dn1_sent, enc_grad, sums))
     last = z_swap(total(last))
-    last, dn1_came, sums_came = lax.optimization_barrier((last, dn1_came, sums_came))
+    last, dn1_came = lax.optimization_barrier((last, dn1_came))
     last_sum = total(last)
     last_came = across_swap(last_sum)
     dn1 = plus(part_of(column, row, 2, 1), dn1_came)

time: 450 us -> 438 us (0.973)
  Pallas kernels: 168 us -> 160 us
  other arithmetic: 53.5 us -> 46.9 us
  transfers between devices with their start and end apart: 72 -> 72, of which waited for: 29 -> 32; matrix products, arithmetic and copies ran while one was open for 16% -> 15% of each run, Pallas kernels for 33% -> 32%
where the time goes in v5:
time: 438 us; the launch traced here: 430 us
  Pallas kernels  160 us (37%)
  waiting for transfers between devices  116 us (26%)
  starting transfers between devices  59.9 us (14%)
  other arithmetic  46.9 us (11%)
  local copies, waits for them, and re-layouts  28.6 us (7%)
  between operations  15.6 us (4%)
    ppermute x17, waiting for transfers between devices, across_swap(): return lax.ppermute(value, 'narrow', ACROSS)  37.2 us
    pallas_call x1, Pallas kernels, cross_backward(): pl.pallas_call(cross_backward_kernel, grid_spec=pltpu.PrefetchScalarGridS...  37.2 us
    ppermute x12, waiting for transfers between devices, wide_gather(): pieces = line + [lax.ppermute(piece, 'wide', BESIDE) for piece in line]  25.5 us
    pallas_call x1, Pallas kernels, feed_forward(): pl.pallas_call(functools.partial(feed_forward_kernel, piece=piece), grid=...  22.8 us
    pallas_call x1, Pallas kernels, cross_forward(): pl.pallas_call(cross_forward_kernel, grid_spec=pltpu.PrefetchScalarGridSp...  22.4 us
    pallas_call x1, Pallas kernels, memory_backward(): pl.pallas_call(memory_backward_kernel, grid_spec=pltpu.PrefetchScalarGrid...  20.1 us
    pallas_call x1, Pallas kernels, self_backward(): pl.pallas_call(self_backward_kernel, grid=(examples,), in_specs=[pl.Block...  17.3 us
    ppermute x9, waiting for transfers between devices, z_swap(): lax.ppermute(s, 'wide', along(i + 1))  16.1 us
  transfers between devices with their start and end apart: 72, of which 32 were waited for; matrix products, arithmetic and copies ran while one was open for 15% of the time, Pallas kernels for 32%

profile of v5, /device:TPU:9, one launch (start us, length us, event | category | flops | bytes accessed | tf_op | source)
XLA Modules:
  0.0 429.7 jit_solution(14062553761763415380)
XLA Ops:
  26.4 4.6 %collective-permute-done.3.refs_2_ = bf16[96,768]{1,0:T(8,128)(2,1)S(1)} collective-permute-done((bf16[96,768]{1,0:T(8,128)(2,1)S(1)}, bf16[96,768]{1,0:T(8,128)(2,1)S(1)}, u32[]{:S(2)}, u32[]{:S(2)}) %collective-permute-start.3) | collective-permute-done | bytes 147488 | tf_op jit(solution)/shard_map/ppermute | solution.py:114
  31.0 2.6 collective-permute-done.4.refs_3_
  40.4 2.6 collective-permute-done.6.refs_5_
  43.1 3.8 collective-permute-done.7.refs_6_
  47.1 5.1 %collective-permute-done.8.refs_7_ = bf16[96,768]{1,0:T(8,128)(2,1)S(1)} collective-permute-done((bf16[96,768]{1,0:T(8,128)(2,1)S(1)}, bf16[96,768]{1,0:T(8,128)(2,1)S(1)}, u32[]{:S(2)}, u32[]{:S(2)}) %collective-permute-start.8) | collective-permute-done | bytes 147488 | tf_op jit(solution)/shard_map/ppermute | solution.py:116
  59.4 9.5 %self_forward.1 = (bf16[3,640,512]{2,1,0:T(8,128)(2,1)S(1)}, bf16[3,192,512]{2,1,0:T(8,128)(2,1)S(1)}, f32[3,8,512]{2,1,0:T(8,128)S(1)}, bf16[640,768]{1,0:T(8,128)(2,1)S(1)}) custom-call(bf16[3,512,768]{2,1,0:T(8,128)(2,1)} %bitcast.195, f32[1,768]{1,0:T(1,128)S(1)} %get-tuple-element.321.gain_ref, bf16[768,640]{1,0:T(8,128)(2,1)S(1)} %bitcast.181, ...), custom_call_target="tpu_custom_call" | custom-call | flops 10350000128 | bytes 8000000 | tf_op jit(solution)/shard_map/self_forward/pallas_call | solution.py:239
  81.1 5.3 %collective-permute-done.13.refs_2_ = bf16[96,768]{1,0:T(8,128)(2,1)S(1)} collective-permute-done((bf16[96,768]{1,0:T(8,128)(2,1)S(1)}, bf16[96,768]{1,0:T(8,128)(2,1)S(1)}, u32[]{:S(2)}, u32[]{:S(2)}) %collective-permute-start.13) | collective-permute-done | bytes 147488 | tf_op jit(solution)/shard_map/ppermute | solution.py:114
  86.4 3.5 collective-permute-done.14.refs_3_
  93.0 3.9 collective-permute-done.15.refs_4_
  103.3 3.2 collective-permute-done.18.refs_7_
  108.9 13.2 %memory_project.1 = (bf16[3,384,2048]{2,1,0:T(8,128)(2,1)}, bf16[3,384,2048]{2,1,0:T(8,128)(2,1)}, bf16[768,768]{1,0:T(8,128)(2,1)S(1)}) custom-call(s32[5,12]{1,0:T(8,128)S(1)} %stack.81.work_ref, bf16[3,1024,768]{2,1,0:T(8,128)(2,1)} %own_ref.3, bf16[3,1024,768]{2,1,0:T(8,128)(2,1)} %collective-permute-done.19.other_ref, bf16[768,768]{1,0:T(8,128)(2,1)S(1)} %bitcast.177), custom_call_target="tpu_custom_call" | custom-call | flops 13799999488 | bytes 12000000 | tf_op jit(solution)/shard_map/memory_project/pallas_call | solution.py:417
  123.7 3.6 collective-permute-done.9.o1_ref
  127.9 9.6 %self_output_stage.1 = (bf16[3,512,768]{2,1,0:T(8,128)(2,1)}, bf16[3,384,512]{2,1,0:T(8,128)(2,1)S(1)}, f32[3,128,768]{2,1,0:T(8,128)S(1)}, bf16[3,768,128]{2,1,...) custom-call(s32[1]{0:T(128)} %bitcast.place_ref, bf16[3,512,768]{2,1,0:T(8,128)(2,1)} %bitcast.196, ...), custom_call_target="tpu_custom_call" | custom-call | flops 6899999744 | bytes 10000000 | tf_op jit(solution)/shard_map/self_output_stage/pallas_call | solution.py:690
  138.3 22.4 %cross_forward.1 = (bf16[3,384,512]{2,1,0:T(8,128)(2,1)S(1)}, f32[3,8,512]{2,1,0:T(8,128)S(1)}) custom-call(s32[5,12]{1,0:T(8,128)S(1)} %stack.81.work_ref, bf16[3,384,512]{2,1,0:T(8,128)(2,1)S(1)} %get-tuple-element.145.q_ref, bf16[3,384,2048]{2,1,0:T(8,128)(2,1)} %get-tuple-element.142.k_ref, bf16[3,384,2048]{2,1,0:T(8,128)(2,1)} %get-tuple-element.146.v_ref), custom_call_target="tpu_custom_call" | custom-call | flops 34500001792 | bytes 16000000 | tf_op jit(solution)/shard_map/cross_forward/pallas_call | solution.py:488
  162.3 14.1 %collective-permute-done.30.other_lse_ref = f32[3,8,512]{2,1,0:T(8,128)S(1)} collective-permute-done((f32[3,8,512]{2,1,0:T(8,128)S(1)}, f32[3,8,512]{2,1,0:T(8,128)S(1)}, u32[]{:S(2)}, u32[]{:S(2)}) %collective-permute-start.30) | collective-permute-done | bytes 49184 | tf_op jit(solution)/shard_map/ppermute | solution.py:55
  179.8 22.8 %feed_forward.1 = (bf16[384,768]{1,0:T(8,128)(2,1)}, f32[384,768]{1,0:T(8,128)S(1)}, bf16[3,384,128]{2,1,0:T(8,128)(2,1)S(1)}, bf16[3,384,128]{2,1,0:T(8,128)(2,...) custom-call(s32[1]{0:T(128)} %bitcast.place_ref, ...), custom_call_target="tpu_custom_call" | custom-call | flops 23000000512 | bytes 24000000 | tf_op jit(solution)/shard_map/feed_forward/pallas_call | solution.py:842
  204.7 6.8 %collective-permute-done.40 = bf16[768,384]{1,0:T(8,128)(2,1)} collective-permute-done((bf16[768,384]{1,0:T(8,128)(2,1)S(1)}, bf16[768,384]{1,0:T(8,128)(2,1)}, u32[]{:S(2)}, u32[]{:S(2)}) %collective-permute-start.40) | collective-permute-done | bytes 589856 | tf_op jit(solution)/shard_map/ppermute | solution.py:51
  219.1 3.1 collective-permute-done.34.do3_ref
  222.2 4.5 %collective-permute-start.42 = (bf16[4,128,768]{2,1,0:T(8,128)(2,1)S(1)}, bf16[4,128,768]{2,1,0:T(8,128)(2,1)S(1)}, u32[]{:S(2)}, u32[]{:S(2)}) collective-permute-start(bf16[4,128,768]{2,1,0:T(8,128)(2,1)S(1)} %dynamic-slice_bitcast_fusion.3), channel_id=1, source_target_pairs={{0,4},{4,0},{8,12},{12,8},{16,20},{20,16},{24,28},{28,24},{1,5},{5... | collective-permute-start | bytes 2359304 | tf_op jit(solution)/shard_map/ppermute | solution.py:146
  227.3 37.2 %cross_backward.1 = (bf16[3,512,384]{2,1,0:T(8,128)(2,1)S(1)}, bf16[3,2048,768]{2,1,0:T(8,128)(2,1)}) custom-call(s32[5,12]{1,0:T(8,128)S(1)} %stack.81.work_ref, s32[1]{0:T(128)} %bitcast.place_ref, bf16[3,384,512]{2,1,0:T(8,128)(2,1)S(1)} %copy-done.17, bf16[3,384,128]{2,1,0:T(8,128)(2,1)S(1)} %get-tuple-element.161.do0_ref, ...), custom_call_target="tpu_custom_call" | custom-call | flops 51749998592 | bytes 24000000 | tf_op jit(solution)/shard_map/cross_backward/pallas_call | solution.py:568
  267.4 4.3 %collective-permute-start.44 = (bf16[4,96,1024]{2,1,0:T(8,128)(2,1)S(1)}, bf16[4,96,1024]{2,1,0:T(8,128)(2,1)S(1)}, u32[]{:S(2)}, u32[]{:S(2)}) collective-permute-start(bf16[4,96,1024]{2,1,0:T(8,128)(2,1)S(1)} %dynamic-slice_bitcast_fusion.2), channel_id=1, source_target_pairs={{0,4},{4,0},{8,12},{12,8},{16,20},{20,16},{24,28},{28,24},{1,5},{5... | collective-permute-start | bytes 2359304 | tf_op jit(solution)/shard_map/ppermute | solution.py:146
  273.3 20.1 %memory_backward.1 = (bf16[3,1024,768]{2,1,0:T(8,128)(2,1)}, bf16[3,1024,768]{2,1,0:T(8,128)(2,1)}, bf16[768,768]{1,0:T(8,128)(2,1)S(1)}) custom-call(s32[3,4]{1,0:T(4,128)S(1)} %copy-done.6, bf16[3,1024,768]{2,1,0:T(8,128)(2,1)} %own_ref.3, bf16[3,1024,768]{2,1,0:T(8,128)(2,1)} %collective-permute-done.19.other_ref, ...), custom_call_target="tpu_custom_call" | custom-call | flops 20700000256 | bytes 30000000 | tf_op jit(solution)/shard_map/memory_backward/pallas_call | solution.py:634
  301.7 6.1 %self_output_back.1 = (f32[3,128,768]{2,1,0:T(8,128)S(1)}, bf16[3,192,128]{2,1,0:T(8,128)(2,1)S(1)}, bf16[3,192,128]{2,1,0:T(8,128)(2,1)S(1)}, bf16[3,384,128]{2...) custom-call(s32[1]{0:T(128)} %bitcast.place_ref, ...), custom_call_target="tpu_custom_call" | custom-call | flops 4600000000 | bytes 8000000 | tf_op jit(solution)/shard_map/self_output_back/pallas_call | solution.py:932
  311.3 5.4 %collective-permute-done.47 = bf16[3,384,128]{2,1,0:T(8,128)(2,1)} collective-permute-done((bf16[3,384,128]{2,1,0:T(8,128)(2,1)S(1)}, bf16[3,384,128]{2,1,0:T(8,128)(2,1)}, u32[]{:S(2)}, u32[]{:S(2)}) %collective-permute-start.47) | collective-permute-done | bytes 294944 | tf_op jit(solution)/shard_map/ppermute | solution.py:55
  321.0 5.2 %collective-permute-done.50 = bf16[4,96,1536]{2,1,0:T(8,128)(2,1)} collective-permute-done((bf16[4,96,1536]{2,1,0:T(8,128)(2,1)}, bf16[4,96,1536]{2,1,0:T(8,128)(2,1)}, u32[]{:S(2)}, u32[]{:S(2)}) %collective-permute-start.50) | collective-permute-done | bytes 1179680 | tf_op jit(solution)/shard_map/ppermute | solution.py:146
  331.5 17.3 %self_backward.1 = (bf16[3,512,768]{2,1,0:T(8,128)(2,1)}, bf16[768,640]{1,0:T(8,128)(2,1)S(1)}, f32[8,512]{1,0:T(8,128)S(1)}, f32[1,768]{1,0:T(1,128)S(1)}) custom-call(s32[1]{0:T(128)} %bitcast.place_ref, bf16[3,512,768]{2,1,0:T(8,128)(2,1)} %bitcast.197, f32[1,768]{1,0:T(1,128)S(1)} %copy-done.8, bf16[3,640,512]{2,1,0:T(8,128)(2,1)S(1)} %copy-done.19, ...), custom_call_target="tpu_custom_call" | custom-call | flops 18400000000 | bytes 12000000 | tf_op jit(solution)/shard_map/self_backward/pallas_call | solution.py:331
  351.6 11.3 %collective-permute-done.55 = bf16[96,1024]{1,0:T(8,128)(2,1)} collective-permute-done((bf16[96,1024]{1,0:T(8,128)(2,1)}, bf16[96,1024]{1,0:T(8,128)(2,1)}, u32[]{:S(2)}, u32[]{:S(2)}) %collective-permute-start.55) | collective-permute-done | bytes 196640 | tf_op jit(solution)/shard_map/ppermute | solution.py:159
  370.3 3.0 collective-permute-done.61
  376.7 5.8 %add_convert_fusion = bf16[3,1024,768]{2,1,0:T(8,128)(2,1)} fusion(bf16[3,1024,768]{2,1,0:T(8,128)(2,1)} %collective-permute-done.60, bf16[3,1024,768]{2,1,0:T(8,128)(2,1)S(1)} %bitcast.190), kind=kLoop, calls=%fused_computation | loop fusion | flops 9437184 | bytes 14155776 | tf_op jit(solution)/shard_map/convert_element_type | solution.py:74
  388.6 4.1 collective-permute-start.69
  392.7 8.3 %collective-permute-done.65 = bf16[3,1,1,128,768]{4,3,0,2,1:T(8,128)(2,1)S(1)} collective-permute-done((bf16[3,1,1,128,768]{4,3,0,2,1:T(8,128)(2,1)S(1)}, bf16[3,1,1,128,768]{4,3,0,2,1:T(8,128)(2,1)S(1)}, u32[]{:S(2)}, u32[]{:S(2)}) %collective-permute-start.65) | collective-permute-done | bytes 589856 | tf_op jit(solution)/shard_map/ppermute | solution.py:55
  403.3 5.0 %collective-permute-done.66 = bf16[48,1792]{1,0:T(8,128)(2,1)S(1)} collective-permute-done((bf16[48,1792]{1,0:T(8,128)(2,1)S(1)}, bf16[48,1792]{1,0:T(8,128)(2,1)S(1)}, u32[]{:S(2)}, u32[]{:S(2)}) %collective-permute-start.66) | collective-permute-done | bytes 172064 | tf_op jit(solution)/shard_map/ppermute | solution.py:55
  (375 shorter events, 137.0 us)
Async XLA Ops:
  7.2 169.9 %all-gather.5.cloned.1.call-start = ((), (), s32[]{:S(2)}) async-start(), calls=%async_computation.1 | async-start | bytes 3244032 | tf_op jit(solution)/shard_map/all_gather | solution.py:1029
  9.0 169.5 %all-gather.3.cloned.1.call-start = ((), (), s32[]{:S(2)}) async-start(), calls=%async_computation | async-start | bytes 7704576 | tf_op jit(solution)/shard_map/all_gather | solution.py:1026
  18.5 15.1 %collective-permute-start.4 = (bf16[96,768]{1,0:T(8,128)(2,1)S(1)}, bf16[96,768]{1,0:T(8,128)(2,1)S(1)}, u32[]{:S(2)}, u32[]{:S(2)}) collective-permute-start(bf16[96,768]{1,0:T(8,128)(2,1)S(1)} %fusion.41.refs_0_), channel_id=1, source_target_pairs={{0,24},{4,28},{8,0},{12,4},{16,8},{20,12},{24,16},{28,20},{1,25},{... | collective-permute-start | bytes 442376 | tf_op jit(solution)/shard_map/ppermute | solution.py:114
  19.9 14.9 %collective-permute-start = (bf16[3,128,768]{2,1,0:T(8,128)(2,1)S(1)}, bf16[3,128,768]{2,1,0:T(8,128)(2,1)S(1)}, u32[]{:S(2)}, u32[]{:S(2)}) collective-permute-start(bf16[3,128,768]{2,1,0:T(8,128)(2,1)S(1)} %copy-done.26), channel_id=1, source_target_pairs={{0,2},{2,0},{1,3},{3,1},{4,6},{6,4},{5,7},{7,5},{8,10},{10,8},{9,1... | collective-permute-start | bytes 1769480 | tf_op jit(solution)/shard_map/ppermute | solution.py:55
  21.1 87.8 %collective-permute-start.19 = (bf16[3,1024,768]{2,1,0:T(8,128)(2,1)}, bf16[3,1024,768]{2,1,0:T(8,128)(2,1)}, u32[]{:S(2)}, u32[]{:S(2)}) collective-permute-start(bf16[3,1024,768]{2,1,0:T(8,128)(2,1)} %own_ref.3), channel_id=1, source_target_pairs={{0,1},{1,0},{2,3},{3,2},{4,5},{5,4},{6,7},{7,6},{8,9},{9,8},{10,11... | collective-permute-start | bytes 14155784 | tf_op jit(solution)/shard_map/ppermute | solution.py:51
  36.1 19.9 %collective-permute-start.1 = (bf16[3,2,128,768]{3,2,0,1:T(8,128)(2,1)}, bf16[3,2,128,768]{3,2,0,1:T(8,128)(2,1)}, u32[]{:S(2)}, u32[]{:S(2)}) collective-permute-start(bf16[3,2,128,768]{3,2,0,1:T(8,128)(2,1)} %pad_maximum_fusion.3), channel_id=1, source_target_pairs={{0,1},{1,0},{2,3},{3,2},{4,5},{5,4},{6,7},{7,6},{8,9},{9,8},{10,11... | collective-permute-start | bytes 3538952 | tf_op jit(solution)/shard_map/ppermute | solution.py:51
  43.1 27.1 %collective-permute-start.20 = (bf16[48,768]{1,0:T(8,128)(2,1)S(1)}, bf16[48,768]{1,0:T(8,128)(2,1)S(1)}, u32[]{:S(2)}, u32[]{:S(2)}) collective-permute-start(bf16[48,768]{1,0:T(8,128)(2,1)S(1)} %fusion.50.refs_0_), channel_id=1, source_target_pairs={{0,8},{4,12},{8,16},{12,20},{16,24},{20,28},{24,0},{28,4},{1,9},{5... | collective-permute-start | bytes 221192 | tf_op jit(solution)/shard_map/ppermute | solution.py:114
  47.0 23.2 %collective-permute-start.21 = (bf16[48,768]{1,0:T(8,128)(2,1)S(1)}, bf16[48,768]{1,0:T(8,128)(2,1)S(1)}, u32[]{:S(2)}, u32[]{:S(2)}) collective-permute-start(bf16[48,768]{1,0:T(8,128)(2,1)S(1)} %fusion.50.refs_0_), channel_id=1, source_target_pairs={{0,16},{4,20},{8,24},{12,28},{16,0},{20,4},{24,8},{28,12},{1,17},{... | collective-permute-start | bytes 221192 | tf_op jit(solution)/shard_map/ppermute | solution.py:114
  52.2 18.0 %collective-permute-start.22 = (bf16[48,768]{1,0:T(8,128)(2,1)S(1)}, bf16[48,768]{1,0:T(8,128)(2,1)S(1)}, u32[]{:S(2)}, u32[]{:S(2)}) collective-permute-start(bf16[48,768]{1,0:T(8,128)(2,1)S(1)} %fusion.50.refs_0_), channel_id=1, source_target_pairs={{0,24},{4,28},{8,0},{12,4},{16,8},{20,12},{24,16},{28,20},{1,25},{... | collective-permute-start | bytes 221192 | tf_op jit(solution)/shard_map/ppermute | solution.py:114
  79.1 27.9 %collective-permute-start.27 = (bf16[8,48,768]{2,1,0:T(8,128)(2,1)S(1)}, bf16[8,48,768]{2,1,0:T(8,128)(2,1)}, u32[]{:S(2)}, u32[]{:S(2)}) collective-permute-start(bf16[8,48,768]{2,1,0:T(8,128)(2,1)S(1)} %assemble.5), channel_id=1, source_target_pairs={{0,2},{2,0},{1,3},{3,1},{4,6},{6,4},{5,7},{7,5},{8,10},{10,8},{9,1... | collective-permute-start | bytes 1769480 | tf_op jit(solution)/shard_map/ppermute | solution.py:55
  100.1 23.5 %collective-permute-start.10 = (bf16[3,192,512]{2,1,0:T(8,128)(2,1)S(1)}, bf16[3,192,512]{2,1,0:T(8,128)(2,1)}, u32[]{:S(2)}, u32[]{:S(2)}) collective-permute-start(bf16[3,192,512]{2,1,0:T(8,128)(2,1)S(1)} %get-tuple-element.132.o0_ref), channel_id=1, source_target_pairs={{0,2},{2,0},{1,3},{3,1},{4,6},{6,4},{5,7},{7,5},{8,10},{10,8},{9,1... | collective-permute-start | bytes 1769480 | tf_op jit(solution)/shard_map/ppermute | solution.py:55
  160.7 15.6 %collective-permute-start.29 = (bf16[3,384,256]{2,1,0:T(8,128)(2,1)S(1)}, bf16[3,384,256]{2,1,0:T(8,128)(2,1)S(1)}, u32[]{:S(2)}, u32[]{:S(2)}) collective-permute-start(bf16[3,384,256]{2,1,0:T(8,128)(2,1)S(1)} %constant_dynamic-slice_fusion.11), channel_id=1, source_target_pairs={{0,2},{2,0},{1,3},{3,1},{4,6},{6,4},{5,7},{7,5},{8,10},{10,8},{9,1... | collective-permute-start | bytes 1769480 | tf_op jit(solution)/shard_map/ppermute | solution.py:55
  160.8 15.5 %collective-permute-start.30 = (f32[3,8,512]{2,1,0:T(8,128)S(1)}, f32[3,8,512]{2,1,0:T(8,128)S(1)}, u32[]{:S(2)}, u32[]{:S(2)}) collective-permute-start(f32[3,8,512]{2,1,0:T(8,128)S(1)} %get-tuple-element.148.lse_ref), channel_id=1, source_target_pairs={{0,2},{2,0},{1,3},{3,1},{4,6},{6,4},{5,7},{7,5},{8,10},{10,8},{9,1... | collective-permute-start | bytes 147464 | tf_op jit(solution)/shard_map/ppermute | solution.py:55
  204.6 14.4 %collective-permute-start.33 = (bf16[3,384,128]{2,1,0:T(8,128)(2,1)S(1)}, bf16[3,384,128]{2,1,0:T(8,128)(2,1)S(1)}, u32[]{:S(2)}, u32[]{:S(2)}) collective-permute-start(bf16[3,384,128]{2,1,0:T(8,128)(2,1)S(1)} %get-tuple-element.161.do0_ref), channel_id=1, source_target_pairs={{0,2},{2,0},{1,3},{3,1},{4,6},{6,4},{5,7},{7,5},{8,10},{10,8},{9,1... | collective-permute-start | bytes 884744 | tf_op jit(solution)/shard_map/ppermute | solution.py:55
  222.2 42.3 %collective-permute-start.42 = (bf16[4,128,768]{2,1,0:T(8,128)(2,1)S(1)}, bf16[4,128,768]{2,1,0:T(8,128)(2,1)S(1)}, u32[]{:S(2)}, u32[]{:S(2)}) collective-permute-start(bf16[4,128,768]{2,1,0:T(8,128)(2,1)S(1)} %dynamic-slice_bitcast_fusion.3), channel_id=1, source_target_pairs={{0,4},{4,0},{8,12},{12,8},{16,20},{20,16},{24,28},{28,24},{1,5},{5... | collective-permute-start | bytes 2359304 | tf_op jit(solution)/shard_map/ppermute | solution.py:146
  226.7 38.0 %collective-permute-start.41 = (bf16[768,1024]{1,0:T(8,128)(2,1)S(1)}, bf16[768,1024]{1,0:T(8,128)(2,1)S(1)}, u32[]{:S(2)}, u32[]{:S(2)}) collective-permute-start(bf16[768,1024]{1,0:T(8,128)(2,1)S(1)} %add_convert_fusion.3), channel_id=1, source_target_pairs={{0,2},{2,0},{1,3},{3,1},{4,6},{6,4},{5,7},{7,5},{8,10},{10,8},{9,1... | collective-permute-start | bytes 4718600 | tf_op jit(solution)/shard_map/ppermute | solution.py:55
  264.7 43.5 %collective-permute-start.51 = (bf16[4,64,768]{2,1,0:T(8,128)(2,1)S(1)}, bf16[4,64,768]{2,1,0:T(8,128)(2,1)S(1)}, u32[]{:S(2)}, u32[]{:S(2)}) collective-permute-start(bf16[4,64,768]{2,1,0:T(8,128)(2,1)S(1)} %constant_dynamic-slice_fusion.3), channel_id=1, source_target_pairs={{0,2},{2,0},{1,3},{3,1},{4,6},{6,4},{5,7},{7,5},{8,10},{10,8},{9,1... | collective-permute-start | bytes 1179656 | tf_op jit(solution)/shard_map/ppermute | solution.py:55
  267.4 27.7 %collective-permute-start.44 = (bf16[4,96,1024]{2,1,0:T(8,128)(2,1)S(1)}, bf16[4,96,1024]{2,1,0:T(8,128)(2,1)S(1)}, u32[]{:S(2)}, u32[]{:S(2)}) collective-permute-start(bf16[4,96,1024]{2,1,0:T(8,128)(2,1)S(1)} %dynamic-slice_bitcast_fusion.2), channel_id=1, source_target_pairs={{0,4},{4,0},{8,12},{12,8},{16,20},{20,16},{24,28},{28,24},{1,5},{5... | collective-permute-start | bytes 2359304 | tf_op jit(solution)/shard_map/ppermute | solution.py:146
  271.8 24.6 %collective-permute-start.43 = (bf16[3,256,384]{2,1,0:T(8,128)(2,1)S(1)}, bf16[3,256,384]{2,1,0:T(8,128)(2,1)S(1)}, u32[]{:S(2)}, u32[]{:S(2)}) collective-permute-start(bf16[3,256,384]{2,1,0:T(8,128)(2,1)S(1)} %constant_dynamic-slice_fusion.8), channel_id=1, source_target_pairs={{0,2},{2,0},{1,3},{3,1},{4,6},{6,4},{5,7},{7,5},{8,10},{10,8},{9,1... | collective-permute-start | bytes 1769480 | tf_op jit(solution)/shard_map/ppermute | solution.py:55
  293.4 83.3 %collective-permute-start.60 = (bf16[3,1024,768]{2,1,0:T(8,128)(2,1)}, bf16[3,1024,768]{2,1,0:T(8,128)(2,1)}, u32[]{:S(2)}, u32[]{:S(2)}) collective-permute-start(bf16[3,1024,768]{2,1,0:T(8,128)(2,1)} %get-tuple-element.217), channel_id=1, source_target_pairs={{0,1},{1,0},{2,3},{3,2},{4,5},{5,4},{6,7},{7,6},{8,9},{9,8},{10,11... | collective-permute-start | bytes 14155784 | tf_op jit(solution)/shard_map/ppermute | solution.py:51
  298.7 27.5 %collective-permute-start.50 = (bf16[4,96,1536]{2,1,0:T(8,128)(2,1)}, bf16[4,96,1536]{2,1,0:T(8,128)(2,1)}, u32[]{:S(2)}, u32[]{:S(2)}) collective-permute-start(bf16[4,96,1536]{2,1,0:T(8,128)(2,1)} %get-tuple-element.245), channel_id=1, source_target_pairs={{0,4},{4,0},{8,12},{12,8},{16,20},{20,16},{24,28},{28,24},{1,5},{5... | collective-permute-start | bytes 3538952 | tf_op jit(solution)/shard_map/ppermute | solution.py:146
  316.7 32.8 %collective-permute-start.53 = (bf16[96,1024]{1,0:T(8,128)(2,1)}, bf16[96,1024]{1,0:T(8,128)(2,1)}, u32[]{:S(2)}, u32[]{:S(2)}) collective-permute-start(bf16[96,1024]{1,0:T(8,128)(2,1)} %get-tuple-element.279), channel_id=1, source_target_pairs={{0,8},{4,12},{8,16},{12,20},{16,24},{20,28},{24,0},{28,4},{1,9},{5... | collective-permute-start | bytes 589832 | tf_op jit(solution)/shard_map/ppermute | solution.py:159
  321.0 29.2 %collective-permute-start.54 = (bf16[96,1024]{1,0:T(8,128)(2,1)}, bf16[96,1024]{1,0:T(8,128)(2,1)}, u32[]{:S(2)}, u32[]{:S(2)}) collective-permute-start(bf16[96,1024]{1,0:T(8,128)(2,1)} %get-tuple-element.278), channel_id=1, source_target_pairs={{0,16},{4,20},{8,24},{12,28},{16,0},{20,4},{24,8},{28,12},{1,17},{... | collective-permute-start | bytes 589832 | tf_op jit(solution)/shard_map/ppermute | solution.py:159
  330.2 33.7 %collective-permute-start.56 = (bf16[96,2048]{1,0:T(8,128)(2,1)}, bf16[96,2048]{1,0:T(8,128)(2,1)}, u32[]{:S(2)}, u32[]{:S(2)}) collective-permute-start(bf16[96,2048]{1,0:T(8,128)(2,1)} %get-tuple-element.253), channel_id=1, source_target_pairs={{0,8},{4,12},{8,16},{12,20},{16,24},{20,28},{24,0},{28,4},{1,9},{5... | collective-permute-start | bytes 1179656 | tf_op jit(solution)/shard_map/ppermute | solution.py:159
  331.4 32.5 %collective-permute-start.57 = (bf16[96,2048]{1,0:T(8,128)(2,1)}, bf16[96,2048]{1,0:T(8,128)(2,1)}, u32[]{:S(2)}, u32[]{:S(2)}) collective-permute-start(bf16[96,2048]{1,0:T(8,128)(2,1)} %get-tuple-element.254), channel_id=1, source_target_pairs={{0,16},{4,20},{8,24},{12,28},{16,0},{20,4},{24,8},{28,12},{1,17},{... | collective-permute-start | bytes 1179656 | tf_op jit(solution)/shard_map/ppermute | solution.py:159
  349.6 14.4 %collective-permute-start.52 = (bf16[8,48,384]{2,1,0:T(8,128)(2,1)}, bf16[8,48,384]{2,1,0:T(8,128)(2,1)S(1)}, u32[]{:S(2)}, u32[]{:S(2)}) collective-permute-start(bf16[8,48,384]{2,1,0:T(8,128)(2,1)} %constant_dynamic-slice_fusion.2), channel_id=1, source_target_pairs={{0,2},{2,0},{1,3},{3,1},{4,6},{6,4},{5,7},{7,5},{8,10},{10,8},{9,1... | collective-permute-start | bytes 884744 | tf_op jit(solution)/shard_map/ppermute | solution.py:55
  367.2 16.8 %collective-permute-start.59 = (bf16[4,48,1792]{2,1,0:T(8,128)(2,1)S(1)}, bf16[4,48,1792]{2,1,0:T(8,128)(2,1)S(1)}, u32[]{:S(2)}, u32[]{:S(2)}) collective-permute-start(bf16[4,48,1792]{2,1,0:T(8,128)(2,1)S(1)} %get-tuple-element.255), channel_id=1, source_target_pairs={{0,4},{4,0},{8,12},{12,8},{16,20},{20,16},{24,28},{28,24},{1,5},{5... | collective-permute-start | bytes 2064392 | tf_op jit(solution)/shard_map/ppermute | solution.py:146
  375.1 25.8 %collective-permute-start.65 = (bf16[3,1,1,128,768]{4,3,0,2,1:T(8,128)(2,1)S(1)}, bf16[3,1,1,128,768]{4,3,0,2,1:T(8,128)(2,1)S(1)}, u32[]{:S(2)}, u32[]{:S(2)}) collective-permute-start(bf16[3,1,1,128,768]{4,3,0,2,1:T(8,128)(2,1)S(1)} %dynamic-slice_convert_fusion), channel_id=1, source_target_pairs={{0,2},{2,0},{1,3},{3,1},{4,6},{6,4},{5,7},{7,5},{8,10},{10,8},{9,1... | collective-permute-start | bytes 1769480 | tf_op jit(solution)/shard_map/ppermute | solution.py:55
  384.3 16.7 %collective-permute-start.62 = (bf16[48,1792]{1,0:T(8,128)(2,1)S(1)}, bf16[48,1792]{1,0:T(8,128)(2,1)S(1)}, u32[]{:S(2)}, u32[]{:S(2)}) collective-permute-start(bf16[48,1792]{1,0:T(8,128)(2,1)S(1)} %get-tuple-element.285), channel_id=1, source_target_pairs={{0,8},{4,12},{8,16},{12,20},{16,24},{20,28},{24,0},{28,4},{1,9},{5... | collective-permute-start | bytes 516104 | tf_op jit(solution)/shard_map/ppermute | solution.py:159
  384.4 16.6 %collective-permute-start.63 = (bf16[48,1792]{1,0:T(8,128)(2,1)S(1)}, bf16[48,1792]{1,0:T(8,128)(2,1)S(1)}, u32[]{:S(2)}, u32[]{:S(2)}) collective-permute-start(bf16[48,1792]{1,0:T(8,128)(2,1)S(1)} %get-tuple-element.284), channel_id=1, source_target_pairs={{0,16},{4,20},{8,24},{12,28},{16,0},{20,4},{24,8},{28,12},{1,17},{... | collective-permute-start | bytes 516104 | tf_op jit(solution)/shard_map/ppermute | solution.py:159
  386.8 15.9 %collective-permute-start.64 = (bf16[48,1792]{1,0:T(8,128)(2,1)S(1)}, bf16[48,1792]{1,0:T(8,128)(2,1)S(1)}, u32[]{:S(2)}, u32[]{:S(2)}) collective-permute-start(bf16[48,1792]{1,0:T(8,128)(2,1)S(1)} %get-tuple-element.283), channel_id=1, source_target_pairs={{0,24},{4,28},{8,0},{12,4},{16,8},{20,12},{24,16},{28,20},{1,25},{... | collective-permute-start | bytes 516104 | tf_op jit(solution)/shard_map/ppermute | solution.py:159
  388.6 27.5 %collective-permute-start.69 = (bf16[96,4608]{1,0:T(8,128)(2,1)S(1)}, bf16[96,4608]{1,0:T(8,128)(2,1)S(1)}, u32[]{:S(2)}, u32[]{:S(2)}) collective-permute-start(bf16[96,4608]{1,0:T(8,128)(2,1)S(1)} %slice_dynamic-update-slice_fusion.2), channel_id=1, source_target_pairs={{0,1},{1,0},{2,3},{3,2},{4,5},{5,4},{6,7},{7,6},{8,9},{9,8},{10,11... | collective-permute-start | bytes 2654216 | tf_op jit(solution)/shard_map/ppermute | solution.py:51
  (84 other events, 785.8 us)
Sparse Core Ops, SparseCore 0:
  11.5 67.0 all-gather.4
  82.1 75.2 all-gather.2

commit v6 on v5

--- a/solution.py
+++ b/solution.py
@@ -480,10 +480,11 @@
             o_ref[0, at, :] = (acc_ref[at, :] * inverse[h : h + 1, :]).astype(o_ref.dtype)
 
 
-def cross_forward(work, q, k, v):
-    examples, feats, length = q.shape
-    q_spec = pl.BlockSpec((1, feats, length), lambda i, work: (work[0, i], 0, 0))
-    k_spec = pl.BlockSpec((1, feats, ROW_BLOCK), lambda i, work: (work[0, i], 0, work[1, i]))
+def cross_forward(work, q, k, v, first, count):
+    _, feats, length = q.shape
+    q_spec = pl.BlockSpec((1, feats, length), lambda i, work: (work[0, i] + first, 0, 0))
+    o_spec = pl.BlockSpec((1, feats, length), lambda i, work: (work[0, i], 0, 0))
+    k_spec = pl.BlockSpec((1, feats, ROW_BLOCK), lambda i, work: (work[0, i] + first, 0, work[1, i]))
     l_spec = pl.BlockSpec((1, 8, length), lambda i, work: (work[0, i], 0, 0))
     return pl.pallas_call(
         cross_forward_kernel,
@@ -491,7 +492,7 @@
             num_scalar_prefetch=1,
             grid=(work.shape[1],),
             in_specs=[q_spec, k_spec, k_spec],
-            out_specs=[q_spec, l_spec],
+            out_specs=[o_spec, l_spec],
             scratch_shapes=[
                 pltpu.VMEM((8, length), F32),
                 pltpu.VMEM((8, length), F32),
@@ -499,11 +500,11 @@
             ],
         ),
         out_shape=[
-            jax.ShapeDtypeStruct((examples, feats, length), BF16),
-            jax.ShapeDtypeStruct((examples, 8, length), F32),
+            jax.ShapeDtypeStruct((count, feats, length), BF16),
+            jax.ShapeDtypeStruct((count, 8, length), F32),
         ],
         compiler_params=pltpu.CompilerParams(vmem_limit_bytes=48 << 20),
-        cost_estimate=cost(30e-6 * PEAK_FLOPS, 16e6),
+        cost_estimate=cost(10e-6 * count * PEAK_FLOPS, 5e6 * count),
         name="cross_forward",
     )(work, q, k, v)
 
@@ -1053,10 +1054,20 @@
         me, x_all, pieces, mine_w, other_w, gain_two
     )
 
-    part_o, part_lse = cross_forward(work, cross_q, keys, values)
-    came = across_swap(part_of(part_o, 1 - row, 2, 2))
-    chip_o, lse = combine(me, part_o, came, part_lse, across_swap(part_lse))
-    mine_o, other_o = part_of(chip_o, core, 2, 2), pair_swap(part_of(chip_o, 1 - core, 2, 2))
+    apart = examples - 1
+    part_o, part_lse = cross_forward(work_list(live[:apart]), cross_q, keys, values, 0, apart)
+    came, came_lse = across_swap(part_of(part_o, 1 - row, 2, 2)), across_swap(part_lse)
+    last_work = after(work_list(live[apart:]), part_o)
+    last_o, last_lse = cross_forward(last_work, cross_q, keys, values, apart, examples - apart)
+    last_o, last_lse, came, came_lse = lax.optimization_barrier((last_o, last_lse, came, came_lse))
+    last_came, last_came_lse = across_swap(part_of(last_o, 1 - row, 2, 2)), across_swap(last_lse)
+    chips = [
+        combine(me, part_o, came, part_lse, came_lse),
+        combine(me, last_o, last_came, last_lse, last_came_lse),
+    ]
+    lse = jnp.concatenate([chip_lse for _, chip_lse in chips])
+    mine_o = jnp.concatenate([part_of(chip_o, core, 2, 2) for chip_o, _ in chips])
+    other_o = jnp.concatenate([pair_swap(part_of(chip_o, 1 - core, 2, 2)) for chip_o, _ in chips])
 
     tokens = examples * own
     down_rows = ffn_down.shape[0] // 2

time: 438 us -> 440 us (level)
  waiting for transfers between devices: 116 us -> 93.7 us
  Pallas kernels: 160 us -> 177 us
  starting transfers between devices: 59.9 us -> 65 us
  other arithmetic: 46.9 us -> 51.8 us
    ppermute x4, starting transfers between devices: 12 us -> 0.64 us  [x_swap(): lax.ppermute(pick(planes, 1 - x, 1), 'wide', BESIDE)]
    ppermute x17 -> x19, waiting for transfers between devices: 37.2 us -> 26.1 us  [across_swap(): return lax.ppermute(value, 'narrow', ACROSS)]
    ppermute x9, starting transfers between devices: 6.17 us -> 16.3 us  [z_swap(): lax.ppermute(s, 'wide', along(i + 1))]
    pallas_call x1, Pallas kernels: 37.2 us -> 43.8 us  [cross_backward(): pl.pallas_call(cross_backward_kernel, grid_spec=pltpu.PrefetchScalarGridS...]
    pallas_call x1 -> x2, Pallas kernels: 22.4 us -> 28.2 us  [cross_forward(): pl.pallas_call(cross_forward_kernel, grid_spec=pltpu.PrefetchScalarGridSp...]
    ppermute x4, waiting for transfers between devices: 6.85 us -> 1.36 us  [x_swap(): lax.ppermute(pick(planes, 1 - x, 1), 'wide', BESIDE)]
    ppermute x19 -> x20, starting transfers between devices: 14 us -> 19.1 us  [pair_swap(): return lax.ppermute(value, 'narrow', PAIR)]
    ppermute x19 -> x20, waiting for transfers between devices: 14.1 us -> 11.8 us  [pair_swap(): return lax.ppermute(value, 'narrow', PAIR)]
  transfers between devices with their start and end apart: 72 -> 75, of which waited for: 32 -> 29; matrix products, arithmetic and copies ran while one was open for 15% -> 15% of each run, Pallas kernels for 32% -> 35%
where the time goes in v6:
time: 440 us; the launch traced here: 434 us
  Pallas kernels  177 us (40%)
  waiting for transfers between devices  93.7 us (21%)
  starting transfers between devices  65 us (15%)
  other arithmetic  51.8 us (12%)
  local copies, waits for them, and re-layouts  29 us (7%)
  between operations  16.1 us (4%)
    pallas_call x1, Pallas kernels, cross_backward(): pl.pallas_call(cross_backward_kernel, grid_spec=pltpu.PrefetchScalarGridS...  43.8 us
    pallas_call x2, Pallas kernels, cross_forward(): pl.pallas_call(cross_forward_kernel, grid_spec=pltpu.PrefetchScalarGridSp...  28.2 us
    ppermute x12, waiting for transfers between devices, wide_gather(): pieces = line + [lax.ppermute(piece, 'wide', BESIDE) for piece in line]  26.4 us
    ppermute x19, waiting for transfers between devices, across_swap(): return lax.ppermute(value, 'narrow', ACROSS)  26.1 us
    pallas_call x1, Pallas kernels, feed_forward(): pl.pallas_call(functools.partial(feed_forward_kernel, piece=piece), grid=...  22.7 us
    pallas_call x1, Pallas kernels, memory_backward(): pl.pallas_call(memory_backward_kernel, grid_spec=pltpu.PrefetchScalarGrid...  22.1 us
    ppermute x20, starting transfers between devices, pair_swap(): return lax.ppermute(value, 'narrow', PAIR)  19.1 us
    pallas_call x1, Pallas kernels, self_backward(): pl.pallas_call(self_backward_kernel, grid=(examples,), in_specs=[pl.Block...  17.4 us
  transfers between devices with their start and end apart: 75, of which 29 were waited for; matrix products, arithmetic and copies ran while one was open for 15% of the time, Pallas kernels for 35%

profile of v6, /device:TPU:9, one launch (start us, length us, event | category | flops | bytes accessed | tf_op | source)
XLA Modules:
  0.0 434.2 jit_solution(10637490622432210925)
XLA Ops:
  28.7 2.5 collective-permute-done.4.refs_3_
  38.0 2.7 collective-permute-done.6.refs_5_
  40.8 4.3 collective-permute-done.7.refs_6_
  45.1 4.8 %collective-permute-done.8.refs_7_ = bf16[96,768]{1,0:T(8,128)(2,1)S(1)} collective-permute-done((bf16[96,768]{1,0:T(8,128)(2,1)S(1)}, bf16[96,768]{1,0:T(8,128)(2,1)S(1)}, u32[]{:S(2)}, u32[]{:S(2)}) %collective-permute-start.8) | collective-permute-done | bytes 147488 | tf_op jit(solution)/shard_map/ppermute | solution.py:116
  56.4 10.1 %self_forward.1 = (bf16[3,640,512]{2,1,0:T(8,128)(2,1)S(1)}, bf16[3,192,512]{2,1,0:T(8,128)(2,1)}, f32[3,8,512]{2,1,0:T(8,128)S(1)}, bf16[640,768]{1,0:T(8,128)(2,1)S(1)}) custom-call(bf16[3,512,768]{2,1,0:T(8,128)(2,1)} %bitcast.263, f32[1,768]{1,0:T(1,128)S(1)} %get-tuple-element.355.gain_ref, bf16[768,640]{1,0:T(8,128)(2,1)S(1)} %bitcast.249, ...), custom_call_target="tpu_custom_call" | custom-call | flops 10350000128 | bytes 8000000 | tf_op jit(solution)/shard_map/self_forward/pallas_call | solution.py:239
  78.2 5.9 %collective-permute-done.13.refs_2_ = bf16[96,768]{1,0:T(8,128)(2,1)S(1)} collective-permute-done((bf16[96,768]{1,0:T(8,128)(2,1)S(1)}, bf16[96,768]{1,0:T(8,128)(2,1)S(1)}, u32[]{:S(2)}, u32[]{:S(2)}) %collective-permute-start.13) | collective-permute-done | bytes 147488 | tf_op jit(solution)/shard_map/ppermute | solution.py:114
  84.0 3.7 collective-permute-done.14.refs_3_
  90.8 4.3 collective-permute-done.15.refs_4_
  101.3 3.2 collective-permute-done.18.refs_7_
  106.9 13.8 %memory_project.1 = (bf16[3,384,2048]{2,1,0:T(8,128)(2,1)}, bf16[3,384,2048]{2,1,0:T(8,128)(2,1)}, bf16[768,768]{1,0:T(8,128)(2,1)S(1)}) custom-call(s32[5,12]{1,0:T(8,128)S(1)} %stack.105.work_ref, bf16[3,1024,768]{2,1,0:T(8,128)(2,1)} %own_ref.3, bf16[3,1024,768]{2,1,0:T(8,128)(2,1)} %collective-permute-done.19.other_ref, bf16[768,768]{1,0:T(8,128)(2,1)S(1)} %bitcast.245), custom_call_target="tpu_custom_call" | custom-call | flops 13799999488 | bytes 12000000 | tf_op jit(solution)/shard_map/memory_project/pallas_call | solution.py:417
  126.5 10.4 %self_output_stage.1 = (bf16[3,512,768]{2,1,0:T(8,128)(2,1)}, bf16[3,384,512]{2,1,0:T(8,128)(2,1)S(1)}, f32[3,128,768]{2,1,0:T(8,128)S(1)}, bf16[3,768,128]{2,1,...) custom-call(s32[1]{0:T(128)} %bitcast.place_ref, bf16[3,512,768]{2,1,0:T(8,128)(2,1)} %bitcast.264, ...), custom_call_target="tpu_custom_call" | custom-call | flops 6899999744 | bytes 10000000 | tf_op jit(solution)/shard_map/self_output_stage/pallas_call | solution.py:691
  137.9 18.0 %cross_forward.2 = (bf16[2,384,512]{2,1,0:T(8,128)(2,1)S(1)}, f32[2,8,512]{2,1,0:T(8,128)S(1)}) custom-call(s32[5,8]{1,0:T(8,128)S(1)} %stack.111.work_ref, bf16[3,384,512]{2,1,0:T(8,128)(2,1)S(1)} %get-tuple-element.154.q_ref, bf16[3,384,2048]{2,1,0:T(8,128)(2,1)} %get-tuple-element.151.k_ref, bf16[3,384,2048]{2,1,0:T(8,128)(2,1)} %get-tuple-element.155.v_ref), custom_call_target="tpu_custom_call" | custom-call | flops 23000000512 | bytes 10000000 | tf_op jit(solution)/shard_map/cross_forward/pallas_call | solution.py:489
  157.5 10.3 %cross_forward.3 = (bf16[1,384,512]{2,1,0:T(8,128)(2,1)S(1)}, f32[1,8,512]{2,1,0:T(8,128)S(1)}) custom-call(s32[5,4]{1,0:T(8,128)S(1)} %stack.114.work_ref, bf16[3,384,512]{2,1,0:T(8,128)(2,1)S(1)} %get-tuple-element.154.q_ref, bf16[3,384,2048]{2,1,0:T(8,128)(2,1)} %get-tuple-element.151.k_ref, bf16[3,384,2048]{2,1,0:T(8,128)(2,1)} %get-tuple-element.155.v_ref), custom_call_target="tpu_custom_call" | custom-call | flops 11500000256 | bytes 5000000 | tf_op jit(solution)/shard_map/cross_forward/pallas_call | solution.py:489
  170.8 3.4 collective-permute-done.32.other_lse_ref
  178.0 22.7 %feed_forward.1 = (bf16[384,768]{1,0:T(8,128)(2,1)}, f32[384,768]{1,0:T(8,128)S(1)}, bf16[3,384,128]{2,1,0:T(8,128)(2,1)S(1)}, bf16[3,384,128]{2,1,0:T(8,128)(2,...) custom-call(s32[1]{0:T(128)} %bitcast.place_ref, ...), custom_call_target="tpu_custom_call" | custom-call | flops 23000000512 | bytes 24000000 | tf_op jit(solution)/shard_map/feed_forward/pallas_call | solution.py:843
  203.0 6.2 %collective-permute-done.43 = bf16[768,384]{1,0:T(8,128)(2,1)S(1)} collective-permute-done((bf16[768,384]{1,0:T(8,128)(2,1)S(1)}, bf16[768,384]{1,0:T(8,128)(2,1)S(1)}, u32[]{:S(2)}, u32[]{:S(2)}) %collective-permute-start.43) | collective-permute-done | bytes 589856 | tf_op jit(solution)/shard_map/ppermute | solution.py:51
  217.3 3.0 collective-permute-done.37.do3_ref
  221.1 43.8 %cross_backward.1 = (bf16[3,512,384]{2,1,0:T(8,128)(2,1)S(1)}, bf16[3,2048,768]{2,1,0:T(8,128)(2,1)}) custom-call(s32[5,12]{1,0:T(8,128)S(1)} %stack.105.work_ref, s32[1]{0:T(128)} %bitcast.place_ref, bf16[3,384,512]{2,1,0:T(8,128)(2,1)S(1)} %copy-done.15, bf16[3,384,128]{2,1,0:T(8,128)(2,1)S(1)} %get-tuple-element.178.do0_ref, ...), custom_call_target="tpu_custom_call" | custom-call | flops 51749998592 | bytes 24000000 | tf_op jit(solution)/shard_map/cross_backward/pallas_call | solution.py:569
  269.5 22.1 %memory_backward.1 = (bf16[3,1024,768]{2,1,0:T(8,128)(2,1)}, bf16[3,1024,768]{2,1,0:T(8,128)(2,1)}, bf16[768,768]{1,0:T(8,128)(2,1)S(1)}) custom-call(s32[3,4]{1,0:T(4,128)S(1)} %get-tuple-element.360.live_ref, bf16[3,1024,768]{2,1,0:T(8,128)(2,1)} %own_ref.3, bf16[3,1024,768]{2,1,0:T(8,128)(2,1)} %collective-permute-done.19.other_ref, ...), custom_call_target="tpu_custom_call" | custom-call | flops 20700000256 | bytes 30000000 | tf_op jit(solution)/shard_map/memory_backward/pallas_call | solution.py:635
  291.6 2.7 collective-permute-start.63
  299.3 3.0 collective-permute-done.48.other_ref
  302.3 6.1 %self_output_back.1 = (f32[3,128,768]{2,1,0:T(8,128)S(1)}, bf16[3,192,128]{2,1,0:T(8,128)(2,1)S(1)}, bf16[3,192,128]{2,1,0:T(8,128)(2,1)S(1)}, bf16[3,384,128]{2...) custom-call(s32[1]{0:T(128)} %bitcast.place_ref, ...), custom_call_target="tpu_custom_call" | custom-call | flops 4600000000 | bytes 8000000 | tf_op jit(solution)/shard_map/self_output_back/pallas_call | solution.py:933
  312.0 5.4 %collective-permute-done.50 = bf16[3,384,128]{2,1,0:T(8,128)(2,1)} collective-permute-done((bf16[3,384,128]{2,1,0:T(8,128)(2,1)S(1)}, bf16[3,384,128]{2,1,0:T(8,128)(2,1)}, u32[]{:S(2)}, u32[]{:S(2)}) %collective-permute-start.50) | collective-permute-done | bytes 294944 | tf_op jit(solution)/shard_map/ppermute | solution.py:55
  321.5 5.9 %collective-permute-start.57 = (bf16[96,1024]{1,0:T(8,128)(2,1)}, bf16[96,1024]{1,0:T(8,128)(2,1)}, u32[]{:S(2)}, u32[]{:S(2)}) collective-permute-start(bf16[96,1024]{1,0:T(8,128)(2,1)} %get-tuple-element.310), channel_id=1, source_target_pairs={{0,16},{4,20},{8,24},{12,28},{16,0},{20,4},{24,8},{28,12},{1,17},{... | collective-permute-start | bytes 589832 | tf_op jit(solution)/shard_map/ppermute | solution.py:159
  332.1 4.5 %collective-permute-start.60 = (bf16[96,2048]{1,0:T(8,128)(2,1)}, bf16[96,2048]{1,0:T(8,128)(2,1)}, u32[]{:S(2)}, u32[]{:S(2)}) collective-permute-start(bf16[96,2048]{1,0:T(8,128)(2,1)} %get-tuple-element.286), channel_id=1, source_target_pairs={{0,16},{4,20},{8,24},{12,28},{16,0},{20,4},{24,8},{28,12},{1,17},{... | collective-permute-start | bytes 1179656 | tf_op jit(solution)/shard_map/ppermute | solution.py:159
  336.7 17.4 %self_backward.1 = (bf16[3,512,768]{2,1,0:T(8,128)(2,1)}, bf16[768,640]{1,0:T(8,128)(2,1)S(1)}, f32[8,512]{1,0:T(8,128)S(1)}, f32[1,768]{1,0:T(1,128)S(1)}) custom-call(s32[1]{0:T(128)} %bitcast.place_ref, bf16[3,512,768]{2,1,0:T(8,128)(2,1)} %bitcast.265, f32[1,768]{1,0:T(1,128)S(1)} %copy-done.6, bf16[3,640,512]{2,1,0:T(8,128)(2,1)S(1)} %copy-done.17, ...), custom_call_target="tpu_custom_call" | custom-call | flops 18400000000 | bytes 12000000 | tf_op jit(solution)/shard_map/self_backward/pallas_call | solution.py:331
  356.5 11.1 %collective-permute-done.58 = bf16[96,1024]{1,0:T(8,128)(2,1)} collective-permute-done((bf16[96,1024]{1,0:T(8,128)(2,1)}, bf16[96,1024]{1,0:T(8,128)(2,1)}, u32[]{:S(2)}, u32[]{:S(2)}) %collective-permute-start.58) | collective-permute-done | bytes 196640 | tf_op jit(solution)/shard_map/ppermute | solution.py:159
  374.5 3.3 collective-permute-done.64
  381.2 5.8 %add_convert_fusion = bf16[3,1024,768]{2,1,0:T(8,128)(2,1)} fusion(bf16[3,1024,768]{2,1,0:T(8,128)(2,1)} %collective-permute-done.63, bf16[3,1024,768]{2,1,0:T(8,128)(2,1)S(1)} %bitcast.258), kind=kLoop, calls=%fused_computation | loop fusion | flops 9437184 | bytes 14155776 | tf_op jit(solution)/shard_map/convert_element_type | solution.py:74
  393.0 4.2 collective-permute-start.72
  397.2 8.2 %collective-permute-done.68 = bf16[3,1,1,128,768]{4,3,0,2,1:T(8,128)(2,1)S(1)} collective-permute-done((bf16[3,1,1,128,768]{4,3,0,2,1:T(8,128)(2,1)S(1)}, bf16[3,1,1,128,768]{4,3,0,2,1:T(8,128)(2,1)S(1)}, u32[]{:S(2)}, u32[]{:S(2)}) %collective-permute-start.68) | collective-permute-done | bytes 589856 | tf_op jit(solution)/shard_map/ppermute | solution.py:55
  407.5 4.7 %collective-permute-done.69 = bf16[48,1792]{1,0:T(8,128)(2,1)S(1)} collective-permute-done((bf16[48,1792]{1,0:T(8,128)(2,1)S(1)}, bf16[48,1792]{1,0:T(8,128)(2,1)S(1)}, u32[]{:S(2)}, u32[]{:S(2)}) %collective-permute-start.69) | collective-permute-done | bytes 172064 | tf_op jit(solution)/shard_map/ppermute | solution.py:55
  (406 shorter events, 140.7 us)
Async XLA Ops:
  7.2 169.5 %all-gather.5.cloned.1.call-start = ((), (), s32[]{:S(2)}) async-start(), calls=%async_computation.1 | async-start | bytes 3244032 | tf_op jit(solution)/shard_map/all_gather | solution.py:1030
  9.0 167.7 %all-gather.3.cloned.1.call-start = ((), (), s32[]{:S(2)}) async-start(), calls=%async_computation | async-start | bytes 7704576 | tf_op jit(solution)/shard_map/all_gather | solution.py:1027
  13.5 15.3 %collective-permute-start.2 = (bf16[96,768]{1,0:T(8,128)(2,1)S(1)}, bf16[96,768]{1,0:T(8,128)(2,1)S(1)}, u32[]{:S(2)}, u32[]{:S(2)}) collective-permute-start(bf16[96,768]{1,0:T(8,128)(2,1)S(1)} %fusion.41.refs_0_), channel_id=1, source_target_pairs={{0,8},{4,12},{8,16},{12,20},{16,24},{20,28},{24,0},{28,4},{1,9},{5... | collective-permute-start | bytes 442376 | tf_op jit(solution)/shard_map/ppermute | solution.py:114
  14.8 13.9 %collective-permute-start.3 = (bf16[96,768]{1,0:T(8,128)(2,1)S(1)}, bf16[96,768]{1,0:T(8,128)(2,1)S(1)}, u32[]{:S(2)}, u32[]{:S(2)}) collective-permute-start(bf16[96,768]{1,0:T(8,128)(2,1)S(1)} %fusion.41.refs_0_), channel_id=1, source_target_pairs={{0,16},{4,20},{8,24},{12,28},{16,0},{20,4},{24,8},{28,12},{1,17},{... | collective-permute-start | bytes 442376 | tf_op jit(solution)/shard_map/ppermute | solution.py:114
  15.9 15.4 %collective-permute-start.4 = (bf16[96,768]{1,0:T(8,128)(2,1)S(1)}, bf16[96,768]{1,0:T(8,128)(2,1)S(1)}, u32[]{:S(2)}, u32[]{:S(2)}) collective-permute-start(bf16[96,768]{1,0:T(8,128)(2,1)S(1)} %fusion.41.refs_0_), channel_id=1, source_target_pairs={{0,24},{4,28},{8,0},{12,4},{16,8},{20,12},{24,16},{28,20},{1,25},{... | collective-permute-start | bytes 442376 | tf_op jit(solution)/shard_map/ppermute | solution.py:114
  17.3 15.1 %collective-permute-start = (bf16[3,128,768]{2,1,0:T(8,128)(2,1)}, bf16[3,128,768]{2,1,0:T(8,128)(2,1)S(1)}, u32[]{:S(2)}, u32[]{:S(2)}) collective-permute-start(bf16[3,128,768]{2,1,0:T(8,128)(2,1)} %param.24), channel_id=1, source_target_pairs={{0,2},{2,0},{1,3},{3,1},{4,6},{6,4},{5,7},{7,5},{8,10},{10,8},{9,1... | collective-permute-start | bytes 1769480 | tf_op jit(solution)/shard_map/ppermute | solution.py:55
  18.5 88.4 %collective-permute-start.19 = (bf16[3,1024,768]{2,1,0:T(8,128)(2,1)}, bf16[3,1024,768]{2,1,0:T(8,128)(2,1)}, u32[]{:S(2)}, u32[]{:S(2)}) collective-permute-start(bf16[3,1024,768]{2,1,0:T(8,128)(2,1)} %own_ref.3), channel_id=1, source_target_pairs={{0,1},{1,0},{2,3},{3,2},{4,5},{5,4},{6,7},{7,6},{8,9},{9,8},{10,11... | collective-permute-start | bytes 14155784 | tf_op jit(solution)/shard_map/ppermute | solution.py:51
  33.6 19.2 %collective-permute-start.1 = (bf16[3,2,128,768]{3,2,0,1:T(8,128)(2,1)}, bf16[3,2,128,768]{3,2,0,1:T(8,128)(2,1)}, u32[]{:S(2)}, u32[]{:S(2)}) collective-permute-start(bf16[3,2,128,768]{3,2,0,1:T(8,128)(2,1)} %pad_maximum_fusion.3), channel_id=1, source_target_pairs={{0,1},{1,0},{2,3},{3,2},{4,5},{5,4},{6,7},{7,6},{8,9},{9,8},{10,11... | collective-permute-start | bytes 3538952 | tf_op jit(solution)/shard_map/ppermute | solution.py:51
  40.7 27.2 %collective-permute-start.20 = (bf16[48,768]{1,0:T(8,128)(2,1)S(1)}, bf16[48,768]{1,0:T(8,128)(2,1)S(1)}, u32[]{:S(2)}, u32[]{:S(2)}) collective-permute-start(bf16[48,768]{1,0:T(8,128)(2,1)S(1)} %fusion.50.refs_0_), channel_id=1, source_target_pairs={{0,8},{4,12},{8,16},{12,20},{16,24},{20,28},{24,0},{28,4},{1,9},{5... | collective-permute-start | bytes 221192 | tf_op jit(solution)/shard_map/ppermute | solution.py:114
  45.1 22.8 %collective-permute-start.21 = (bf16[48,768]{1,0:T(8,128)(2,1)S(1)}, bf16[48,768]{1,0:T(8,128)(2,1)S(1)}, u32[]{:S(2)}, u32[]{:S(2)}) collective-permute-start(bf16[48,768]{1,0:T(8,128)(2,1)S(1)} %fusion.50.refs_0_), channel_id=1, source_target_pairs={{0,16},{4,20},{8,24},{12,28},{16,0},{20,4},{24,8},{28,12},{1,17},{... | collective-permute-start | bytes 221192 | tf_op jit(solution)/shard_map/ppermute | solution.py:114
  49.9 17.9 %collective-permute-start.22 = (bf16[48,768]{1,0:T(8,128)(2,1)S(1)}, bf16[48,768]{1,0:T(8,128)(2,1)S(1)}, u32[]{:S(2)}, u32[]{:S(2)}) collective-permute-start(bf16[48,768]{1,0:T(8,128)(2,1)S(1)} %fusion.50.refs_0_), channel_id=1, source_target_pairs={{0,24},{4,28},{8,0},{12,4},{16,8},{20,12},{24,16},{28,20},{1,25},{... | collective-permute-start | bytes 221192 | tf_op jit(solution)/shard_map/ppermute | solution.py:114
  76.7 28.3 %collective-permute-start.27 = (bf16[8,48,768]{2,1,0:T(8,128)(2,1)S(1)}, bf16[8,48,768]{2,1,0:T(8,128)(2,1)}, u32[]{:S(2)}, u32[]{:S(2)}) collective-permute-start(bf16[8,48,768]{2,1,0:T(8,128)(2,1)S(1)} %assemble.5), channel_id=1, source_target_pairs={{0,2},{2,0},{1,3},{3,1},{4,6},{6,4},{5,7},{7,5},{8,10},{10,8},{9,1... | collective-permute-start | bytes 1769480 | tf_op jit(solution)/shard_map/ppermute | solution.py:55
  98.2 24.4 %collective-permute-start.10 = (bf16[3,192,512]{2,1,0:T(8,128)(2,1)}, bf16[3,192,512]{2,1,0:T(8,128)(2,1)S(1)}, u32[]{:S(2)}, u32[]{:S(2)}) collective-permute-start(bf16[3,192,512]{2,1,0:T(8,128)(2,1)} %get-tuple-element.141.o0_ref), channel_id=1, source_target_pairs={{0,2},{2,0},{1,3},{3,1},{4,6},{6,4},{5,7},{7,5},{8,10},{10,8},{9,1... | collective-permute-start | bytes 1769480 | tf_op jit(solution)/shard_map/ppermute | solution.py:55
  202.9 14.5 %collective-permute-start.36 = (bf16[3,384,128]{2,1,0:T(8,128)(2,1)S(1)}, bf16[3,384,128]{2,1,0:T(8,128)(2,1)S(1)}, u32[]{:S(2)}, u32[]{:S(2)}) collective-permute-start(bf16[3,384,128]{2,1,0:T(8,128)(2,1)S(1)} %get-tuple-element.178.do0_ref), channel_id=1, source_target_pairs={{0,2},{2,0},{1,3},{3,1},{4,6},{6,4},{5,7},{7,5},{8,10},{10,8},{9,1... | collective-permute-start | bytes 884744 | tf_op jit(solution)/shard_map/ppermute | solution.py:55
  220.4 44.4 %collective-permute-start.45 = (bf16[4,128,768]{2,1,0:T(8,128)(2,1)S(1)}, bf16[4,128,768]{2,1,0:T(8,128)(2,1)S(1)}, u32[]{:S(2)}, u32[]{:S(2)}) collective-permute-start(bf16[4,128,768]{2,1,0:T(8,128)(2,1)S(1)} %dynamic-slice_bitcast_fusion.3), channel_id=1, source_target_pairs={{0,4},{4,0},{8,12},{12,8},{16,20},{20,16},{24,28},{28,24},{1,5},{5... | collective-permute-start | bytes 2359304 | tf_op jit(solution)/shard_map/ppermute | solution.py:146
  220.5 44.6 %collective-permute-start.44 = (bf16[768,1024]{1,0:T(8,128)(2,1)S(1)}, bf16[768,1024]{1,0:T(8,128)(2,1)S(1)}, u32[]{:S(2)}, u32[]{:S(2)}) collective-permute-start(bf16[768,1024]{1,0:T(8,128)(2,1)S(1)} %add_convert_fusion.3), channel_id=1, source_target_pairs={{0,2},{2,0},{1,3},{3,1},{4,6},{6,4},{5,7},{7,5},{8,10},{10,8},{9,1... | collective-permute-start | bytes 4718600 | tf_op jit(solution)/shard_map/ppermute | solution.py:55
  265.1 43.7 %collective-permute-start.54 = (bf16[4,64,768]{2,1,0:T(8,128)(2,1)S(1)}, bf16[4,64,768]{2,1,0:T(8,128)(2,1)S(1)}, u32[]{:S(2)}, u32[]{:S(2)}) collective-permute-start(bf16[4,64,768]{2,1,0:T(8,128)(2,1)S(1)} %constant_dynamic-slice_fusion.3), channel_id=1, source_target_pairs={{0,2},{2,0},{1,3},{3,1},{4,6},{6,4},{5,7},{7,5},{8,10},{10,8},{9,1... | collective-permute-start | bytes 1179656 | tf_op jit(solution)/shard_map/ppermute | solution.py:55
  267.8 28.0 %collective-permute-start.47 = (bf16[4,96,1024]{2,1,0:T(8,128)(2,1)S(1)}, bf16[4,96,1024]{2,1,0:T(8,128)(2,1)S(1)}, u32[]{:S(2)}, u32[]{:S(2)}) collective-permute-start(bf16[4,96,1024]{2,1,0:T(8,128)(2,1)S(1)} %dynamic-slice_bitcast_fusion.2), channel_id=1, source_target_pairs={{0,4},{4,0},{8,12},{12,8},{16,20},{20,16},{24,28},{28,24},{1,5},{5... | collective-permute-start | bytes 2359304 | tf_op jit(solution)/shard_map/ppermute | solution.py:146
  267.9 29.0 %collective-permute-start.46 = (bf16[3,256,384]{2,1,0:T(8,128)(2,1)S(1)}, bf16[3,256,384]{2,1,0:T(8,128)(2,1)S(1)}, u32[]{:S(2)}, u32[]{:S(2)}) collective-permute-start(bf16[3,256,384]{2,1,0:T(8,128)(2,1)S(1)} %constant_dynamic-slice_fusion.8), channel_id=1, source_target_pairs={{0,2},{2,0},{1,3},{3,1},{4,6},{6,4},{5,7},{7,5},{8,10},{10,8},{9,1... | collective-permute-start | bytes 1769480 | tf_op jit(solution)/shard_map/ppermute | solution.py:55
  291.6 89.6 %collective-permute-start.63 = (bf16[3,1024,768]{2,1,0:T(8,128)(2,1)}, bf16[3,1024,768]{2,1,0:T(8,128)(2,1)}, u32[]{:S(2)}, u32[]{:S(2)}) collective-permute-start(bf16[3,1024,768]{2,1,0:T(8,128)(2,1)} %get-tuple-element.235), channel_id=1, source_target_pairs={{0,1},{1,0},{2,3},{3,2},{4,5},{5,4},{6,7},{7,6},{8,9},{9,8},{10,11... | collective-permute-start | bytes 14155784 | tf_op jit(solution)/shard_map/ppermute | solution.py:51
  299.2 28.2 %collective-permute-start.53 = (bf16[4,96,1536]{2,1,0:T(8,128)(2,1)}, bf16[4,96,1536]{2,1,0:T(8,128)(2,1)}, u32[]{:S(2)}, u32[]{:S(2)}) collective-permute-start(bf16[4,96,1536]{2,1,0:T(8,128)(2,1)} %get-tuple-element.277), channel_id=1, source_target_pairs={{0,4},{4,0},{8,12},{12,8},{16,20},{20,16},{24,28},{28,24},{1,5},{5... | collective-permute-start | bytes 3538952 | tf_op jit(solution)/shard_map/ppermute | solution.py:146
  317.4 36.7 %collective-permute-start.56 = (bf16[96,1024]{1,0:T(8,128)(2,1)}, bf16[96,1024]{1,0:T(8,128)(2,1)}, u32[]{:S(2)}, u32[]{:S(2)}) collective-permute-start(bf16[96,1024]{1,0:T(8,128)(2,1)} %get-tuple-element.311), channel_id=1, source_target_pairs={{0,8},{4,12},{8,16},{12,20},{16,24},{20,28},{24,0},{28,4},{1,9},{5... | collective-permute-start | bytes 589832 | tf_op jit(solution)/shard_map/ppermute | solution.py:159
  321.5 33.3 %collective-permute-start.57 = (bf16[96,1024]{1,0:T(8,128)(2,1)}, bf16[96,1024]{1,0:T(8,128)(2,1)}, u32[]{:S(2)}, u32[]{:S(2)}) collective-permute-start(bf16[96,1024]{1,0:T(8,128)(2,1)} %get-tuple-element.310), channel_id=1, source_target_pairs={{0,16},{4,20},{8,24},{12,28},{16,0},{20,4},{24,8},{28,12},{1,17},{... | collective-permute-start | bytes 589832 | tf_op jit(solution)/shard_map/ppermute | solution.py:159
  331.5 37.2 %collective-permute-start.59 = (bf16[96,2048]{1,0:T(8,128)(2,1)}, bf16[96,2048]{1,0:T(8,128)(2,1)}, u32[]{:S(2)}, u32[]{:S(2)}) collective-permute-start(bf16[96,2048]{1,0:T(8,128)(2,1)} %get-tuple-element.285), channel_id=1, source_target_pairs={{0,8},{4,12},{8,16},{12,20},{16,24},{20,28},{24,0},{28,4},{1,9},{5... | collective-permute-start | bytes 1179656 | tf_op jit(solution)/shard_map/ppermute | solution.py:159
  332.1 36.7 %collective-permute-start.60 = (bf16[96,2048]{1,0:T(8,128)(2,1)}, bf16[96,2048]{1,0:T(8,128)(2,1)}, u32[]{:S(2)}, u32[]{:S(2)}) collective-permute-start(bf16[96,2048]{1,0:T(8,128)(2,1)} %get-tuple-element.286), channel_id=1, source_target_pairs={{0,16},{4,20},{8,24},{12,28},{16,0},{20,4},{24,8},{28,12},{1,17},{... | collective-permute-start | bytes 1179656 | tf_op jit(solution)/shard_map/ppermute | solution.py:159
  354.1 14.6 %collective-permute-start.55 = (bf16[8,48,384]{2,1,0:T(8,128)(2,1)S(1)}, bf16[8,48,384]{2,1,0:T(8,128)(2,1)S(1)}, u32[]{:S(2)}, u32[]{:S(2)}) collective-permute-start(bf16[8,48,384]{2,1,0:T(8,128)(2,1)S(1)} %constant_dynamic-slice_fusion.2), channel_id=1, source_target_pairs={{0,2},{2,0},{1,3},{3,1},{4,6},{6,4},{5,7},{7,5},{8,10},{10,8},{9,1... | collective-permute-start | bytes 884744 | tf_op jit(solution)/shard_map/ppermute | solution.py:55
  372.1 16.3 %collective-permute-start.62 = (bf16[4,48,1792]{2,1,0:T(8,128)(2,1)S(1)}, bf16[4,48,1792]{2,1,0:T(8,128)(2,1)S(1)}, u32[]{:S(2)}, u32[]{:S(2)}) collective-permute-start(bf16[4,48,1792]{2,1,0:T(8,128)(2,1)S(1)} %get-tuple-element.287), channel_id=1, source_target_pairs={{0,4},{4,0},{8,12},{12,8},{16,20},{20,16},{24,28},{28,24},{1,5},{5... | collective-permute-start | bytes 2064392 | tf_op jit(solution)/shard_map/ppermute | solution.py:146
  379.6 25.7 %collective-permute-start.68 = (bf16[3,1,1,128,768]{4,3,0,2,1:T(8,128)(2,1)S(1)}, bf16[3,1,1,128,768]{4,3,0,2,1:T(8,128)(2,1)S(1)}, u32[]{:S(2)}, u32[]{:S(2)}) collective-permute-start(bf16[3,1,1,128,768]{4,3,0,2,1:T(8,128)(2,1)S(1)} %dynamic-slice_convert_fusion), channel_id=1, source_target_pairs={{0,2},{2,0},{1,3},{3,1},{4,6},{6,4},{5,7},{7,5},{8,10},{10,8},{9,1... | collective-permute-start | bytes 1769480 | tf_op jit(solution)/shard_map/ppermute | solution.py:55
  388.6 16.8 %collective-permute-start.65 = (bf16[48,1792]{1,0:T(8,128)(2,1)S(1)}, bf16[48,1792]{1,0:T(8,128)(2,1)S(1)}, u32[]{:S(2)}, u32[]{:S(2)}) collective-permute-start(bf16[48,1792]{1,0:T(8,128)(2,1)S(1)} %get-tuple-element.317), channel_id=1, source_target_pairs={{0,8},{4,12},{8,16},{12,20},{16,24},{20,28},{24,0},{28,4},{1,9},{5... | collective-permute-start | bytes 516104 | tf_op jit(solution)/shard_map/ppermute | solution.py:159
  388.9 16.5 %collective-permute-start.66 = (bf16[48,1792]{1,0:T(8,128)(2,1)S(1)}, bf16[48,1792]{1,0:T(8,128)(2,1)S(1)}, u32[]{:S(2)}, u32[]{:S(2)}) collective-permute-start(bf16[48,1792]{1,0:T(8,128)(2,1)S(1)} %get-tuple-element.316), channel_id=1, source_target_pairs={{0,16},{4,20},{8,24},{12,28},{16,0},{20,4},{24,8},{28,12},{1,17},{... | collective-permute-start | bytes 516104 | tf_op jit(solution)/shard_map/ppermute | solution.py:159
  391.0 15.9 %collective-permute-start.67 = (bf16[48,1792]{1,0:T(8,128)(2,1)S(1)}, bf16[48,1792]{1,0:T(8,128)(2,1)S(1)}, u32[]{:S(2)}, u32[]{:S(2)}) collective-permute-start(bf16[48,1792]{1,0:T(8,128)(2,1)S(1)} %get-tuple-element.315), channel_id=1, source_target_pairs={{0,24},{4,28},{8,0},{12,4},{16,8},{20,12},{24,16},{28,20},{1,25},{... | collective-permute-start | bytes 516104 | tf_op jit(solution)/shard_map/ppermute | solution.py:159
  393.0 27.3 %collective-permute-start.72 = (bf16[96,4608]{1,0:T(8,128)(2,1)S(1)}, bf16[96,4608]{1,0:T(8,128)(2,1)S(1)}, u32[]{:S(2)}, u32[]{:S(2)}) collective-permute-start(bf16[96,4608]{1,0:T(8,128)(2,1)S(1)} %slice_dynamic-update-slice_fusion.2), channel_id=1, source_target_pairs={{0,1},{1,0},{2,3},{3,2},{4,5},{5,4},{6,7},{7,6},{8,9},{9,8},{10,11... | collective-permute-start | bytes 2654216 | tf_op jit(solution)/shard_map/ppermute | solution.py:51
  (85 other events, 697.5 us)
Sparse Core Ops, SparseCore 0:
  11.5 64.5 all-gather.4
  79.6 75.1 all-gather.2
